TPU v7x, 32 devices: a whole 2x2x4 slice. The times are simulated.
32 devices in a mesh: lat: 4 (over z), lon: 8 (over y, x, core).
Axes of the slice: x: 2, y: 2, z: 4, core: 2. Of those that a mesh axis runs over, the one named last changes fastest.
Arguments:
- conc: float32 [64, 128, 1024], P('lat', None, 'lon'), may hold values from 0.1 to 2
- wind_lon: float32 [64, 1024], P('lat', 'lon'), may hold values from 0.1 to 0.35
- wind_lat: float32 [64, 1024], P('lat', 'lon'), may hold values from 0.05 to 0.25
- mixing: float32 [64, 1024], P('lat', 'lon'), may hold values from 0.02 to 0.1
- sun: float32 [64, 1024], replicated, may hold values from 0.1 to 1
- rate: float32 [512], replicated, may hold values from 0.02 to 0.3
- night_loss: float32 [128], replicated, may hold values from 0.05 to 1
- stoich: int32 [4, 512], replicated, may hold values from 0 to 127
- plan: int32 [2, 64, 8], replicated, may hold values from -2 to 4, as said below
Outputs:
- conc_out: float32 [64, 128, 1024], P('lat', None, 'lon')
Inputs may be any that keep to these rules, and one draw needn't show every extreme that they name: `plan`: code -2 marks a dark block, -1 a sunlit block computed where it lies; a sunlit block with code k in 0, 1, 2 is computed on the lon sector half the axis plus k - 1 further along (modulo the axis), with code 3 on the next sector, with code 4 on the previous one, always in the same latitude band. A sector sends at most 3 blocks of one band with one code, some exactly 3; a sector that sends receives nothing; the blocks a device keeps plus those it receives in a substep number at most 9, exactly 9 on some device.
All inputs are finite; a program needn't handle non-finite values.
Results may differ from a plain program's by a relative error of at most 0.0003.
Values sent between devices are 32-bit elements; how exact they have to be, the bound alone decides.
No kernel may reach another device: no remote copies, remote signals or barrier semaphores. Data moves between devices by JAX's collectives and lax.ppermute only.
A program may use at most 128 MiB of HBM per device.

v0:
```python
import jax
import jax.numpy as jnp
from jax import lax
from jax.experimental import pallas as pl
from jax.experimental.pallas import tpu as pltpu
from jax.sharding import PartitionSpec as P

SUBSTEPS = 2
PICARD = 3
PHOT = 128
LANES = 128
VMEM_LIMIT = 56 << 20

f32 = jnp.float32
bf16 = jnp.bfloat16


def split(x):
    high = x.astype(bf16)
    return high, (x - high.astype(f32)).astype(bf16)


def twice(x):
    return jnp.concatenate([x, x], axis=1)


def dot(a, b):
    return jnp.dot(a, b, preferred_element_type=f32)


def dot_nt(a, b):
    return lax.dot_general(
        a, b, (((1,), (1,)), ((), ())), precision=lax.Precision.HIGHEST, preferred_element_type=f32
    )


def edge_kernel(conc, wlon, wlat, mix, to_right, to_left, to_north, to_south):
    rows, species, cells = conc.shape
    for g in range(rows):
        turned = conc[g].T
        to_right[0:2, g, :] = turned[cells - 2 : cells]
        to_left[0:2, g, :] = turned[0:2]
    for k, ref in enumerate((wlon, wlat, mix)):
        to_right[2 + k] = jnp.broadcast_to(ref[:, cells - 1 : cells], (rows, species))
        to_left[2 + k] = jnp.broadcast_to(ref[:, 0:1], (rows, species))
    for q in range(2):
        to_north[q * species : (q + 1) * species, :] = conc[rows - 2 + q]
        to_south[q * species : (q + 1) * species, :] = conc[q]
    base = 2 * species
    pad = jnp.zeros((5, cells), f32)
    to_north[base:, :] = jnp.concatenate([r[rows - 1 : rows, :] for r in (wlon, wlat, mix)] + [pad])
    to_south[base:, :] = jnp.concatenate([r[0:1, :] for r in (wlon, wlat, mix)] + [pad])


def table_kernel(
    stoich, rate, night, plan, sun, gather, products, losses, speeds, decay, sun_own, lit, sem
):
    species = decay.shape[0]
    reactions = stoich.shape[1]
    rows = sun_own.shape[0]
    chunks = reactions // LANES
    band = lax.axis_index("lat")
    sector = lax.axis_index("lon")
    fetch = pltpu.make_async_copy(
        sun.at[
            pl.ds(pl.multiple_of(band * rows, 8), rows),
            pl.ds(pl.multiple_of(sector * LANES, LANES), LANES),
        ],
        sun_own,
        sem,
    )
    fetch.start()
    ids = lax.broadcasted_iota(jnp.int32, (species, LANES), 0)
    mats = []
    for k in range(chunks):
        cols = pl.ds(k * LANES, LANES)
        hot = [(stoich[q : q + 1, cols] == ids).astype(f32) for q in range(4)]
        for q in range(2):
            gather[pl.ds(q * reactions + k * LANES, LANES), :] = twice(hot[q].T.astype(bf16))
        products[k] = twice((hot[2] + hot[3]).astype(bf16))
        row = jnp.broadcast_to(rate[0:1, cols], (species, LANES))
        speeds[pl.ds(k * LANES, LANES), :] = row.T
        mats.append(dot_nt(hot[0] * row, hot[1]) + dot_nt(hot[1] * row, hot[0]))
    photo = sum(mats[1 : PHOT // LANES], mats[0])
    dark = sum(mats[PHOT // LANES + 1 :], mats[PHOT // LANES])
    for q, mat in enumerate((dark, photo)):
        high, low = split(mat)
        losses[pl.ds(2 * q * species, species), :] = twice(high)
        losses[pl.ds((2 * q + 1) * species, species), :] = twice(low)
    decay[...] = jnp.broadcast_to(jnp.exp(-night[...]), (species, LANES)).T
    for s in range(SUBSTEPS):
        codes = plan[s, pl.ds(pl.multiple_of(band * rows, 8), rows), :]
        lane = lax.broadcasted_iota(jnp.int32, codes.shape, 1)
        own = jnp.sum(jnp.where(lane == sector, codes, 0).astype(f32), axis=1, keepdims=True)
        lit[s] = jnp.broadcast_to((own >= -1.0).astype(f32), (rows, LANES))
    fetch.wait()


def sweep(start, now, photo, gather, products, losses, speeds):
    reactions = speeds.shape[0]
    species = start.shape[0]
    wide = start.shape[1] // LANES
    weights = jnp.concatenate(split(now), axis=0)
    produced = None
    for k in range(reactions // LANES):
        first = dot(gather[pl.ds(k * LANES, LANES), :], weights)
        second = dot(gather[pl.ds(reactions + k * LANES, LANES), :], weights)
        speed = jnp.concatenate([speeds[pl.ds(k * LANES, LANES), :]] * wide, axis=1)
        made = first * speed * second
        if k < PHOT // LANES:
            made = made * photo
        part = dot(products[k], jnp.concatenate(split(made), axis=0))
        produced = part if produced is None else produced + part
    lost = dot(losses[...], weights)
    s = species
    lost = (lost[0:s] + lost[s : 2 * s]) + photo * (lost[2 * s : 3 * s] + lost[3 * s : 4 * s])
    return (start + produced) / (1.0 + lost)


def chemistry(pairs, suns, lits, decay, tables):
    for s in range(SUBSTEPS):
        now = list(pairs)
        for _ in range(PICARD):
            now = [sweep(p, n, u, *tables) for p, n, u in zip(pairs, now, suns)]
        pairs = [
            jnp.where(l > 0.0, n, p * twice(decay)) for p, n, l in zip(pairs, now, lits[s])
        ]
    return pairs


def step(center, west, east, south, north, wl, wt, mx):
    return (
        center
        - wl * (center - west)
        - wt * (center - south)
        + mx * (east + west + north + south - 4.0 * center)
    )


def block_step(center, west_edge, east_edge, south, north, wl, wt, mx):
    cells = center.shape[1]
    lane = lax.broadcasted_iota(jnp.int32, center.shape, 1)
    west = jnp.where(lane == 0, west_edge, pltpu.roll(center, 1, 1))
    east = jnp.where(lane == cells - 1, east_edge, pltpu.roll(center, cells - 1, 1))
    return step(center, west, east, south, north, wl, wt, mx)


def side_columns(from_left, from_right, to_right, to_left, corners):
    rows = from_left.shape[1]
    far_l, near_l = from_left[0], from_left[1]
    near_r, far_r = from_right[0], from_right[1]
    first, last = to_left[0], to_right[1]
    if corners is None:
        zero = jnp.zeros((1, near_l.shape[1]), f32)
        sl, sr, nl, nr = zero, zero, zero, zero
    else:
        sl, sr, nl, nr = corners
    ls = jnp.concatenate([sl, near_l[:-1]], axis=0)
    ln = jnp.concatenate([near_l[1:], nl], axis=0)
    rs = jnp.concatenate([sr, near_r[:-1]], axis=0)
    rn = jnp.concatenate([near_r[1:], nr], axis=0)
    moved_l = step(near_l, far_l, first, ls, ln, from_left[2], from_left[3], from_left[4])
    moved_r = step(near_r, last, far_r, rs, rn, from_right[2], from_right[3], from_right[4])
    extra = jnp.concatenate([sl, sr, nl, nr], axis=0)
    stack = [near_l, near_r, moved_l, moved_r, extra]
    pad = LANES - 4 * rows - 4
    stack.append(jnp.zeros((pad, near_l.shape[1]), f32))
    return jnp.concatenate(stack, axis=0).T


def inner_kernel(
    conc, wlon, wlat, mix, from_left, from_right, to_right, to_left,
    gather, products, losses, speeds, decay, sun, lit, out, moved,
):
    rows = conc.shape[0]
    group = pl.program_id(0)

    @pl.when(group == 0)
    def _():
        turned = side_columns(from_left, from_right, to_right, to_left, None)

        def col(k, g):
            c = k * rows + g
            return turned[:, c : c + 1]

        def coef(g):
            return wlon[g : g + 1, :], wlat[g : g + 1, :], mix[g : g + 1, :]

        once = {}
        for g in range(1, rows - 1):
            once[g] = block_step(
                conc[g], col(0, g), col(1, g), conc[g - 1], conc[g + 1], *coef(g)
            )
            h = g - 1
            if h >= 2:
                moved[h] = block_step(
                    once[h], col(2, h), col(3, h), once[h - 1], once[h + 1], *coef(h)
                )

    base = 2 + 4 * group
    tables = (gather, products, losses, speeds)

    def row_pair(ref, p):
        return jnp.concatenate([ref[pl.ds(base + 2 * p, 1), :], ref[pl.ds(base + 2 * p + 1, 1), :]], axis=1)

    pairs = [
        jnp.concatenate([moved[base + 2 * p], moved[base + 2 * p + 1]], axis=1) for p in range(2)
    ]
    suns = [row_pair(sun, p) for p in range(2)]
    lits = [[row_pair(lit.at[s], p) for p in range(2)] for s in range(SUBSTEPS)]
    pairs = chemistry(pairs, suns, lits, decay[...], tables)
    for p in range(2):
        out[base + 2 * p] = pairs[p][:, :LANES]
        out[base + 2 * p + 1] = pairs[p][:, LANES:]


def outer_kernel(
    conc, wlon, wlat, mix, from_left, from_right, to_right, to_left,
    from_south, from_north, corner_south, corner_north,
    gather, products, losses, speeds, decay, sun, lit, whole, out,
    halves, sem,
):
    rows, species, cells = conc.shape
    corners = (
        corner_south[0:1, :], corner_south[1:2, :], corner_north[0:1, :], corner_north[1:2, :]
    )
    turned = side_columns(from_left, from_right, to_right, to_left, corners)

    def column(c):
        return turned[:, c : c + 1]

    def field(g):
        if g < 0:
            return from_south[(2 + g) * species : (3 + g) * species, :]
        if g >= rows:
            return from_north[(g - rows) * species : (g - rows + 1) * species, :]
        return conc[g]

    def coef(g):
        base = 2 * species
        if g < 0:
            return [from_south[base + k : base + k + 1, :] for k in range(3)]
        if g >= rows:
            return [from_north[base + k : base + k + 1, :] for k in range(3)]
        return [r[g : g + 1, :] for r in (wlon, wlat, mix)]

    def edge(g, side):
        if g < 0:
            return column(4 * rows + side)
        if g >= rows:
            return column(4 * rows + 2 + side)
        return column(side * rows + g)

    pairs = []
    for low in (0, rows - 2):
        once = {}
        for g in range(low - 1, low + 3):
            once[g] = block_step(
                field(g), edge(g, 0), edge(g, 1), field(g - 1), field(g + 1), *coef(g)
            )
        pairs.append(
            jnp.concatenate(
                [
                    block_step(
                        once[g], column(2 * rows + g), column(3 * rows + g),
                        once[g - 1], once[g + 1], *coef(g),
                    )
                    for g in (low, low + 1)
                ],
                axis=1,
            )
        )

    def row_pair(ref, low):
        return jnp.concatenate([ref[low : low + 1, :], ref[low + 1 : low + 2, :]], axis=1)

    lows = (0, rows - 2)
    suns = [row_pair(sun, low) for low in lows]
    lits = [[row_pair(lit.at[s], low) for low in lows] for s in range(SUBSTEPS)]
    pairs = chemistry(pairs, suns, lits, decay[...], (gather, products, losses, speeds))
    for p in range(2):
        halves[p, 0] = pairs[p][:, :LANES]
        halves[p, 1] = pairs[p][:, LANES:]
    copies = [
        pltpu.make_async_copy(halves.at[p], out.at[pl.ds(lows[p], 2)], sem.at[p]) for p in range(2)
    ]
    for c in copies:
        c.start()
    for c in copies:
        c.wait()


def local(conc, wind_lon, wind_lat, mixing, sun, rate, night_loss, stoich, plan):
    rows, species, cells = conc.shape
    reactions = rate.shape[0]
    lons = lax.axis_size("lon")
    lats = lax.axis_size("lat")
    params = pltpu.CompilerParams(vmem_limit_bytes=VMEM_LIMIT)
    vmem = pl.BlockSpec(memory_space=pltpu.VMEM)
    hbm = pl.BlockSpec(memory_space=pl.ANY)
    shape = jax.ShapeDtypeStruct
    side = shape((5, rows, species), f32)
    ends = shape((2 * species + 8, cells), f32)
    to_right, to_left, to_north, to_south = pl.pallas_call(
        edge_kernel, out_shape=(side, side, ends, ends),
        in_specs=[vmem] * 4, out_specs=[vmem] * 4,
        compiler_params=params, name="edges",
    )(conc, wind_lon, wind_lat, mixing)

    east = [(i, (i + 1) % lons) for i in range(lons)]
    west = [(j, i) for i, j in east]
    north = [(i, i + 1) for i in range(lats - 1)]
    south = [(j, i) for i, j in north]
    from_left = lax.ppermute(to_right, "lon", east)
    from_right = lax.ppermute(to_left, "lon", west)
    from_south = lax.ppermute(to_north, "lat", north)
    from_north = lax.ppermute(to_south, "lat", south)

    tables = pl.pallas_call(
        table_kernel,
        out_shape=(
            shape((2 * reactions, 2 * species), bf16),
            shape((reactions // LANES, species, 2 * LANES), bf16),
            shape((4 * species, 2 * species), bf16),
            shape((reactions, LANES), f32),
            shape((species, LANES), f32),
            shape((rows, LANES), f32),
            shape((SUBSTEPS, rows, LANES), f32),
        ),
        in_specs=[vmem] * 4 + [hbm], out_specs=[vmem] * 7,
        scratch_shapes=[pltpu.SemaphoreType.DMA],
        compiler_params=params, name="tables",
    )(stoich, rate.reshape(1, reactions), night_loss.reshape(1, species), plan, sun)

    def corner(g):
        return jnp.concatenate([from_left[1, g : g + 1], from_right[0, g : g + 1]], axis=0)

    corner_south = lax.ppermute(corner(rows - 1), "lat", north)
    corner_north = lax.ppermute(corner(0), "lat", south)

    inner = pl.pallas_call(
        inner_kernel, grid=((rows - 4) // 4,),
        out_shape=shape(conc.shape, f32),
        in_specs=[vmem] * 15, out_specs=vmem,
        scratch_shapes=[pltpu.VMEM((rows, species, cells), f32)],
        compiler_params=params, name="inner",
    )(conc, wind_lon, wind_lat, mixing, from_left, from_right, to_right, to_left, *tables)

    return pl.pallas_call(
        outer_kernel, out_shape=shape(conc.shape, f32),
        in_specs=[vmem] * 19 + [hbm], out_specs=hbm,
        scratch_shapes=[pltpu.VMEM((2, 2, species, cells), f32), pltpu.SemaphoreType.DMA((2,))],
        input_output_aliases={19: 0},
        compiler_params=params, name="outer",
    )(
        conc, wind_lon, wind_lat, mixing, from_left, from_right, to_right, to_left,
        from_south, from_north, corner_south, corner_north, *tables, inner,
    )


def solution(mesh):
    field = P("lat", None, "lon")
    cell = P("lat", "lon")
    return jax.shard_map(
        local,
        mesh=mesh,
        in_specs=(field, cell, cell, cell, P(), P(), P(), P(), P()),
        out_specs=field,
        check_vma=False,
    )
```

profile of v0, /device:TPU:0, one launch (start us, length us, event | category | flops | bytes accessed | tf_op | source)
XLA Modules:
  0.0 57.9 jit_solution(8308025122219227670)
XLA Ops:
  0.0 2.3 %edges.1 = (f32[5,16,128]{2,1,0:T(8,128)}, f32[5,16,128]{2,1,0:T(8,128)}, f32[264,128]{1,0:T(8,128)}, f32[264,128]{1,0:T(8,128)}) custom-call(f32[16,128,128]{2,1,0:T(8,128)} %conc.5, f32[16,128]{1,0:T(8,128)} %wlon.5, f32[16,128]{1,0:T(8,128)} %wlat.5, f32[16,128]{1,0:T(8,128)} %mix.5), custom_call_target="tpu_custom_call" | custom-call | tf_op jit(solution)/shard_map/edges/pallas_call | solution.py:304
  2.3 0.5 collective-permute-start
  2.8 2.9 %collective-permute-start.1 = (f32[5,16,128]{2,1,0:T(8,128)}, f32[5,16,128]{2,1,0:T(8,128)S(1)}, u32[]{:S(2)}, u32[]{:S(2)}) collective-permute-start(f32[5,16,128]{2,1,0:T(8,128)} %get-tuple-element.17.to_left), channel_id=1, source_target_pairs={{1,0},{2,1},{3,2},{4,3},{5,4},{6,5},{7,6},{0,7},{9,8},{10,9},{11,1... | collective-permute-start | bytes 122888 | tf_op jit(solution)/shard_map/ppermute | solution.py:315
  5.7 4.2 %collective-permute-start.2 = (f32[264,128]{1,0:T(8,128)}, f32[264,128]{1,0:T(8,128)S(1)}, u32[]{:S(2)}, u32[]{:S(2)}) collective-permute-start(f32[264,128]{1,0:T(8,128)} %get-tuple-element.18), channel_id=1, source_target_pairs={{0,8},{8,16},{16,24},{1,9},{9,17},{17,25},{2,10},{10,18},{18,26},{... | collective-permute-start | bytes 405512 | tf_op jit(solution)/shard_map/ppermute | solution.py:316
  9.9 0.0 copy-start.4
  9.9 1.3 %collective-permute-start.3 = (f32[264,128]{1,0:T(8,128)}, f32[264,128]{1,0:T(8,128)S(1)}, u32[]{:S(2)}, u32[]{:S(2)}) collective-permute-start(f32[264,128]{1,0:T(8,128)} %get-tuple-element.19), channel_id=1, source_target_pairs={{8,0},{16,8},{24,16},{9,1},{17,9},{25,17},{10,2},{18,10},{26,18},{... | collective-permute-start | bytes 405512 | tf_op jit(solution)/shard_map/ppermute | solution.py:317
  11.2 0.0 collective-permute-done.from_left
  11.2 0.0 copy-start
  11.2 0.0 collective-permute-done.1.from_right
  11.2 0.0 copy-start.1
  11.3 4.5 %collective-permute-start.4 = (f32[2,128]{1,0:T(2,128)S(1)}, f32[2,128]{1,0:T(2,128)S(1)}, u32[]{:S(2)}, u32[]{:S(2)}) collective-permute-start(f32[2,128]{1,0:T(2,128)S(1)} %pad_maximum_fusion), channel_id=1, source_target_pairs={{0,8},{8,16},{16,24},{1,9},{9,17},{17,25},{2,10},{10,18},{18,26},{... | collective-permute-start | bytes 3080 | tf_op jit(solution)/shard_map/ppermute | solution.py:338
  15.8 1.3 %collective-permute-start.5 = (f32[2,128]{1,0:T(2,128)S(1)}, f32[2,128]{1,0:T(2,128)S(1)}, u32[]{:S(2)}, u32[]{:S(2)}) collective-permute-start(f32[2,128]{1,0:T(2,128)S(1)} %pad_maximum_fusion.1), channel_id=1, source_target_pairs={{8,0},{16,8},{24,16},{9,1},{17,9},{25,17},{10,2},{18,10},{26,18},{... | collective-permute-start | bytes 3080 | tf_op jit(solution)/shard_map/ppermute | solution.py:339
  17.1 0.7 %copy.11.plan = s32[2,64,8]{2,1,0:T(8,128)} copy(s32[2,64,8]{1,2,0:T(8,128)S(1)} %copy-done.4) | data formatting | bytes 8192 | tf_op args[8]
  17.9 3.3 %tables.1 = (bf16[1024,256]{1,0:T(8,128)(2,1)}, bf16[4,128,256]{2,1,0:T(8,128)(2,1)}, bf16[512,256]{1,0:T(8,128)(2,1)}, f32[512,128]{1,0:T(8,128)}, f32[128,128]...) custom-call(s32[4,512]{1,0:T(4,128)} %stoich.1, f32[1,512]{1,0:T(1,128)} %bitcast.10, f32[1,128]{1,0:T(1,128)} %bitcast.11, ...), custom_call_target="tpu_custom_call" | custom-call | tf_op jit(solution)/shard_map/tables/pallas_call | solution.py:319
  21.2 25.1 %inner.1.whole = f32[16,128,128]{2,1,0:T(8,128)} custom-call(f32[16,128,128]{2,1,0:T(8,128)} %conc.5, f32[16,128]{1,0:T(8,128)} %wlon.5, f32[16,128]{1,0:T(8,128)} %wlat.5, f32[16,128]{1,0:T(8,128)} %mix.5, f32[5,16,128]{2,1,0:T(8,128)} %copy-done, f32[5,16,128]{2,1,0:T(8,128)} %copy-done.1, f32[5,16,128]{2,1,0:T(8,128)} %get-tuple-element.16.to_right, ...), custom_call_target="tpu_custom_call" | custom-call | tf_op jit(solution)/shard_map/inner/pallas_call | solution.py:341
  46.3 0.0 collective-permute-done.4.corner_south
  46.3 0.0 collective-permute-done.5.corner_north
  46.3 0.0 collective-permute-done.2.from_south
  46.3 0.0 collective-permute-done.3.from_north
  46.3 0.5 copy-done.5
  46.8 0.0 copy-done.6
  46.9 0.1 copy-done.2
  47.0 0.7 %copy-done.3 = f32[264,128]{1,0:T(8,128)} copy-done((f32[264,128]{1,0:T(8,128)}, f32[264,128]{1,0:T(8,128)S(1)}, u32[]{:S(2)}) %copy-start.3) | copy-done | bytes 135192
  47.6 10.1 %outer.1 = f32[16,128,128]{2,1,0:T(8,128)} custom-call(f32[16,128,128]{2,1,0:T(8,128)} %conc.5, f32[16,128]{1,0:T(8,128)} %wlon.5, f32[16,128]{1,0:T(8,128)} %wlat.5, f32[16,128]{1,0:T(8,128)} %mix.5, f32[5,16,128]{2,1,0:T(8,128)} %copy-done, f32[5,16,128]{2,1,0:T(8,128)} %copy-done.1, ...), custom_call_target="tpu_custom_call", output_to_operand_aliasing={{}: (19, {})} | custom-call | tf_op jit(solution)/shard_map/outer/pallas_call | solution.py:349
  (11 shorter events, 0.0 us)
Async XLA Ops:
  2.3 8.9 %collective-permute-start = (f32[5,16,128]{2,1,0:T(8,128)}, f32[5,16,128]{2,1,0:T(8,128)S(1)}, u32[]{:S(2)}, u32[]{:S(2)}) collective-permute-start(f32[5,16,128]{2,1,0:T(8,128)} %get-tuple-element.16.to_right), channel_id=1, source_target_pairs={{0,1},{1,2},{2,3},{3,4},{4,5},{5,6},{6,7},{7,0},{8,9},{9,10},{10,1... | collective-permute-start | bytes 122888 | tf_op jit(solution)/shard_map/ppermute | solution.py:314
  2.8 8.5 %collective-permute-start.1 = (f32[5,16,128]{2,1,0:T(8,128)}, f32[5,16,128]{2,1,0:T(8,128)S(1)}, u32[]{:S(2)}, u32[]{:S(2)}) collective-permute-start(f32[5,16,128]{2,1,0:T(8,128)} %get-tuple-element.17.to_left), channel_id=1, source_target_pairs={{1,0},{2,1},{3,2},{4,3},{5,4},{6,5},{7,6},{0,7},{9,8},{10,9},{11,1... | collective-permute-start | bytes 122888 | tf_op jit(solution)/shard_map/ppermute | solution.py:315
  5.7 40.6 %collective-permute-start.2 = (f32[264,128]{1,0:T(8,128)}, f32[264,128]{1,0:T(8,128)S(1)}, u32[]{:S(2)}, u32[]{:S(2)}) collective-permute-start(f32[264,128]{1,0:T(8,128)} %get-tuple-element.18), channel_id=1, source_target_pairs={{0,8},{8,16},{16,24},{1,9},{9,17},{17,25},{2,10},{10,18},{18,26},{... | collective-permute-start | bytes 405512 | tf_op jit(solution)/shard_map/ppermute | solution.py:316
  9.9 7.3 %copy-start.4 = (s32[2,64,8]{1,2,0:T(8,128)S(1)}, s32[2,64,8]{1,2,0:T(8,128)}, u32[]{:S(2)}) copy-start(s32[2,64,8]{1,2,0:T(8,128)} %param.17) | copy-start | bytes 12292
  9.9 36.4 %collective-permute-start.3 = (f32[264,128]{1,0:T(8,128)}, f32[264,128]{1,0:T(8,128)S(1)}, u32[]{:S(2)}, u32[]{:S(2)}) collective-permute-start(f32[264,128]{1,0:T(8,128)} %get-tuple-element.19), channel_id=1, source_target_pairs={{8,0},{16,8},{24,16},{9,1},{17,9},{25,17},{10,2},{18,10},{26,18},{... | collective-permute-start | bytes 405512 | tf_op jit(solution)/shard_map/ppermute | solution.py:317
  11.2 6.7 %copy-start = (f32[5,16,128]{2,1,0:T(8,128)}, f32[5,16,128]{2,1,0:T(8,128)S(1)}, u32[]{:S(2)}) copy-start(f32[5,16,128]{2,1,0:T(8,128)S(1)} %collective-permute-done.from_left) | copy-start | bytes 122884
  11.2 6.7 %copy-start.1 = (f32[5,16,128]{2,1,0:T(8,128)}, f32[5,16,128]{2,1,0:T(8,128)S(1)}, u32[]{:S(2)}) copy-start(f32[5,16,128]{2,1,0:T(8,128)S(1)} %collective-permute-done.1.from_right) | copy-start | bytes 122884
  11.3 35.0 %collective-permute-start.4 = (f32[2,128]{1,0:T(2,128)S(1)}, f32[2,128]{1,0:T(2,128)S(1)}, u32[]{:S(2)}, u32[]{:S(2)}) collective-permute-start(f32[2,128]{1,0:T(2,128)S(1)} %pad_maximum_fusion), channel_id=1, source_target_pairs={{0,8},{8,16},{16,24},{1,9},{9,17},{17,25},{2,10},{10,18},{18,26},{... | collective-permute-start | bytes 3080 | tf_op jit(solution)/shard_map/ppermute | solution.py:338
  15.8 30.4 %collective-permute-start.5 = (f32[2,128]{1,0:T(2,128)S(1)}, f32[2,128]{1,0:T(2,128)S(1)}, u32[]{:S(2)}, u32[]{:S(2)}) collective-permute-start(f32[2,128]{1,0:T(2,128)S(1)} %pad_maximum_fusion.1), channel_id=1, source_target_pairs={{8,0},{16,8},{24,16},{9,1},{17,9},{25,17},{10,2},{18,10},{26,18},{... | collective-permute-start | bytes 3080 | tf_op jit(solution)/shard_map/ppermute | solution.py:339
  46.3 0.6 copy-start.5
  46.3 0.6 %copy-start.6 = (f32[2,128]{1,0:T(2,128)}, f32[2,128]{1,0:T(2,128)S(1)}, u32[]{:S(2)}) copy-start(f32[2,128]{1,0:T(2,128)S(1)} %collective-permute-done.5.corner_north) | copy-start | bytes 3076
  46.3 0.7 %copy-start.2 = (f32[264,128]{1,0:T(8,128)}, f32[264,128]{1,0:T(8,128)S(1)}, u32[]{:S(2)}) copy-start(f32[264,128]{1,0:T(8,128)S(1)} %collective-permute-done.2.from_south) | copy-start | bytes 405508
  47.0 0.7 %copy-start.3 = (f32[264,128]{1,0:T(8,128)}, f32[264,128]{1,0:T(8,128)S(1)}, u32[]{:S(2)}) copy-start(f32[264,128]{1,0:T(8,128)S(1)} %collective-permute-done.3.from_north) | copy-start | bytes 405508
where the time goes:
time: 58.3 us; the launch traced here: 57.9 us
  Pallas kernels  40.8 us (70%)
  starting transfers between devices  14.7 us (25%)
  local copies, waits for them, and re-layouts  2.05 us (4%)
    pallas_call x1, Pallas kernels, local(): pl.pallas_call(inner_kernel, grid=((rows - 4) // 4,), out_shape=shape(con...  25.1 us
    pallas_call x1, Pallas kernels, local(): pl.pallas_call(outer_kernel, out_shape=shape(conc.shape, f32), in_specs=[...  10.1 us
    ppermute x1, starting transfers between devices, local(): corner_south = lax.ppermute(corner(rows - 1), 'lat', north)  4.55 us
    ppermute x1, starting transfers between devices, local(): from_south = lax.ppermute(to_north, 'lat', north)  4.18 us
    pallas_call x1, Pallas kernels, local(): pl.pallas_call(table_kernel, out_shape=(shape((2 * reactions, 2 * species...  3.27 us
    ppermute x1, starting transfers between devices, local(): from_right = lax.ppermute(to_left, 'lon', west)  2.93 us
    pallas_call x1, Pallas kernels, local(): pl.pallas_call(edge_kernel, out_shape=(side, side, ends, ends), in_specs=...  2.3 us
    unnamed x15, local copies, waits for them, and re-layouts  2.05 us
  transfers between devices with their start and end apart: 6, of which 0 were waited for; matrix products, arithmetic and copies ran while one was open for 1% of the time, Pallas kernels for 49%

commit v1 on v0

v1 whole, which is shorter than its diff:
```python
import jax
import jax.numpy as jnp
from jax import lax
from jax.experimental import pallas as pl
from jax.experimental.pallas import tpu as pltpu
from jax.sharding import PartitionSpec as P

SUBSTEPS = 2
PICARD = 3
PHOT = 128
LANES = 128
VMEM_LIMIT = 48 << 20
KEPT = jax.ShapeDtypeStruct

f32 = jnp.float32
bf16 = jnp.bfloat16


def split(x):
    high = x.astype(bf16)
    return high, (x - high.astype(f32)).astype(bf16)


def twice(x):
    return jnp.concatenate([x, x], axis=1)


def dot(a, b):
    return jnp.dot(a, b, preferred_element_type=f32)


def iota(shape, axis):
    return lax.broadcasted_iota(jnp.int32, shape, axis)


def edge_kernel(conc, wlon, wlat, mix, to_pair, to_other, own, to_north, to_south, columns):
    rows, species, cells = conc.shape
    lane = iota((species, cells), 1)
    picked = jnp.zeros((species, cells), f32)
    for g in range(rows):
        turned = pltpu.roll(conc[g], (4 * g + 2) % cells, 1)
        picked = jnp.where((lane >= 4 * g) & (lane < 4 * g + 4), turned, picked)
    columns[...] = picked.T
    last2, last1, first1, first2 = [columns[pl.ds(q, rows, stride=4), :] for q in range(4)]
    even = lax.rem(lax.axis_index("lon"), 2) == 0

    def put(k, right, left):
        to_pair[k] = jnp.where(even, right, left)
        to_other[k] = jnp.where(even, left, right)

    put(0, last1, first1)
    put(1, last2, first2)
    for k, ref in enumerate((wlon, wlat, mix)):
        put(
            2 + k,
            jnp.broadcast_to(ref[:, cells - 1 : cells], (rows, species)),
            jnp.broadcast_to(ref[:, 0:1], (rows, species)),
        )
    own[0] = first1
    own[1] = last1
    for q in range(2):
        to_north[q * species : (q + 1) * species, :] = conc[rows - 2 + q]
        to_south[q * species : (q + 1) * species, :] = conc[q]
    base = 2 * species
    pad = jnp.zeros((5, cells), f32)
    to_north[base : base + 8, :] = jnp.concatenate([r[rows - 1 : rows, :] for r in (wlon, wlat, mix)] + [pad])
    to_south[base : base + 8, :] = jnp.concatenate([r[0:1, :] for r in (wlon, wlat, mix)] + [pad])


def sides(of_pair, of_other):
    even = lax.rem(lax.axis_index("lon"), 2) == 0
    return (
        lambda k: jnp.where(even, of_other[k], of_pair[k]),
        lambda k: jnp.where(even, of_pair[k], of_other[k]),
    )


def corner_kernel(of_pair, of_other, _, __, ___, to_north, to_south, ends, sem):
    rows = of_pair.shape[1]
    left, right = sides(of_pair, of_other)
    near_l, near_r = left(0), right(0)
    pad = jnp.zeros((6, near_l.shape[1]), f32)
    copies = []
    for p, (g, ref) in enumerate(((rows - 1, to_north), (0, to_south))):
        ends[p] = jnp.concatenate([near_l[g : g + 1], near_r[g : g + 1], pad], axis=0)
        dest = ref.at[pl.ds(ref.shape[0] - 8, 8), :]
        copies.append(pltpu.make_async_copy(ends.at[p], dest, sem.at[p]))
        copies[p].start()
    for c in copies:
        c.wait()


def table_kernel(
    stoich, rate, night, plan, sun, gather, products, speeds, decay, sun_own, lit, turned, sem
):
    species = decay.shape[0]
    reactions = stoich.shape[1]
    rows = sun_own.shape[0]
    chunks = reactions // LANES
    band = lax.axis_index("lat")
    sector = lax.axis_index("lon")
    fetch = pltpu.make_async_copy(
        sun.at[
            pl.ds(pl.multiple_of(band * rows, 8), rows),
            pl.ds(pl.multiple_of(sector * LANES, LANES), LANES),
        ],
        sun_own,
        sem,
    )
    fetch.start()
    down = iota((species, LANES), 0)
    across = iota((LANES, species), 1).astype(f32)
    mats = []
    for k in range(chunks):
        cols = pl.ds(k * LANES, LANES)
        codes = stoich[:, cols]
        row = rate[0:1, cols]
        small = jnp.concatenate([codes.astype(f32), row, jnp.zeros((3, LANES), f32)], axis=0).T
        hot = [(codes[q : q + 1, :] == down).astype(f32) for q in range(4)]
        seconds = None
        for q in range(2):
            picks = (small[:, q : q + 1] == across).astype(f32).astype(bf16)
            gather[pl.ds(q * reactions + k * LANES, LANES), :] = twice(picks)
            seconds = picks
        products[:, 2 * k * LANES : (2 * k + 2) * LANES] = twice((hot[2] + hot[3]).astype(bf16))
        speeds[pl.ds(k * LANES, LANES), :] = jnp.broadcast_to(small[:, 4:5], (LANES, LANES))
        parts = jnp.concatenate(split(hot[0] * row), axis=0)
        both = dot(parts, seconds)
        mats.append(both[:species] + both[species:])
    photo = sum(mats[1 : PHOT // LANES], mats[0])
    dark = sum(mats[PHOT // LANES + 1 :], mats[PHOT // LANES])
    for q, mat in enumerate((dark, photo)):
        high, low = split(mat + mat.T)
        base = 2 * reactions + 2 * q * species
        gather[pl.ds(base, species), :] = twice(high)
        gather[pl.ds(base + species, species), :] = twice(low)
    strip = []
    for s in range(SUBSTEPS):
        codes = plan[s]
        own = jnp.where(iota(codes.shape, 0) == sector, codes, 0).astype(f32)
        strip.append(jnp.sum(own, axis=0, keepdims=True))
    lats = plan.shape[2]
    flags = jnp.concatenate(strip + [jnp.zeros((8 - SUBSTEPS, lats), f32)], axis=0)
    flags = jnp.concatenate([flags, jnp.zeros((8, LANES - lats), f32)], axis=1)
    fade = jnp.exp(-night[...])
    spread = jnp.concatenate([flags, fade, jnp.zeros((7, LANES), f32)], axis=0).T
    decay[...] = jnp.broadcast_to(spread[:, 8:9], (species, LANES))
    for s in range(SUBSTEPS):
        turned[...] = jnp.broadcast_to(spread[:, s : s + 1], turned.shape)
        mine = turned[pl.ds(pl.multiple_of(band * rows, 8), rows), :]
        lit[s] = (mine >= -1.0).astype(f32)
    fetch.wait()


def sweep(starts, nows, photos, gather, products, speeds):
    reactions = speeds.shape[0]
    species = starts[0].shape[0]
    weights = [jnp.concatenate(split(now), axis=0) for now in nows]
    losses = [dot(gather[2 * reactions :, :], w) for w in weights]
    made = [[] for _ in nows]
    for k in range(reactions // LANES):
        speed = twice(speeds[k * LANES : (k + 1) * LANES, :])
        for p, w in enumerate(weights):
            first = dot(gather[k * LANES : (k + 1) * LANES, :], w)
            second = dot(gather[reactions + k * LANES : reactions + (k + 1) * LANES, :], w)
            flow = first * speed * second
            if k < PHOT // LANES:
                flow = flow * photos[p]
            made[p].extend(split(flow))
    after = []
    s = species
    for start, flows, loss, photo in zip(starts, made, losses, photos):
        produced = dot(products[...], jnp.concatenate(flows, axis=0))
        lost = (loss[0:s] + loss[s : 2 * s]) + photo * (loss[2 * s : 3 * s] + loss[3 * s :])
        after.append((start + produced) / (1.0 + lost))
    return after


def chemistry(pairs, lows, decay, sun, lit, tables):
    def both(ref, low):
        return jnp.concatenate([ref[low : low + 1, :], ref[low + 1 : low + 2, :]], axis=1)

    photos = [both(sun, low) for low in lows]
    fade = twice(decay[...])
    for s in range(SUBSTEPS):
        now = list(pairs)
        for _ in range(PICARD):
            now = sweep(pairs, now, photos, *tables)
        pairs = [
            jnp.where(both(lit.at[s], low) > 0.0, n, p * fade)
            for p, n, low in zip(pairs, now, lows)
        ]
    return pairs


def step(center, west, east, south, north, wl, wt, mx):
    return (
        center
        - wl * (center - west)
        - wt * (center - south)
        + mx * (east + west + north + south - 4.0 * center)
    )


def block_step(center, west_edge, east_edge, south, north, wl, wt, mx):
    cells = center.shape[1]
    lane = lax.broadcasted_iota(jnp.int32, center.shape, 1)
    west = jnp.where(lane == 0, west_edge, pltpu.roll(center, 1, 1))
    east = jnp.where(lane == cells - 1, east_edge, pltpu.roll(center, cells - 1, 1))
    return step(center, west, east, south, north, wl, wt, mx)


def side_columns(of_pair, of_other, own, corners):
    rows = of_pair.shape[1]
    left, right = sides(of_pair, of_other)
    near_l, near_r = left(0), right(0)
    zero = jnp.zeros((1, near_l.shape[1]), f32)
    sl, sr, nl, nr = corners if corners else (zero, zero, zero, zero)

    def moved(near, west, east, south, north, side):
        south = jnp.concatenate([south, near[:-1]], axis=0)
        north = jnp.concatenate([near[1:], north], axis=0)
        return step(near, west, east, south, north, side(2), side(3), side(4))

    moved_l = moved(near_l, left(1), own[0], sl, nl, left)
    moved_r = moved(near_r, own[1], right(1), sr, nr, right)
    pad = jnp.zeros((LANES - 4 * rows - 4, near_l.shape[1]), f32)
    stack = [near_l, near_r, moved_l, moved_r, sl, sr, nl, nr, pad]
    return jnp.concatenate(stack, axis=0).T


def moved_pairs(runs, field, coef, turned, rows):
    def column(c):
        return turned[:, c : c + 1]

    def edge(g, side):
        if g < 0:
            return column(4 * rows + side)
        if g >= rows:
            return column(4 * rows + 2 + side)
        return column(side * rows + g)

    pairs, lows = [], []
    for low, count in runs:
        once, twofold = {}, {}
        for g in range(low - 1, low + count + 1):
            once[g] = block_step(
                field(g), edge(g, 0), edge(g, 1), field(g - 1), field(g + 1), *coef(g)
            )
            h = g - 1
            if h >= low:
                twofold[h] = block_step(
                    once[h], column(2 * rows + h), column(3 * rows + h),
                    once[h - 1], once[h + 1], *coef(h),
                )
        for h in range(low, low + count, 2):
            lows.append(h)
            pairs.append(jnp.concatenate([twofold[h], twofold[h + 1]], axis=1))
    return pairs, lows


def store_pairs(pairs, lows, out, stage, sem):
    copies = []
    for p, low in enumerate(lows):
        stage[2 * p] = pairs[p][:, :LANES]
        stage[2 * p + 1] = pairs[p][:, LANES:]
        copies.append(
            pltpu.make_async_copy(stage.at[pl.ds(2 * p, 2)], out.at[pl.ds(low, 2)], sem.at[p])
        )
        copies[p].start()
    for c in copies:
        c.wait()


def inner_kernel(
    conc, wlon, wlat, mix, of_pair, of_other, own,
    gather, products, speeds, decay, sun, lit, out, stage, sem,
):
    rows = conc.shape[0]
    turned = side_columns(of_pair, of_other, own, None)

    def coef(g):
        return [r[g : g + 1, :] for r in (wlon, wlat, mix)]

    runs = [(rows // 4, rows // 2)]
    pairs, lows = moved_pairs(runs, lambda g: conc[g], coef, turned, rows)
    pairs = chemistry(pairs, lows, decay, sun, lit, (gather, products, speeds))
    store_pairs(pairs, lows, out, stage, sem)


def outer_kernel(
    conc, wlon, wlat, mix, of_pair, of_other, own, of_south, of_north,
    gather, products, speeds, decay, sun, lit, _, out, stage, sem,
):
    rows, species, cells = conc.shape
    base = 2 * species
    band = lax.axis_index("lat")
    below = jnp.where(band > 0, 1.0, 0.0)
    above = jnp.where(band < lax.axis_size("lat") - 1, 1.0, 0.0)
    corners = [
        r[base + 8 + k : base + 9 + k, :] * inside
        for r, inside in ((of_south, below), (of_north, above))
        for k in range(2)
    ]
    turned = side_columns(of_pair, of_other, own, corners)

    def field(g):
        if g < 0:
            return of_south[(2 + g) * species : (3 + g) * species, :] * below
        if g >= rows:
            return of_north[(g - rows) * species : (g - rows + 1) * species, :] * above
        return conc[g]

    def coef(g):
        if g < 0:
            return [of_south[base + k : base + k + 1, :] * below for k in range(3)]
        if g >= rows:
            return [of_north[base + k : base + k + 1, :] * above for k in range(3)]
        return [r[g : g + 1, :] for r in (wlon, wlat, mix)]

    runs = [(0, rows // 4), (rows - rows // 4, rows // 4)]
    pairs, lows = moved_pairs(runs, field, coef, turned, rows)
    pairs = chemistry(pairs, lows, decay, sun, lit, (gather, products, speeds))
    store_pairs(pairs, lows, out, stage, sem)


def local(conc, wind_lon, wind_lat, mixing, sun, rate, night_loss, stoich, plan):
    rows, species, cells = conc.shape
    reactions = rate.shape[0]
    lons = lax.axis_size("lon")
    lats = lax.axis_size("lat")
    params = pltpu.CompilerParams(vmem_limit_bytes=VMEM_LIMIT)
    vmem = pl.BlockSpec(memory_space=pltpu.VMEM)
    hbm = pl.BlockSpec(memory_space=pl.ANY)

    def shape(*dims, dtype=f32):
        return KEPT(dims, dtype)

    side = shape(5, rows, species)
    ends = shape(2 * species + 16, cells)
    to_pair, to_other, own, to_north, to_south = pl.pallas_call(
        edge_kernel, out_shape=(side, side, shape(2, rows, species), ends, ends),
        in_specs=[vmem] * 4, out_specs=[vmem] * 5,
        scratch_shapes=[pltpu.VMEM((cells, species), f32)],
        compiler_params=params, name="edges",
    )(conc, wind_lon, wind_lat, mixing)

    pair = [(i, i ^ 1) for i in range(lons)]
    other = [(i, (i - 1) % lons if i % 2 == 0 else (i + 1) % lons) for i in range(lons)]
    north = [(i, (i + 1) % lats) for i in range(lats)]
    south = [(j, i) for i, j in north]
    of_pair = lax.ppermute(to_pair, "lon", pair)
    of_other = lax.ppermute(to_other, "lon", other)

    tables = pl.pallas_call(
        table_kernel,
        out_shape=(
            shape(2 * reactions + 4 * species, 2 * species, dtype=bf16),
            shape(species, 2 * reactions, dtype=bf16),
            shape(reactions, LANES),
            shape(species, LANES),
            shape(rows, LANES),
            shape(SUBSTEPS, rows, LANES),
        ),
        in_specs=[vmem] * 4 + [hbm], out_specs=[vmem] * 6,
        scratch_shapes=[pltpu.VMEM((LANES, LANES), f32), pltpu.SemaphoreType.DMA],
        cost_estimate=pl.CostEstimate(flops=10**9, transcendentals=0, bytes_accessed=2 * 10**6),
        compiler_params=params, name="tables",
    )(
        stoich, rate.reshape(1, reactions), night_loss.reshape(1, species),
        jnp.swapaxes(plan, 1, 2), sun,
    )

    to_north, to_south = pl.pallas_call(
        corner_kernel, out_shape=(ends, ends),
        in_specs=[vmem] * 2 + [hbm] * 3, out_specs=[hbm] * 2,
        scratch_shapes=[pltpu.VMEM((2, 8, species), f32), pltpu.SemaphoreType.DMA((2,))],
        input_output_aliases={2: 0, 3: 1},
        compiler_params=params, name="corners",
    )(of_pair, of_other, to_north, to_south, tables[4])
    of_south = lax.ppermute(to_north, "lat", north)
    of_north = lax.ppermute(to_south, "lat", south)

    shared = (conc, wind_lon, wind_lat, mixing, of_pair, of_other, own)
    scratch = [pltpu.VMEM((rows // 2, species, cells), f32), pltpu.SemaphoreType.DMA((rows // 4,))]
    inner = pl.pallas_call(
        inner_kernel, out_shape=jax.ShapeDtypeStruct(conc.shape, f32),
        in_specs=[vmem] * 13, out_specs=hbm, scratch_shapes=scratch,
        compiler_params=params, name="inner",
    )(*shared, *tables)
    return pl.pallas_call(
        outer_kernel, out_shape=jax.ShapeDtypeStruct(conc.shape, f32),
        in_specs=[vmem] * 15 + [hbm], out_specs=hbm, scratch_shapes=scratch,
        input_output_aliases={15: 0},
        compiler_params=params, name="outer",
    )(*shared, of_south, of_north, *tables, inner)


def solution(mesh):
    field = P("lat", None, "lon")
    cell = P("lat", "lon")
    return jax.shard_map(
        local,
        mesh=mesh,
        in_specs=(field, cell, cell, cell, P(), P(), P(), P(), P()),
        out_specs=field,
        check_vma=False,
    )
```

time: 58.3 us -> 33.6 us (0.58)
  Pallas kernels: 40.8 us -> 21 us
  starting transfers between devices: 14.7 us -> 7.95 us
  local copies, waits for them, and re-layouts: 2.05 us -> 3.97 us
    pallas_call x4 -> x5, Pallas kernels: 40.8 us -> 21 us  [the longest x1 10 us: local(): pl.pallas_call(outer_kernel, out_shape=jax.ShapeDtypeStruct(conc.shape, f...]
    ppermute x6 -> x4, starting transfers between devices: 14.7 us -> 7.95 us  [the longest x1 3.56 us: local(): of_other = lax.ppermute(to_other, 'lon', other)]
    unnamed x15 -> x20, local copies, waits for them, and re-layouts: 2.05 us -> 3.97 us
  transfers between devices with their start and end apart: 6 -> 4, of which waited for: 0 -> 0; matrix products, arithmetic and copies ran while one was open for 1% -> 0% of each run, Pallas kernels for 49% -> 32%
where the time goes in v1:
time: 33.6 us; the launch traced here: 33.2 us
  Pallas kernels  21 us (62%)
  starting transfers between devices  7.95 us (24%)
  local copies, waits for them, and re-layouts  3.97 us (12%)
    pallas_call x1, Pallas kernels, local(): pl.pallas_call(outer_kernel, out_shape=jax.ShapeDtypeStruct(conc.shape, f...  10 us
    pallas_call x1, Pallas kernels, local(): pl.pallas_call(inner_kernel, out_shape=jax.ShapeDtypeStruct(conc.shape, f...  9.6 us
    unnamed x20, local copies, waits for them, and re-layouts  3.97 us
    ppermute x1, starting transfers between devices, local(): of_other = lax.ppermute(to_other, 'lon', other)  3.56 us
    ppermute x1, starting transfers between devices, local(): of_north = lax.ppermute(to_south, 'lat', south)  2.09 us
    ppermute x1, starting transfers between devices, local(): of_south = lax.ppermute(to_north, 'lat', north)  1.79 us
    pallas_call x1, Pallas kernels, local(): pl.pallas_call(table_kernel, out_shape=(shape(2 * reactions + 4 * species...  0.96 us
  transfers between devices with their start and end apart: 4, of which 0 were waited for; matrix products, arithmetic and copies ran while one was open for 0% of the time, Pallas kernels for 32%

profile of v1, /device:TPU:0, one launch (start us, length us, event | category | flops | bytes accessed | tf_op | source)
XLA Modules:
  0.0 33.2 jit_solution(14491623019567696673)
XLA Ops:
  0.0 0.0 copy-start
  0.0 1.2 %copy-done = f32[16,128,128]{2,1,0:T(8,128)S(1)} copy-done((f32[16,128,128]{2,1,0:T(8,128)S(1)}, f32[16,128,128]{2,1,0:T(8,128)}, u32[]{:S(2)}) %copy-start) | copy-done | bytes 1048600
  1.2 0.7 %copy-done.2 = f32[16,128]{1,0:T(8,128)S(1)} copy-done((f32[16,128]{1,0:T(8,128)S(1)}, f32[16,128]{1,0:T(8,128)}, u32[]{:S(2)}) %copy-start.2) | copy-done | bytes 8216
  1.9 0.7 %copy-done.3 = f32[16,128]{1,0:T(8,128)S(1)} copy-done((f32[16,128]{1,0:T(8,128)S(1)}, f32[16,128]{1,0:T(8,128)}, u32[]{:S(2)}) %copy-start.3) | copy-done | bytes 8216
  2.6 0.7 %copy-done.4 = f32[16,128]{1,0:T(8,128)S(1)} copy-done((f32[16,128]{1,0:T(8,128)S(1)}, f32[16,128]{1,0:T(8,128)}, u32[]{:S(2)}) %copy-start.4) | copy-done | bytes 8216
  3.3 0.4 %edges.1 = (f32[5,16,128]{2,1,0:T(8,128)S(1)}, f32[5,16,128]{2,1,0:T(8,128)S(1)}, f32[2,16,128]{2,1,0:T(8,128)S(1)}, f32[272,128]{1,0:T(8,128)S(1)}, f32[272,128]{1,0:T(8,128)S(1)}) custom-call(f32[16,128,128]{2,1,0:T(8,128)S(1)} %copy-done, f32[16,128]{1,0:T(8,128)S(1)} %copy-done.2, f32[16,128]{1,0:T(8,128)S(1)} %copy-done.3, f32[16,128]{1,0:T(8,128)S(1)} %copy-done.4), custom_call_target="tpu_custom_call" | custom-call | tf_op jit(solution)/shard_map/edges/pallas_call | solution.py:341
  3.7 0.0 copy-start.6
  3.7 0.5 %collective-permute-start = (f32[5,16,128]{2,1,0:T(8,128)S(1)}, f32[5,16,128]{2,1,0:T(8,128)S(1)}, u32[]{:S(2)}, u32[]{:S(2)}) collective-permute-start(f32[5,16,128]{2,1,0:T(8,128)S(1)} %get-tuple-element.18), channel_id=1, source_target_pairs={{0,1},{1,0},{2,3},{3,2},{4,5},{5,4},{6,7},{7,6},{8,9},{9,8},{10,11... | collective-permute-start | bytes 122888 | tf_op jit(solution)/shard_map/ppermute | solution.py:352
  4.3 3.6 %collective-permute-start.1 = (f32[5,16,128]{2,1,0:T(8,128)S(1)}, f32[5,16,128]{2,1,0:T(8,128)S(1)}, u32[]{:S(2)}, u32[]{:S(2)}) collective-permute-start(f32[5,16,128]{2,1,0:T(8,128)S(1)} %get-tuple-element.19), channel_id=1, source_target_pairs={{0,7},{1,2},{2,1},{3,4},{4,3},{5,6},{6,5},{7,0},{8,15},{9,10},{10,... | collective-permute-start | bytes 122888 | tf_op jit(solution)/shard_map/ppermute | solution.py:353
  7.8 0.0 copy-done.5
  7.8 0.0 copy-done.7
  7.8 0.0 copy-done.8
  7.8 0.0 copy-done.6
  7.8 0.6 %copy-done.9 = f32[128]{0:T(128)S(1)} copy-done((f32[128]{0:T(128)S(1)}, f32[128]{0:T(128)}, u32[]{:S(2)}) %copy-start.9) | copy-done | bytes 536
  8.5 1.0 %tables.1 = (bf16[1536,256]{1,0:T(8,128)(2,1)S(1)}, bf16[128,1024]{1,0:T(8,128)(2,1)S(1)}, f32[512,128]{1,0:T(8,128)S(1)}, f32[128,128]{1,0:T(8,128)S(1)}, f32[1...) custom-call(s32[4,512]{1,0:T(4,128)S(1)} %copy-done.6, f32[1,512]{1,0:T(1,128)S(1)} %bitcast.4, f32[1,128]{1,0:T(1,128)S(1)} %bitcast.5, ...), custom_call_target="tpu_custom_call" | custom-call | flops 1000000000 | bytes 2000000 | tf_op jit(solution)/shard_map/tables/pallas_call | solution.py:355
  9.4 0.0 collective-permute-done.of_pair
  9.5 0.0 collective-permute-done.1.of_other
  9.6 1.8 %collective-permute-start.2 = (f32[272,128]{1,0:T(8,128)S(1)}, f32[272,128]{1,0:T(8,128)S(1)}, u32[]{:S(2)}, u32[]{:S(2)}) collective-permute-start(f32[272,128]{1,0:T(8,128)S(1)} %get-tuple-element.24), channel_id=1, source_target_pairs={{0,8},{8,16},{16,24},{24,0},{1,9},{9,17},{17,25},{25,1},{2,10},{10... | collective-permute-start | bytes 417800 | tf_op jit(solution)/shard_map/ppermute | solution.py:381
  11.3 2.1 %collective-permute-start.3 = (f32[272,128]{1,0:T(8,128)S(1)}, f32[272,128]{1,0:T(8,128)S(1)}, u32[]{:S(2)}, u32[]{:S(2)}) collective-permute-start(f32[272,128]{1,0:T(8,128)S(1)} %get-tuple-element.25), channel_id=1, source_target_pairs={{8,0},{16,8},{24,16},{0,24},{9,1},{17,9},{25,17},{1,25},{10,2},{18... | collective-permute-start | bytes 417800 | tf_op jit(solution)/shard_map/ppermute | solution.py:382
  13.4 0.0 copy-done.1
  13.4 9.6 %inner.1._ = f32[16,128,128]{2,1,0:T(8,128)} custom-call(f32[16,128,128]{2,1,0:T(8,128)S(1)} %copy-done.1, f32[16,128]{1,0:T(8,128)S(1)} %copy-done.2, f32[16,128]{1,0:T(8,128)S(1)} %copy-done.3, f32[16,128]{1,0:T(8,128)S(1)} %copy-done.4, f32[5,16,128]{2,1,0:T(8,128)S(1)} %collective-permute-done.of_pair, ...), custom_call_target="tpu_custom_call" | custom-call | tf_op jit(solution)/shard_map/inner/pallas_call | solution.py:386
  23.0 0.0 collective-permute-done.2.of_south
  23.1 0.0 collective-permute-done.3.of_north
  23.1 10.0 %outer.1 = f32[16,128,128]{2,1,0:T(8,128)} custom-call(f32[16,128,128]{2,1,0:T(8,128)S(1)} %copy-done.1, f32[16,128]{1,0:T(8,128)S(1)} %copy-done.2, f32[16,128]{1,0:T(8,128)S(1)} %copy-done.3, f32[16,128]{1,0:T(8,128)S(1)} %copy-done.4, f32[5,16,128]{2,1,0:T(8,128)S(1)} %collective-permute-done.of_pair, ...), custom_call_target="tpu_custom_call", output_to_operand_aliasing={{}: (15, {})} | custom-call | tf_op jit(solution)/shard_map/outer/pallas_call | solution.py:391
  (9 shorter events, 0.1 us)
Async XLA Ops:
  0.0 1.2 %copy-start = (f32[16,128,128]{2,1,0:T(8,128)S(1)}, f32[16,128,128]{2,1,0:T(8,128)}, u32[]{:S(2)}) copy-start(f32[16,128,128]{2,1,0:T(8,128)} %conc.5) | copy-start | bytes 3145732
  1.2 0.7 %copy-start.2 = (f32[16,128]{1,0:T(8,128)S(1)}, f32[16,128]{1,0:T(8,128)}, u32[]{:S(2)}) copy-start(f32[16,128]{1,0:T(8,128)} %wlon.5) | copy-start | bytes 24580
  1.9 0.7 %copy-start.3 = (f32[16,128]{1,0:T(8,128)S(1)}, f32[16,128]{1,0:T(8,128)}, u32[]{:S(2)}) copy-start(f32[16,128]{1,0:T(8,128)} %wlat.5) | copy-start | bytes 24580
  2.6 0.7 %copy-start.4 = (f32[16,128]{1,0:T(8,128)S(1)}, f32[16,128]{1,0:T(8,128)}, u32[]{:S(2)}) copy-start(f32[16,128]{1,0:T(8,128)} %mix.5) | copy-start | bytes 24580
  3.3 4.5 %copy-start.5 = (f32[64,1024]{1,0:T(8,128)S(1)}, f32[64,1024]{1,0:T(8,128)}, u32[]{:S(2)}) copy-start(f32[64,1024]{1,0:T(8,128)} %sun.1) | copy-start | bytes 786436
  3.3 4.5 %copy-start.7 = (s32[2,64,8]{1,2,0:T(8,128)S(1)}, s32[2,64,8]{1,2,0:T(8,128)}, u32[]{:S(2)}) copy-start(s32[2,64,8]{1,2,0:T(8,128)} %param.17) | copy-start | bytes 12292
  3.3 4.5 %copy-start.8 = (f32[512]{0:T(512)S(1)}, f32[512]{0:T(512)}, u32[]{:S(2)}) copy-start(f32[512]{0:T(512)} %param.14) | copy-start | bytes 6148
  3.7 4.1 %copy-start.6 = (s32[4,512]{1,0:T(4,128)S(1)}, s32[4,512]{1,0:T(4,128)}, u32[]{:S(2)}) copy-start(s32[4,512]{1,0:T(4,128)} %stoich.1) | copy-start | bytes 24580
  3.7 5.7 %collective-permute-start = (f32[5,16,128]{2,1,0:T(8,128)S(1)}, f32[5,16,128]{2,1,0:T(8,128)S(1)}, u32[]{:S(2)}, u32[]{:S(2)}) collective-permute-start(f32[5,16,128]{2,1,0:T(8,128)S(1)} %get-tuple-element.18), channel_id=1, source_target_pairs={{0,1},{1,0},{2,3},{3,2},{4,5},{5,4},{6,7},{7,6},{8,9},{9,8},{10,11... | collective-permute-start | bytes 122888 | tf_op jit(solution)/shard_map/ppermute | solution.py:352
  4.3 5.2 %collective-permute-start.1 = (f32[5,16,128]{2,1,0:T(8,128)S(1)}, f32[5,16,128]{2,1,0:T(8,128)S(1)}, u32[]{:S(2)}, u32[]{:S(2)}) collective-permute-start(f32[5,16,128]{2,1,0:T(8,128)S(1)} %get-tuple-element.19), channel_id=1, source_target_pairs={{0,7},{1,2},{2,1},{3,4},{4,3},{5,6},{6,5},{7,0},{8,15},{9,10},{10,... | collective-permute-start | bytes 122888 | tf_op jit(solution)/shard_map/ppermute | solution.py:353
  7.8 0.7 %copy-start.9 = (f32[128]{0:T(128)S(1)}, f32[128]{0:T(128)}, u32[]{:S(2)}) copy-start(f32[128]{0:T(128)} %param.15) | copy-start | bytes 1540
  8.5 5.0 %copy-start.1 = (f32[16,128,128]{2,1,0:T(8,128)S(1)}, f32[16,128,128]{2,1,0:T(8,128)}, u32[]{:S(2)}) copy-start(f32[16,128,128]{2,1,0:T(8,128)} %conc.5) | copy-start | bytes 3145732
  9.6 13.5 %collective-permute-start.2 = (f32[272,128]{1,0:T(8,128)S(1)}, f32[272,128]{1,0:T(8,128)S(1)}, u32[]{:S(2)}, u32[]{:S(2)}) collective-permute-start(f32[272,128]{1,0:T(8,128)S(1)} %get-tuple-element.24), channel_id=1, source_target_pairs={{0,8},{8,16},{16,24},{24,0},{1,9},{9,17},{17,25},{25,1},{2,10},{10... | collective-permute-start | bytes 417800 | tf_op jit(solution)/shard_map/ppermute | solution.py:381
  11.3 11.7 %collective-permute-start.3 = (f32[272,128]{1,0:T(8,128)S(1)}, f32[272,128]{1,0:T(8,128)S(1)}, u32[]{:S(2)}, u32[]{:S(2)}) collective-permute-start(f32[272,128]{1,0:T(8,128)S(1)} %get-tuple-element.25), channel_id=1, source_target_pairs={{8,0},{16,8},{24,16},{0,24},{9,1},{17,9},{25,17},{1,25},{10,2},{18... | collective-permute-start | bytes 417800 | tf_op jit(solution)/shard_map/ppermute | solution.py:382

commit v2 on v1

--- a/solution.py
+++ b/solution.py
@@ -11,6 +11,8 @@
 LANES = 128
 VMEM_LIMIT = 48 << 20
 KEPT = jax.ShapeDtypeStruct
+CHUNK = 256
+STAGGER = 2
 
 f32 = jnp.float32
 bf16 = jnp.bfloat16
@@ -33,8 +35,21 @@
     return lax.broadcasted_iota(jnp.int32, shape, axis)
 
 
-def edge_kernel(conc, wlon, wlat, mix, to_pair, to_other, own, to_north, to_south, columns):
+def edge_kernel(
+    conc_in, wlon_in, wlat_in, mix_in, to_pair, to_other, own, to_north, to_south,
+    conc, winds, columns, sem,
+):
     rows, species, cells = conc.shape
+    fetches = [
+        pltpu.make_async_copy(ref, winds.at[k], sem.at[k])
+        for k, ref in enumerate((wlon_in, wlat_in, mix_in))
+    ]
+    fetches.append(pltpu.make_async_copy(conc_in, conc, sem.at[3]))
+    for fetch in fetches:
+        fetch.start()
+    for fetch in fetches:
+        fetch.wait()
+    wlon, wlat, mix = [winds.at[k] for k in range(3)]
     lane = iota((species, cells), 1)
     picked = jnp.zeros((species, cells), f32)
     for g in range(rows):
@@ -91,7 +106,8 @@
 
 
 def table_kernel(
-    stoich, rate, night, plan, sun, gather, products, speeds, decay, sun_own, lit, turned, sem
+    stoich, rate, plan, night_in, sun, gather, products, losses, speeds, decay, sun_own, lit,
+    night, turned, sem,
 ):
     species = decay.shape[0]
     reactions = stoich.shape[1]
@@ -105,9 +121,11 @@
             pl.ds(pl.multiple_of(sector * LANES, LANES), LANES),
         ],
         sun_own,
-        sem,
+        sem.at[0],
     )
     fetch.start()
+    fetch_night = pltpu.make_async_copy(night_in, night, sem.at[1])
+    fetch_night.start()
     down = iota((species, LANES), 0)
     across = iota((LANES, species), 1).astype(f32)
     mats = []
@@ -131,9 +149,8 @@
     dark = sum(mats[PHOT // LANES + 1 :], mats[PHOT // LANES])
     for q, mat in enumerate((dark, photo)):
         high, low = split(mat + mat.T)
-        base = 2 * reactions + 2 * q * species
-        gather[pl.ds(base, species), :] = twice(high)
-        gather[pl.ds(base + species, species), :] = twice(low)
+        losses[:, 2 * q * species : 2 * (q + 1) * species] = twice(high)
+        losses[:, (4 + q) * species : (5 + q) * species] = low
     strip = []
     for s in range(SUBSTEPS):
         codes = plan[s]
@@ -142,6 +159,7 @@
     lats = plan.shape[2]
     flags = jnp.concatenate(strip + [jnp.zeros((8 - SUBSTEPS, lats), f32)], axis=0)
     flags = jnp.concatenate([flags, jnp.zeros((8, LANES - lats), f32)], axis=1)
+    fetch_night.wait()
     fade = jnp.exp(-night[...])
     spread = jnp.concatenate([flags, fade, jnp.zeros((7, LANES), f32)], axis=0).T
     decay[...] = jnp.broadcast_to(spread[:, 8:9], (species, LANES))
@@ -152,45 +170,71 @@
     fetch.wait()
 
 
-def sweep(starts, nows, photos, gather, products, speeds):
-    reactions = speeds.shape[0]
-    species = starts[0].shape[0]
-    weights = [jnp.concatenate(split(now), axis=0) for now in nows]
-    losses = [dot(gather[2 * reactions :, :], w) for w in weights]
-    made = [[] for _ in nows]
-    for k in range(reactions // LANES):
-        speed = twice(speeds[k * LANES : (k + 1) * LANES, :])
-        for p, w in enumerate(weights):
-            first = dot(gather[k * LANES : (k + 1) * LANES, :], w)
-            second = dot(gather[reactions + k * LANES : reactions + (k + 1) * LANES, :], w)
-            flow = first * speed * second
-            if k < PHOT // LANES:
-                flow = flow * photos[p]
-            made[p].extend(split(flow))
-    after = []
-    s = species
-    for start, flows, loss, photo in zip(starts, made, losses, photos):
-        produced = dot(products[...], jnp.concatenate(flows, axis=0))
-        lost = (loss[0:s] + loss[s : 2 * s]) + photo * (loss[2 * s : 3 * s] + loss[3 * s :])
-        after.append((start + produced) / (1.0 + lost))
-    return after
-
-
-def chemistry(pairs, lows, decay, sun, lit, tables):
-    def both(ref, low):
+def pair_steps(field, low, store, decay, sun, lit, gather, products, losses, speeds):
+    reactions, species = speeds.shape[0], decay.shape[0]
+
+    def both(ref):
         return jnp.concatenate([ref[low : low + 1, :], ref[low + 1 : low + 2, :]], axis=1)
 
-    photos = [both(sun, low) for low in lows]
-    fade = twice(decay[...])
+    def begin(d):
+        d["start"] = d["now"] = jnp.concatenate([field(low), field(low + 1)], axis=1)
+
+    def prepare(d):
+        photo = both(sun)
+        high, low_part = split(d["now"])
+        sun_high, sun_low = split(d["now"] * photo)
+        d["weights"] = jnp.concatenate([high, low_part], axis=0)
+        d["all"] = jnp.concatenate([high, low_part, sun_high, sun_low, high, sun_high], axis=0)
+        d["made"] = []
+
+    def lose(d):
+        d["lost"] = dot(losses[...], d["all"])
+
+    def react(k):
+        def run(d):
+            rows = slice(k * CHUNK, (k + 1) * CHUNK)
+            later = slice(reactions + k * CHUNK, reactions + (k + 1) * CHUNK)
+            first, second = dot(gather[rows, :], d["weights"]), dot(gather[later, :], d["weights"])
+            for q in range(CHUNK // LANES):
+                part = slice(q * LANES, (q + 1) * LANES)
+                base = k * CHUNK + q * LANES
+                flow = first[part] * twice(speeds[base : base + LANES, :]) * second[part]
+                if base < PHOT:
+                    flow = flow * both(sun)
+                d["made"].extend(split(flow))
+
+        return run
+
+    def produce(d):
+        d["produced"] = dot(products[...], jnp.concatenate(d["made"], axis=0))
+
+    def close(s, last):
+        def run(d):
+            d["now"] = (d["start"] + d["produced"]) / (1.0 + d["lost"])
+            if last:
+                dark = d["start"] * twice(decay[...])
+                d["now"] = d["start"] = jnp.where(both(lit.at[s]) > 0.0, d["now"], dark)
+
+        return run
+
+    steps = [begin]
     for s in range(SUBSTEPS):
-        now = list(pairs)
-        for _ in range(PICARD):
-            now = sweep(pairs, now, photos, *tables)
-        pairs = [
-            jnp.where(both(lit.at[s], low) > 0.0, n, p * fade)
-            for p, n, low in zip(pairs, now, lows)
-        ]
-    return pairs
+        for sweep in range(PICARD):
+            steps += [prepare, react(0), lose]
+            steps += [react(k) for k in range(1, reactions // CHUNK)]
+            steps += [produce, close(s, sweep == PICARD - 1)]
+    steps.append(lambda d: store(low, d["now"]))
+    return steps
+
+
+def chemistry(lows, field, store, *refs):
+    lists = [pair_steps(field, low, store, *refs) for low in lows]
+    state = [{} for _ in lows]
+    for t in range(len(lists[0]) + STAGGER * (len(lows) - 1)):
+        for p, steps in enumerate(lists):
+            at = t - STAGGER * p
+            if 0 <= at < len(steps):
+                steps[at](state[p])
 
 
 def step(center, west, east, south, north, wl, wt, mx):
@@ -229,7 +273,7 @@
     return jnp.concatenate(stack, axis=0).T
 
 
-def moved_pairs(runs, field, coef, turned, rows):
+def mover(field, coef, turned, rows):
     def column(c):
         return turned[:, c : c + 1]
 
@@ -240,41 +284,47 @@
             return column(4 * rows + 2 + side)
         return column(side * rows + g)
 
-    pairs, lows = [], []
-    for low, count in runs:
-        once, twofold = {}, {}
-        for g in range(low - 1, low + count + 1):
-            once[g] = block_step(
+    known = {}
+
+    def once(g):
+        if g not in known:
+            known[g] = block_step(
                 field(g), edge(g, 0), edge(g, 1), field(g - 1), field(g + 1), *coef(g)
             )
-            h = g - 1
-            if h >= low:
-                twofold[h] = block_step(
-                    once[h], column(2 * rows + h), column(3 * rows + h),
-                    once[h - 1], once[h + 1], *coef(h),
-                )
-        for h in range(low, low + count, 2):
-            lows.append(h)
-            pairs.append(jnp.concatenate([twofold[h], twofold[h + 1]], axis=1))
-    return pairs, lows
-
-
-def store_pairs(pairs, lows, out, stage, sem):
+        return known[g]
+
+    def moved(g):
+        sides = column(2 * rows + g), column(3 * rows + g)
+        return block_step(once(g), *sides, once(g - 1), once(g + 1), *coef(g))
+
+    return moved
+
+
+def storer(lows, out, stage, sem):
     copies = []
-    for p, low in enumerate(lows):
-        stage[2 * p] = pairs[p][:, :LANES]
-        stage[2 * p + 1] = pairs[p][:, LANES:]
+
+    def store(low, pair):
+        p = lows.index(low)
+        stage[2 * p] = pair[:, :LANES]
+        stage[2 * p + 1] = pair[:, LANES:]
         copies.append(
             pltpu.make_async_copy(stage.at[pl.ds(2 * p, 2)], out.at[pl.ds(low, 2)], sem.at[p])
         )
-        copies[p].start()
+        copies[-1].start()
+
+    return store, copies
+
+
+def finish(lows, moved, refs, out, stage, sem):
+    store, copies = storer(lows, out, stage, sem)
+    chemistry(lows, moved, store, *refs)
     for c in copies:
         c.wait()
 
 
 def inner_kernel(
     conc, wlon, wlat, mix, of_pair, of_other, own,
-    gather, products, speeds, decay, sun, lit, out, stage, sem,
+    gather, products, losses, speeds, decay, sun, lit, out, stage, sem,
 ):
     rows = conc.shape[0]
     turned = side_columns(of_pair, of_other, own, None)
@@ -282,15 +332,14 @@
     def coef(g):
         return [r[g : g + 1, :] for r in (wlon, wlat, mix)]
 
-    runs = [(rows // 4, rows // 2)]
-    pairs, lows = moved_pairs(runs, lambda g: conc[g], coef, turned, rows)
-    pairs = chemistry(pairs, lows, decay, sun, lit, (gather, products, speeds))
-    store_pairs(pairs, lows, out, stage, sem)
+    lows = list(range(rows // 4, rows - rows // 4, 2))
+    moved = mover(lambda g: conc[g], coef, turned, rows)
+    finish(lows, moved, (decay, sun, lit, gather, products, losses, speeds), out, stage, sem)
 
 
 def outer_kernel(
     conc, wlon, wlat, mix, of_pair, of_other, own, of_south, of_north,
-    gather, products, speeds, decay, sun, lit, _, out, stage, sem,
+    gather, products, losses, speeds, decay, sun, lit, _, out, stage, sem,
 ):
     rows, species, cells = conc.shape
     base = 2 * species
@@ -318,10 +367,9 @@
             return [of_north[base + k : base + k + 1, :] * above for k in range(3)]
         return [r[g : g + 1, :] for r in (wlon, wlat, mix)]
 
-    runs = [(0, rows // 4), (rows - rows // 4, rows // 4)]
-    pairs, lows = moved_pairs(runs, field, coef, turned, rows)
-    pairs = chemistry(pairs, lows, decay, sun, lit, (gather, products, speeds))
-    store_pairs(pairs, lows, out, stage, sem)
+    lows = list(range(0, rows // 4, 2)) + list(range(rows - rows // 4, rows, 2))
+    moved = mover(field, coef, turned, rows)
+    finish(lows, moved, (decay, sun, lit, gather, products, losses, speeds), out, stage, sem)
 
 
 def local(conc, wind_lon, wind_lat, mixing, sun, rate, night_loss, stoich, plan):
@@ -332,6 +380,10 @@
     params = pltpu.CompilerParams(vmem_limit_bytes=VMEM_LIMIT)
     vmem = pl.BlockSpec(memory_space=pltpu.VMEM)
     hbm = pl.BlockSpec(memory_space=pl.ANY)
+    far = pl.BlockSpec(memory_space=pltpu.HBM)
+
+    def pinned(x):
+        return pltpu.with_memory_space_constraint(x, pltpu.HBM)
 
     def shape(*dims, dtype=f32):
         return KEPT(dims, dtype)
@@ -340,10 +392,15 @@
     ends = shape(2 * species + 16, cells)
     to_pair, to_other, own, to_north, to_south = pl.pallas_call(
         edge_kernel, out_shape=(side, side, shape(2, rows, species), ends, ends),
-        in_specs=[vmem] * 4, out_specs=[vmem] * 5,
-        scratch_shapes=[pltpu.VMEM((cells, species), f32)],
+        in_specs=[far] * 4, out_specs=[vmem] * 5,
+        scratch_shapes=[
+            pltpu.VMEM(conc.shape, f32),
+            pltpu.VMEM((3, rows, cells), f32),
+            pltpu.VMEM((cells, species), f32),
+            pltpu.SemaphoreType.DMA((4,)),
+        ],
         compiler_params=params, name="edges",
-    )(conc, wind_lon, wind_lat, mixing)
+    )(*[pinned(x) for x in (conc, wind_lon, wind_lat, mixing)])
 
     pair = [(i, i ^ 1) for i in range(lons)]
     other = [(i, (i - 1) % lons if i % 2 == 0 else (i + 1) % lons) for i in range(lons)]
@@ -355,20 +412,25 @@
     tables = pl.pallas_call(
         table_kernel,
         out_shape=(
-            shape(2 * reactions + 4 * species, 2 * species, dtype=bf16),
+            shape(2 * reactions, 2 * species, dtype=bf16),
             shape(species, 2 * reactions, dtype=bf16),
+            shape(species, 6 * species, dtype=bf16),
             shape(reactions, LANES),
             shape(species, LANES),
             shape(rows, LANES),
             shape(SUBSTEPS, rows, LANES),
         ),
-        in_specs=[vmem] * 4 + [hbm], out_specs=[vmem] * 6,
-        scratch_shapes=[pltpu.VMEM((LANES, LANES), f32), pltpu.SemaphoreType.DMA],
+        in_specs=[vmem] * 3 + [far] * 2, out_specs=[vmem] * 7,
+        scratch_shapes=[
+            pltpu.VMEM((1, species), f32),
+            pltpu.VMEM((LANES, LANES), f32),
+            pltpu.SemaphoreType.DMA((2,)),
+        ],
         cost_estimate=pl.CostEstimate(flops=10**9, transcendentals=0, bytes_accessed=2 * 10**6),
         compiler_params=params, name="tables",
     )(
-        stoich, rate.reshape(1, reactions), night_loss.reshape(1, species),
-        jnp.swapaxes(plan, 1, 2), sun,
+        stoich, rate.reshape(1, reactions), jnp.swapaxes(plan, 1, 2),
+        pinned(night_loss.reshape(1, species)), pinned(sun),
     )
 
     to_north, to_south = pl.pallas_call(
@@ -377,7 +439,7 @@
         scratch_shapes=[pltpu.VMEM((2, 8, species), f32), pltpu.SemaphoreType.DMA((2,))],
         input_output_aliases={2: 0, 3: 1},
         compiler_params=params, name="corners",
-    )(of_pair, of_other, to_north, to_south, tables[4])
+    )(of_pair, of_other, to_north, to_south, tables[5])
     of_south = lax.ppermute(to_north, "lat", north)
     of_north = lax.ppermute(to_south, "lat", south)
 
@@ -385,13 +447,13 @@
     scratch = [pltpu.VMEM((rows // 2, species, cells), f32), pltpu.SemaphoreType.DMA((rows // 4,))]
     inner = pl.pallas_call(
         inner_kernel, out_shape=jax.ShapeDtypeStruct(conc.shape, f32),
-        in_specs=[vmem] * 13, out_specs=hbm, scratch_shapes=scratch,
+        in_specs=[vmem] * 14, out_specs=hbm, scratch_shapes=scratch,
         compiler_params=params, name="inner",
     )(*shared, *tables)
     return pl.pallas_call(
         outer_kernel, out_shape=jax.ShapeDtypeStruct(conc.shape, f32),
-        in_specs=[vmem] * 15 + [hbm], out_specs=hbm, scratch_shapes=scratch,
-        input_output_aliases={15: 0},
+        in_specs=[vmem] * 16 + [hbm], out_specs=hbm, scratch_shapes=scratch,
+        input_output_aliases={16: 0},
         compiler_params=params, name="outer",
     )(*shared, of_south, of_north, *tables, inner)
 

time: 33.6 us -> 31.2 us (0.929)
  local copies, waits for them, and re-layouts: 3.97 us -> 0.03 us
  Pallas kernels: 21 us -> 22.6 us
    unnamed x20 -> x14, local copies, waits for them, and re-layouts: 3.97 us -> 0.03 us
    pallas_call x1, Pallas kernels: 0.4 us -> 1.75 us  [local(): pl.pallas_call(edge_kernel, out_shape=(side, side, shape(2, rows, species...]
    pallas_call x1, Pallas kernels: 0.96 us -> 1.53 us  [local(): pl.pallas_call(table_kernel, out_shape=(shape(2 * reactions, 2 * species,...]
  transfers between devices with their start and end apart: 4 -> 4, of which waited for: 0 -> 1; matrix products, arithmetic and copies ran while one was open for 0% -> 0% of each run, Pallas kernels for 32% -> 35%
where the time goes in v2:
time: 31.2 us; the launch traced here: 31 us
  Pallas kernels  22.6 us (72%)
  starting transfers between devices  7.95 us (25%)
    pallas_call x1, Pallas kernels, local(): pl.pallas_call(outer_kernel, out_shape=jax.ShapeDtypeStruct(conc.shape, f...  9.85 us
    pallas_call x1, Pallas kernels, local(): pl.pallas_call(inner_kernel, out_shape=jax.ShapeDtypeStruct(conc.shape, f...  9.46 us
    ppermute x1, starting transfers between devices, local(): of_other = lax.ppermute(to_other, 'lon', other)  3.56 us
    ppermute x1, starting transfers between devices, local(): of_north = lax.ppermute(to_south, 'lat', south)  2.09 us
    ppermute x1, starting transfers between devices, local(): of_south = lax.ppermute(to_north, 'lat', north)  1.79 us
    pallas_call x1, Pallas kernels, local(): pl.pallas_call(edge_kernel, out_shape=(side, side, shape(2, rows, species...  1.75 us
    pallas_call x1, Pallas kernels, local(): pl.pallas_call(table_kernel, out_shape=(shape(2 * reactions, 2 * species,...  1.53 us
  transfers between devices with their start and end apart: 4, of which 1 were waited for; matrix products, arithmetic and copies ran while one was open for 0% of the time, Pallas kernels for 35%

profile of v2, /device:TPU:0, one launch (start us, length us, event | category | flops | bytes accessed | tf_op | source)
XLA Modules:
  0.0 31.0 jit_solution(14207574423392831747)
XLA Ops:
  0.0 0.0 copy-start.5
  0.0 1.8 %edges.1 = (f32[5,16,128]{2,1,0:T(8,128)S(1)}, f32[5,16,128]{2,1,0:T(8,128)S(1)}, f32[2,16,128]{2,1,0:T(8,128)S(1)}, f32[272,128]{1,0:T(8,128)S(1)}, f32[272,128]{1,0:T(8,128)S(1)}) custom-call(f32[16,128,128]{2,1,0:T(8,128)} %conc.3, f32[16,128]{1,0:T(8,128)} %wlon.3, f32[16,128]{1,0:T(8,128)} %wlat.3, f32[16,128]{1,0:T(8,128)} %mix.3), custom_call_target="tpu_custom_call" | custom-call | tf_op jit(solution)/shard_map/edges/pallas_call | solution.py:393
  1.8 0.0 copy-start.4
  1.8 0.5 %collective-permute-start = (f32[5,16,128]{2,1,0:T(8,128)S(1)}, f32[5,16,128]{2,1,0:T(8,128)S(1)}, u32[]{:S(2)}, u32[]{:S(2)}) collective-permute-start(f32[5,16,128]{2,1,0:T(8,128)S(1)} %get-tuple-element.19), channel_id=1, source_target_pairs={{0,1},{1,0},{2,3},{3,2},{4,5},{5,4},{6,7},{7,6},{8,9},{9,8},{10,11... | collective-permute-start | bytes 122888 | tf_op jit(solution)/shard_map/ppermute | solution.py:409
  2.3 3.6 %collective-permute-start.1 = (f32[5,16,128]{2,1,0:T(8,128)S(1)}, f32[5,16,128]{2,1,0:T(8,128)S(1)}, u32[]{:S(2)}, u32[]{:S(2)}) collective-permute-start(f32[5,16,128]{2,1,0:T(8,128)S(1)} %get-tuple-element.20), channel_id=1, source_target_pairs={{0,7},{1,2},{2,1},{3,4},{4,3},{5,6},{6,5},{7,0},{8,15},{9,10},{10,... | collective-permute-start | bytes 122888 | tf_op jit(solution)/shard_map/ppermute | solution.py:410
  5.9 0.0 copy-done.5
  5.9 0.0 copy-done.6
  5.9 0.0 copy-done.4
  5.9 0.0 copy-start
  5.9 1.5 %tables.1 = (bf16[1024,256]{1,0:T(8,128)(2,1)S(1)}, bf16[128,1024]{1,0:T(8,128)(2,1)S(1)}, bf16[128,768]{1,0:T(8,128)(2,1)S(1)}, f32[512,128]{1,0:T(8,128)S(1)},...) custom-call(s32[4,512]{1,0:T(4,128)S(1)} %copy-done.4, f32[1,512]{1,0:T(1,128)S(1)} %bitcast.4, ...), custom_call_target="tpu_custom_call" | custom-call | flops 1000000000 | bytes 2000000 | tf_op jit(solution)/shard_map/tables/pallas_call | solution.py:412
  7.4 0.0 collective-permute-done.of_pair
  7.4 0.1 collective-permute-done.1.of_other
  7.6 0.0 copy-start.2
  7.6 0.0 copy-start.1
  7.6 1.8 %collective-permute-start.2 = (f32[272,128]{1,0:T(8,128)S(1)}, f32[272,128]{1,0:T(8,128)S(1)}, u32[]{:S(2)}, u32[]{:S(2)}) collective-permute-start(f32[272,128]{1,0:T(8,128)S(1)} %get-tuple-element.25), channel_id=1, source_target_pairs={{0,8},{8,16},{16,24},{24,0},{1,9},{9,17},{17,25},{25,1},{2,10},{10... | collective-permute-start | bytes 417800 | tf_op jit(solution)/shard_map/ppermute | solution.py:443
  9.4 2.1 %collective-permute-start.3 = (f32[272,128]{1,0:T(8,128)S(1)}, f32[272,128]{1,0:T(8,128)S(1)}, u32[]{:S(2)}, u32[]{:S(2)}) collective-permute-start(f32[272,128]{1,0:T(8,128)S(1)} %get-tuple-element.26), channel_id=1, source_target_pairs={{8,0},{16,8},{24,16},{0,24},{9,1},{17,9},{25,17},{1,25},{10,2},{18... | collective-permute-start | bytes 417800 | tf_op jit(solution)/shard_map/ppermute | solution.py:444
  11.5 0.0 copy-done
  11.5 0.0 copy-done.3
  11.5 0.0 copy-done.2
  11.5 0.0 copy-done.1
  11.5 9.5 %inner.1._ = f32[16,128,128]{2,1,0:T(8,128)} custom-call(f32[16,128,128]{2,1,0:T(8,128)S(1)} %copy-done, f32[16,128]{1,0:T(8,128)S(1)} %copy-done.1, f32[16,128]{1,0:T(8,128)S(1)} %copy-done.2, f32[16,128]{1,0:T(8,128)S(1)} %copy-done.3, f32[5,16,128]{2,1,0:T(8,128)S(1)} %collective-permute-done.of_pair, f32[5,16,128]{2,1,0:T(8,128)S(1)} %collective-permute-done.1.of_other, ...), custom_call_target="tpu_custom_call" | custom-call | tf_op jit(solution)/shard_map/inner/pallas_call | solution.py:448
  21.0 0.0 collective-permute-done.2.of_south
  21.0 0.0 collective-permute-done.3.of_north
  21.0 9.9 %outer.1 = f32[16,128,128]{2,1,0:T(8,128)} custom-call(f32[16,128,128]{2,1,0:T(8,128)S(1)} %copy-done, f32[16,128]{1,0:T(8,128)S(1)} %copy-done.1, f32[16,128]{1,0:T(8,128)S(1)} %copy-done.2, f32[16,128]{1,0:T(8,128)S(1)} %copy-done.3, f32[5,16,128]{2,1,0:T(8,128)S(1)} %collective-permute-done.of_pair, ...), custom_call_target="tpu_custom_call", output_to_operand_aliasing={{}: (16, {})} | custom-call | tf_op jit(solution)/shard_map/outer/pallas_call | solution.py:453
  (3 shorter events, 0.0 us)
Async XLA Ops:
  0.0 5.9 %copy-start.5 = (s32[2,64,8]{1,2,0:T(8,128)S(1)}, s32[2,64,8]{1,2,0:T(8,128)}, u32[]{:S(2)}) copy-start(s32[2,64,8]{1,2,0:T(8,128)} %param.17) | copy-start | bytes 12292
  0.0 5.9 %copy-start.6 = (f32[512]{0:T(512)S(1)}, f32[512]{0:T(512)}, u32[]{:S(2)}) copy-start(f32[512]{0:T(512)} %param.14) | copy-start | bytes 6148
  1.8 4.1 %copy-start.4 = (s32[4,512]{1,0:T(4,128)S(1)}, s32[4,512]{1,0:T(4,128)}, u32[]{:S(2)}) copy-start(s32[4,512]{1,0:T(4,128)} %stoich.1) | copy-start | bytes 24580
  1.8 5.6 %collective-permute-start = (f32[5,16,128]{2,1,0:T(8,128)S(1)}, f32[5,16,128]{2,1,0:T(8,128)S(1)}, u32[]{:S(2)}, u32[]{:S(2)}) collective-permute-start(f32[5,16,128]{2,1,0:T(8,128)S(1)} %get-tuple-element.19), channel_id=1, source_target_pairs={{0,1},{1,0},{2,3},{3,2},{4,5},{5,4},{6,7},{7,6},{8,9},{9,8},{10,11... | collective-permute-start | bytes 122888 | tf_op jit(solution)/shard_map/ppermute | solution.py:409
  2.3 5.2 %collective-permute-start.1 = (f32[5,16,128]{2,1,0:T(8,128)S(1)}, f32[5,16,128]{2,1,0:T(8,128)S(1)}, u32[]{:S(2)}, u32[]{:S(2)}) collective-permute-start(f32[5,16,128]{2,1,0:T(8,128)S(1)} %get-tuple-element.20), channel_id=1, source_target_pairs={{0,7},{1,2},{2,1},{3,4},{4,3},{5,6},{6,5},{7,0},{8,15},{9,10},{10,... | collective-permute-start | bytes 122888 | tf_op jit(solution)/shard_map/ppermute | solution.py:410
  5.9 5.6 %copy-start = (f32[16,128,128]{2,1,0:T(8,128)S(1)}, f32[16,128,128]{2,1,0:T(8,128)}, u32[]{:S(2)}) copy-start(f32[16,128,128]{2,1,0:T(8,128)} %conc.3) | copy-start | bytes 3145732
  7.5 4.0 %copy-start.3 = (f32[16,128]{1,0:T(8,128)S(1)}, f32[16,128]{1,0:T(8,128)}, u32[]{:S(2)}) copy-start(f32[16,128]{1,0:T(8,128)} %mix.3) | copy-start | bytes 24580
  7.6 3.9 %copy-start.2 = (f32[16,128]{1,0:T(8,128)S(1)}, f32[16,128]{1,0:T(8,128)}, u32[]{:S(2)}) copy-start(f32[16,128]{1,0:T(8,128)} %wlat.3) | copy-start | bytes 24580
  7.6 3.9 %copy-start.1 = (f32[16,128]{1,0:T(8,128)S(1)}, f32[16,128]{1,0:T(8,128)}, u32[]{:S(2)}) copy-start(f32[16,128]{1,0:T(8,128)} %wlon.3) | copy-start | bytes 24580
  7.6 13.4 %collective-permute-start.2 = (f32[272,128]{1,0:T(8,128)S(1)}, f32[272,128]{1,0:T(8,128)S(1)}, u32[]{:S(2)}, u32[]{:S(2)}) collective-permute-start(f32[272,128]{1,0:T(8,128)S(1)} %get-tuple-element.25), channel_id=1, source_target_pairs={{0,8},{8,16},{16,24},{24,0},{1,9},{9,17},{17,25},{25,1},{2,10},{10... | collective-permute-start | bytes 417800 | tf_op jit(solution)/shard_map/ppermute | solution.py:443
  9.4 11.6 %collective-permute-start.3 = (f32[272,128]{1,0:T(8,128)S(1)}, f32[272,128]{1,0:T(8,128)S(1)}, u32[]{:S(2)}, u32[]{:S(2)}) collective-permute-start(f32[272,128]{1,0:T(8,128)S(1)} %get-tuple-element.26), channel_id=1, source_target_pairs={{8,0},{16,8},{24,16},{0,24},{9,1},{17,9},{25,17},{1,25},{10,2},{18... | collective-permute-start | bytes 417800 | tf_op jit(solution)/shard_map/ppermute | solution.py:444

commit v3 on v2

--- a/solution.py
+++ b/solution.py
@@ -36,8 +36,8 @@
 
 
 def edge_kernel(
-    conc_in, wlon_in, wlat_in, mix_in, to_pair, to_other, own, to_north, to_south,
-    conc, winds, columns, sem,
+    conc_in, wlon_in, wlat_in, mix_in, to_pair, to_other, own, to_north, to_south, conc, coefs,
+    winds, columns, sem,
 ):
     rows, species, cells = conc.shape
     fetches = [
@@ -47,9 +47,35 @@
     fetches.append(pltpu.make_async_copy(conc_in, conc, sem.at[3]))
     for fetch in fetches:
         fetch.start()
-    for fetch in fetches:
+    for fetch in fetches[:3]:
         fetch.wait()
-    wlon, wlat, mix = [winds.at[k] for k in range(3)]
+    wlon, wlat, mix = [winds[k] for k in range(3)]
+    place = iota((rows, cells), 1)
+    stay = 1.0 - wlon - wlat - 4.0 * mix
+    west, south = wlon + mix, wlat + mix
+    coefs[0] = stay
+    coefs[1] = jnp.where(place == 0, 0.0, west)
+    coefs[2] = south
+    coefs[3] = jnp.where(place == cells - 1, 0.0, mix)
+    coefs[4] = mix
+    coefs[5] = jnp.where(place == 0, west, jnp.where(place == cells - 1, mix, 0.0))
+    even = lax.rem(lax.axis_index("lon"), 2) == 0
+
+    def put(k, right, left):
+        to_pair[k] = jnp.where(even, right, left)
+        to_other[k] = jnp.where(even, left, right)
+
+    for k, ref in enumerate((stay, west, south, mix)):
+        put(
+            2 + k,
+            jnp.broadcast_to(ref[:, cells - 1 : cells], (rows, species)),
+            jnp.broadcast_to(ref[:, 0:1], (rows, species)),
+        )
+    base = 2 * species
+    pad = jnp.zeros((2, cells), f32)
+    for ref, g in ((to_north, rows - 1), (to_south, 0)):
+        ref[base : base + 8, :] = jnp.concatenate([coefs[k, g : g + 1] for k in range(6)] + [pad])
+    fetches[3].wait()
     lane = iota((species, cells), 1)
     picked = jnp.zeros((species, cells), f32)
     for g in range(rows):
@@ -57,29 +83,13 @@
         picked = jnp.where((lane >= 4 * g) & (lane < 4 * g + 4), turned, picked)
     columns[...] = picked.T
     last2, last1, first1, first2 = [columns[pl.ds(q, rows, stride=4), :] for q in range(4)]
-    even = lax.rem(lax.axis_index("lon"), 2) == 0
-
-    def put(k, right, left):
-        to_pair[k] = jnp.where(even, right, left)
-        to_other[k] = jnp.where(even, left, right)
-
     put(0, last1, first1)
     put(1, last2, first2)
-    for k, ref in enumerate((wlon, wlat, mix)):
-        put(
-            2 + k,
-            jnp.broadcast_to(ref[:, cells - 1 : cells], (rows, species)),
-            jnp.broadcast_to(ref[:, 0:1], (rows, species)),
-        )
     own[0] = first1
     own[1] = last1
     for q in range(2):
         to_north[q * species : (q + 1) * species, :] = conc[rows - 2 + q]
         to_south[q * species : (q + 1) * species, :] = conc[q]
-    base = 2 * species
-    pad = jnp.zeros((5, cells), f32)
-    to_north[base : base + 8, :] = jnp.concatenate([r[rows - 1 : rows, :] for r in (wlon, wlat, mix)] + [pad])
-    to_south[base : base + 8, :] = jnp.concatenate([r[0:1, :] for r in (wlon, wlat, mix)] + [pad])
 
 
 def sides(of_pair, of_other):
@@ -106,26 +116,34 @@
 
 
 def table_kernel(
-    stoich, rate, plan, night_in, sun, gather, products, losses, speeds, decay, sun_own, lit,
-    night, turned, sem,
+    conc, coefs, stoich_in, rate_in, plan_in, night_in, sun, once, gather, products, losses, speeds, decay, sun_own, lit,
+    stoich, rate, plan, night, turned, sem,
 ):
     species = decay.shape[0]
-    reactions = stoich.shape[1]
+    reactions = stoich_in.shape[1]
     rows = sun_own.shape[0]
     chunks = reactions // LANES
     band = lax.axis_index("lat")
     sector = lax.axis_index("lon")
-    fetch = pltpu.make_async_copy(
-        sun.at[
-            pl.ds(pl.multiple_of(band * rows, 8), rows),
-            pl.ds(pl.multiple_of(sector * LANES, LANES), LANES),
-        ],
-        sun_own,
-        sem.at[0],
+    here = sun.at[
+        pl.ds(pl.multiple_of(band * rows, 8), rows),
+        pl.ds(pl.multiple_of(sector * LANES, LANES), LANES),
+    ]
+    moves = (
+        (here, sun_own), (stoich_in, stoich), (rate_in, rate), (plan_in, plan), (night_in, night)
     )
-    fetch.start()
-    fetch_night = pltpu.make_async_copy(night_in, night, sem.at[1])
-    fetch_night.start()
+    fetches = [pltpu.make_async_copy(a, b, sem.at[k]) for k, (a, b) in enumerate(moves)]
+    for fetch in fetches:
+        fetch.start()
+    for g in range(rows):
+        row = inner_step(conc[g], coefs, g)
+        if g > 0:
+            row = row + coefs[2, g : g + 1, :] * conc[g - 1]
+        if g < rows - 1:
+            row = row + coefs[4, g : g + 1, :] * conc[g + 1]
+        once[g] = row
+    for fetch in fetches:
+        fetch.wait()
     down = iota((species, LANES), 0)
     across = iota((LANES, species), 1).astype(f32)
     mats = []
@@ -159,7 +177,6 @@
     lats = plan.shape[2]
     flags = jnp.concatenate(strip + [jnp.zeros((8 - SUBSTEPS, lats), f32)], axis=0)
     flags = jnp.concatenate([flags, jnp.zeros((8, LANES - lats), f32)], axis=1)
-    fetch_night.wait()
     fade = jnp.exp(-night[...])
     spread = jnp.concatenate([flags, fade, jnp.zeros((7, LANES), f32)], axis=0).T
     decay[...] = jnp.broadcast_to(spread[:, 8:9], (species, LANES))
@@ -167,7 +184,6 @@
         turned[...] = jnp.broadcast_to(spread[:, s : s + 1], turned.shape)
         mine = turned[pl.ds(pl.multiple_of(band * rows, 8), rows), :]
         lit[s] = (mine >= -1.0).astype(f32)
-    fetch.wait()
 
 
 def pair_steps(field, low, store, decay, sun, lit, gather, products, losses, speeds):
@@ -237,24 +253,13 @@
                 steps[at](state[p])
 
 
-def step(center, west, east, south, north, wl, wt, mx):
-    return (
-        center
-        - wl * (center - west)
-        - wt * (center - south)
-        + mx * (east + west + north + south - 4.0 * center)
-    )
-
-
-def block_step(center, west_edge, east_edge, south, north, wl, wt, mx):
+def inner_step(center, coefs, g):
     cells = center.shape[1]
-    lane = lax.broadcasted_iota(jnp.int32, center.shape, 1)
-    west = jnp.where(lane == 0, west_edge, pltpu.roll(center, 1, 1))
-    east = jnp.where(lane == cells - 1, east_edge, pltpu.roll(center, cells - 1, 1))
-    return step(center, west, east, south, north, wl, wt, mx)
-
-
-def side_columns(of_pair, of_other, own, corners):
+    stay, west, _, east = [coefs[k, g : g + 1, :] for k in range(4)]
+    return stay * center + west * pltpu.roll(center, 1, 1) + east * pltpu.roll(center, cells - 1, 1)
+
+
+def side_columns(of_pair, of_other, own, corners, columns):
     rows = of_pair.shape[1]
     left, right = sides(of_pair, of_other)
     near_l, near_r = left(0), right(0)
@@ -264,38 +269,35 @@
     def moved(near, west, east, south, north, side):
         south = jnp.concatenate([south, near[:-1]], axis=0)
         north = jnp.concatenate([near[1:], north], axis=0)
-        return step(near, west, east, south, north, side(2), side(3), side(4))
-
-    moved_l = moved(near_l, left(1), own[0], sl, nl, left)
-    moved_r = moved(near_r, own[1], right(1), sr, nr, right)
-    pad = jnp.zeros((LANES - 4 * rows - 4, near_l.shape[1]), f32)
-    stack = [near_l, near_r, moved_l, moved_r, sl, sr, nl, nr, pad]
-    return jnp.concatenate(stack, axis=0).T
-
-
-def mover(field, coef, turned, rows):
-    def column(c):
-        return turned[:, c : c + 1]
-
-    def edge(g, side):
-        if g < 0:
-            return column(4 * rows + side)
-        if g >= rows:
-            return column(4 * rows + 2 + side)
-        return column(side * rows + g)
+        return side(2) * near + side(3) * west + side(4) * south + side(5) * (east + north)
+
+    columns[...] = jnp.zeros_like(columns)
+    columns[pl.ds(0, rows, stride=2), :] = near_r
+    columns[pl.ds(1, rows, stride=2), :] = near_l
+    columns[pl.ds(2 * rows, rows, stride=2), :] = moved(near_r, own[1], right(1), sr, nr, right)
+    columns[pl.ds(2 * rows + 1, rows, stride=2), :] = moved(near_l, left(1), own[0], sl, nl, left)
+    for k, row in enumerate((sr, sl, nr, nl)):
+        columns[4 * rows + k : 4 * rows + k + 1, :] = row
+    return columns[...].T
+
+
+def mover(first, coefs, turned, rows):
+    def beside(i):
+        return pltpu.roll(turned, LANES - 2 * i - 1, 1)
 
     known = {}
 
     def once(g):
         if g not in known:
-            known[g] = block_step(
-                field(g), edge(g, 0), edge(g, 1), field(g - 1), field(g + 1), *coef(g)
-            )
+            i = 2 * rows if g < 0 else 2 * rows + 1 if g >= rows else g
+            row, side = first(g)
+            known[g] = row + side * beside(i)
         return known[g]
 
     def moved(g):
-        sides = column(2 * rows + g), column(3 * rows + g)
-        return block_step(once(g), *sides, once(g - 1), once(g + 1), *coef(g))
+        row = inner_step(once(g), coefs, g) + coefs[2, g : g + 1, :] * once(g - 1)
+        row = row + coefs[4, g : g + 1, :] * once(g + 1)
+        return row + coefs[5, g : g + 1, :] * beside(rows + g)
 
     return moved
 
@@ -323,23 +325,19 @@
 
 
 def inner_kernel(
-    conc, wlon, wlat, mix, of_pair, of_other, own,
-    gather, products, losses, speeds, decay, sun, lit, out, stage, sem,
+    once, coefs, of_pair, of_other, own,
+    gather, products, losses, speeds, decay, sun, lit, out, stage, columns, sem,
 ):
-    rows = conc.shape[0]
-    turned = side_columns(of_pair, of_other, own, None)
-
-    def coef(g):
-        return [r[g : g + 1, :] for r in (wlon, wlat, mix)]
-
+    rows = once.shape[0]
+    turned = side_columns(of_pair, of_other, own, None, columns)
     lows = list(range(rows // 4, rows - rows // 4, 2))
-    moved = mover(lambda g: conc[g], coef, turned, rows)
+    moved = mover(lambda g: (once[g], coefs[5, g : g + 1, :]), coefs, turned, rows)
     finish(lows, moved, (decay, sun, lit, gather, products, losses, speeds), out, stage, sem)
 
 
 def outer_kernel(
-    conc, wlon, wlat, mix, of_pair, of_other, own, of_south, of_north,
-    gather, products, losses, speeds, decay, sun, lit, _, out, stage, sem,
+    once, coefs, of_pair, of_other, own, conc, of_south, of_north,
+    gather, products, losses, speeds, decay, sun, lit, _, out, stage, columns, sem,
 ):
     rows, species, cells = conc.shape
     base = 2 * species
@@ -351,24 +349,36 @@
         for r, inside in ((of_south, below), (of_north, above))
         for k in range(2)
     ]
-    turned = side_columns(of_pair, of_other, own, corners)
-
-    def field(g):
+    turned = side_columns(of_pair, of_other, own, corners, columns)
+
+    def halo(ref, q, inside):
+        return ref[q * species : (q + 1) * species, :] * inside
+
+    def across(ref, k, inside):
+        return ref[base + k : base + k + 1, :] * inside
+
+    def outside(ref, near, far, beyond, home, back, inside):
+        center = halo(ref, near, inside)
+        stay, west, east = [across(ref, k, inside) for k in (0, 1, 3)]
+        row = stay * center + west * pltpu.roll(center, 1, 1)
+        row = row + east * pltpu.roll(center, cells - 1, 1)
+        row = row + across(ref, beyond, inside) * halo(ref, far, inside)
+        return row + across(ref, back, inside) * home, across(ref, 5, inside)
+
+    def first(g):
         if g < 0:
-            return of_south[(2 + g) * species : (3 + g) * species, :] * below
+            return outside(of_south, 1, 0, 2, conc[0], 4, below)
         if g >= rows:
-            return of_north[(g - rows) * species : (g - rows + 1) * species, :] * above
-        return conc[g]
-
-    def coef(g):
-        if g < 0:
-            return [of_south[base + k : base + k + 1, :] * below for k in range(3)]
-        if g >= rows:
-            return [of_north[base + k : base + k + 1, :] * above for k in range(3)]
-        return [r[g : g + 1, :] for r in (wlon, wlat, mix)]
+            return outside(of_north, 0, 1, 4, conc[rows - 1], 2, above)
+        row, side = once[g], coefs[5, g : g + 1, :]
+        if g == 0:
+            row = row + coefs[2, g : g + 1, :] * halo(of_south, 1, below)
+        if g == rows - 1:
+            row = row + coefs[4, g : g + 1, :] * halo(of_north, 0, above)
+        return row, side
 
     lows = list(range(0, rows // 4, 2)) + list(range(rows - rows // 4, rows, 2))
-    moved = mover(field, coef, turned, rows)
+    moved = mover(first, coefs, turned, rows)
     finish(lows, moved, (decay, sun, lit, gather, products, losses, speeds), out, stage, sem)
 
 
@@ -388,13 +398,16 @@
     def shape(*dims, dtype=f32):
         return KEPT(dims, dtype)
 
-    side = shape(5, rows, species)
+    side = shape(6, rows, species)
     ends = shape(2 * species + 16, cells)
-    to_pair, to_other, own, to_north, to_south = pl.pallas_call(
-        edge_kernel, out_shape=(side, side, shape(2, rows, species), ends, ends),
-        in_specs=[far] * 4, out_specs=[vmem] * 5,
+    to_pair, to_other, own, to_north, to_south, held, coefs = pl.pallas_call(
+        edge_kernel,
+        out_shape=(
+            side, side, shape(2, rows, species), ends, ends,
+            shape(rows, species, cells), shape(6, rows, cells),
+        ),
+        in_specs=[far] * 4, out_specs=[vmem] * 7,
         scratch_shapes=[
-            pltpu.VMEM(conc.shape, f32),
             pltpu.VMEM((3, rows, cells), f32),
             pltpu.VMEM((cells, species), f32),
             pltpu.SemaphoreType.DMA((4,)),
@@ -409,9 +422,10 @@
     of_pair = lax.ppermute(to_pair, "lon", pair)
     of_other = lax.ppermute(to_other, "lon", other)
 
-    tables = pl.pallas_call(
+    once, *tables = pl.pallas_call(
         table_kernel,
         out_shape=(
+            shape(rows, species, cells),
             shape(2 * reactions, 2 * species, dtype=bf16),
             shape(species, 2 * reactions, dtype=bf16),
             shape(species, 6 * species, dtype=bf16),
@@ -420,17 +434,20 @@
             shape(rows, LANES),
             shape(SUBSTEPS, rows, LANES),
         ),
-        in_specs=[vmem] * 3 + [far] * 2, out_specs=[vmem] * 7,
+        in_specs=[vmem] * 2 + [far] * 5, out_specs=[vmem] * 8,
         scratch_shapes=[
+            pltpu.VMEM(stoich.shape, jnp.int32),
+            pltpu.VMEM((1, reactions), f32),
+            pltpu.VMEM((plan.shape[0], plan.shape[2], plan.shape[1]), jnp.int32),
             pltpu.VMEM((1, species), f32),
             pltpu.VMEM((LANES, LANES), f32),
-            pltpu.SemaphoreType.DMA((2,)),
+            pltpu.SemaphoreType.DMA((5,)),
         ],
         cost_estimate=pl.CostEstimate(flops=10**9, transcendentals=0, bytes_accessed=2 * 10**6),
         compiler_params=params, name="tables",
     )(
-        stoich, rate.reshape(1, reactions), jnp.swapaxes(plan, 1, 2),
-        pinned(night_loss.reshape(1, species)), pinned(sun),
+        held, coefs, pinned(stoich), pinned(rate.reshape(1, reactions)),
+        pinned(jnp.swapaxes(plan, 1, 2)), pinned(night_loss.reshape(1, species)), pinned(sun),
     )
 
     to_north, to_south = pl.pallas_call(
@@ -443,19 +460,23 @@
     of_south = lax.ppermute(to_north, "lat", north)
     of_north = lax.ppermute(to_south, "lat", south)
 
-    shared = (conc, wind_lon, wind_lat, mixing, of_pair, of_other, own)
-    scratch = [pltpu.VMEM((rows // 2, species, cells), f32), pltpu.SemaphoreType.DMA((rows // 4,))]
+    shared = (once, coefs, of_pair, of_other, own)
+    scratch = [
+        pltpu.VMEM((rows // 2, species, cells), f32),
+        pltpu.VMEM((LANES, species), f32),
+        pltpu.SemaphoreType.DMA((rows // 4,)),
+    ]
     inner = pl.pallas_call(
         inner_kernel, out_shape=jax.ShapeDtypeStruct(conc.shape, f32),
-        in_specs=[vmem] * 14, out_specs=hbm, scratch_shapes=scratch,
+        in_specs=[vmem] * 12, out_specs=hbm, scratch_shapes=scratch,
         compiler_params=params, name="inner",
     )(*shared, *tables)
     return pl.pallas_call(
         outer_kernel, out_shape=jax.ShapeDtypeStruct(conc.shape, f32),
-        in_specs=[vmem] * 16 + [hbm], out_specs=hbm, scratch_shapes=scratch,
-        input_output_aliases={16: 0},
+        in_specs=[vmem] * 15 + [hbm], out_specs=hbm, scratch_shapes=scratch,
+        input_output_aliases={15: 0},
         compiler_params=params, name="outer",
-    )(*shared, of_south, of_north, *tables, inner)
+    )(*shared, held, of_south, of_north, *tables, inner)
 
 
 def solution(mesh):

time: 31.2 us -> 28.8 us (0.923)
  Pallas kernels: 22.6 us -> 20.4 us
    pallas_call x1, Pallas kernels: 9.85 us -> 8.33 us  [local(): pl.pallas_call(outer_kernel, out_shape=jax.ShapeDtypeStruct(conc.shape, f...]
    pallas_call x1, Pallas kernels: 9.46 us -> 8.03 us  [local(): pl.pallas_call(inner_kernel, out_shape=jax.ShapeDtypeStruct(conc.shape, f...]
    pallas_call x1, Pallas kernels: 1.53 us -> 2.31 us  [local(): pl.pallas_call(table_kernel, out_shape=(shape(rows, species, cells), shap...]
  transfers between devices with their start and end apart: 4 -> 4, of which waited for: 1 -> 0; matrix products, arithmetic and copies ran while one was open for 0% -> 0% of each run, Pallas kernels for 35% -> 36%
where the time goes in v3:
time: 28.8 us; the launch traced here: 28.6 us
  Pallas kernels  20.4 us (71%)
  starting transfers between devices  7.95 us (28%)
    pallas_call x1, Pallas kernels, local(): pl.pallas_call(outer_kernel, out_shape=jax.ShapeDtypeStruct(conc.shape, f...  8.33 us
    pallas_call x1, Pallas kernels, local(): pl.pallas_call(inner_kernel, out_shape=jax.ShapeDtypeStruct(conc.shape, f...  8.03 us
    ppermute x1, starting transfers between devices, local(): of_other = lax.ppermute(to_other, 'lon', other)  3.56 us
    pallas_call x1, Pallas kernels, local(): pl.pallas_call(table_kernel, out_shape=(shape(rows, species, cells), shap...  2.31 us
    ppermute x1, starting transfers between devices, local(): of_north = lax.ppermute(to_south, 'lat', south)  2.25 us
    pallas_call x1, Pallas kernels, local(): pl.pallas_call(edge_kernel, out_shape=(side, side, shape(2, rows, species...  1.73 us
    ppermute x1, starting transfers between devices, local(): of_south = lax.ppermute(to_north, 'lat', north)  1.63 us
  transfers between devices with their start and end apart: 4, of which 0 were waited for; matrix products, arithmetic and copies ran while one was open for 0% of the time, Pallas kernels for 36%

profile of v3, /device:TPU:0, one launch (start us, length us, event | category | flops | bytes accessed | tf_op | source)
XLA Modules:
  0.0 28.6 jit_solution(13073475867774368298)
XLA Ops:
  0.0 1.7 %edges.1 = (f32[6,16,128]{2,1,0:T(8,128)S(1)}, f32[6,16,128]{2,1,0:T(8,128)S(1)}, f32[2,16,128]{2,1,0:T(8,128)S(1)}, f32[272,128]{1,0:T(8,128)S(1)}, f32[272,128...) custom-call(f32[16,128,128]{2,1,0:T(8,128)} %conc_in.1, f32[16,128]{1,0:T(8,128)} %wlon_in.1, ...), custom_call_target="tpu_custom_call" | custom-call | tf_op jit(solution)/shard_map/edges/pallas_call | solution.py:403
  1.7 0.5 %collective-permute-start = (f32[6,16,128]{2,1,0:T(8,128)S(1)}, f32[6,16,128]{2,1,0:T(8,128)S(1)}, u32[]{:S(2)}, u32[]{:S(2)}) collective-permute-start(f32[6,16,128]{2,1,0:T(8,128)S(1)} %get-tuple-element.25), channel_id=1, source_target_pairs={{0,1},{1,0},{2,3},{3,2},{4,5},{5,4},{6,7},{7,6},{8,9},{9,8},{10,11... | collective-permute-start | bytes 147464 | tf_op jit(solution)/shard_map/ppermute | solution.py:422
  2.3 3.6 %collective-permute-start.1 = (f32[6,16,128]{2,1,0:T(8,128)S(1)}, f32[6,16,128]{2,1,0:T(8,128)S(1)}, u32[]{:S(2)}, u32[]{:S(2)}) collective-permute-start(f32[6,16,128]{2,1,0:T(8,128)S(1)} %get-tuple-element.26), channel_id=1, source_target_pairs={{0,7},{1,2},{2,1},{3,4},{4,3},{5,6},{6,5},{7,0},{8,15},{9,10},{10,... | collective-permute-start | bytes 147464 | tf_op jit(solution)/shard_map/ppermute | solution.py:423
  5.8 2.3 %tables.1 = (f32[16,128,128]{2,1,0:T(8,128)S(1)}, bf16[1024,256]{1,0:T(8,128)(2,1)S(1)}, bf16[128,1024]{1,0:T(8,128)(2,1)S(1)}, bf16[128,768]{1,0:T(8,128)(2,1)S...) custom-call(f32[16,128,128]{2,1,0:T(8,128)S(1)} %get-tuple-element.22., ...), custom_call_target="tpu_custom_call" | custom-call | flops 1000000000 | bytes 2000000 | tf_op jit(solution)/shard_map/tables/pallas_call | solution.py:425
  8.1 0.0 collective-permute-done.of_pair
  8.1 0.0 collective-permute-done.1.of_other
  8.2 0.1 corners.1
  8.2 1.6 %collective-permute-start.2 = (f32[272,128]{1,0:T(8,128)S(1)}, f32[272,128]{1,0:T(8,128)S(1)}, u32[]{:S(2)}, u32[]{:S(2)}) collective-permute-start(f32[272,128]{1,0:T(8,128)S(1)} %get-tuple-element.31), channel_id=1, source_target_pairs={{0,8},{8,16},{16,24},{24,0},{1,9},{9,17},{17,25},{25,1},{2,10},{10... | collective-permute-start | bytes 417800 | tf_op jit(solution)/shard_map/ppermute | solution.py:460
  9.8 2.2 %collective-permute-start.3 = (f32[272,128]{1,0:T(8,128)S(1)}, f32[272,128]{1,0:T(8,128)S(1)}, u32[]{:S(2)}, u32[]{:S(2)}) collective-permute-start(f32[272,128]{1,0:T(8,128)S(1)} %get-tuple-element.32), channel_id=1, source_target_pairs={{8,0},{16,8},{24,16},{0,24},{9,1},{17,9},{25,17},{1,25},{10,2},{18... | collective-permute-start | bytes 417800 | tf_op jit(solution)/shard_map/ppermute | solution.py:461
  12.1 8.0 %inner.1._ = f32[16,128,128]{2,1,0:T(8,128)} custom-call(f32[16,128,128]{2,1,0:T(8,128)S(1)} %get-tuple-element.24.once, f32[6,16,128]{2,1,0:T(8,128)S(1)} %get-tuple-element.23.coefs, f32[6,16,128]{2,1,0:T(8,128)S(1)} %collective-permute-done.of_pair, f32[6,16,128]{2,1,0:T(8,128)S(1)} %collective-permute-done.1.of_other, ...), custom_call_target="tpu_custom_call" | custom-call | tf_op jit(solution)/shard_map/inner/pallas_call | solution.py:469
  20.1 0.0 collective-permute-done.2.of_south
  20.1 0.0 collective-permute-done.3.of_north
  20.1 8.3 %outer.1 = f32[16,128,128]{2,1,0:T(8,128)} custom-call(f32[16,128,128]{2,1,0:T(8,128)S(1)} %get-tuple-element.24.once, f32[6,16,128]{2,1,0:T(8,128)S(1)} %get-tuple-element.23.coefs, f32[6,16,128]{2,1,0:T(8,128)S(1)} %collective-permute-done.of_pair, f32[6,16,128]{2,1,0:T(8,128)S(1)} %collective-permute-done.1.of_other, ...), custom_call_target="tpu_custom_call", output_to_operand_aliasing={{}: (15, {})} | custom-call | tf_op jit(solution)/shard_map/outer/pallas_call | solution.py:474
Async XLA Ops:
  1.7 6.4 %collective-permute-start = (f32[6,16,128]{2,1,0:T(8,128)S(1)}, f32[6,16,128]{2,1,0:T(8,128)S(1)}, u32[]{:S(2)}, u32[]{:S(2)}) collective-permute-start(f32[6,16,128]{2,1,0:T(8,128)S(1)} %get-tuple-element.25), channel_id=1, source_target_pairs={{0,1},{1,0},{2,3},{3,2},{4,5},{5,4},{6,7},{7,6},{8,9},{9,8},{10,11... | collective-permute-start | bytes 147464 | tf_op jit(solution)/shard_map/ppermute | solution.py:422
  2.3 5.9 %collective-permute-start.1 = (f32[6,16,128]{2,1,0:T(8,128)S(1)}, f32[6,16,128]{2,1,0:T(8,128)S(1)}, u32[]{:S(2)}, u32[]{:S(2)}) collective-permute-start(f32[6,16,128]{2,1,0:T(8,128)S(1)} %get-tuple-element.26), channel_id=1, source_target_pairs={{0,7},{1,2},{2,1},{3,4},{4,3},{5,6},{6,5},{7,0},{8,15},{9,10},{10,... | collective-permute-start | bytes 147464 | tf_op jit(solution)/shard_map/ppermute | solution.py:423
  8.2 11.9 %collective-permute-start.2 = (f32[272,128]{1,0:T(8,128)S(1)}, f32[272,128]{1,0:T(8,128)S(1)}, u32[]{:S(2)}, u32[]{:S(2)}) collective-permute-start(f32[272,128]{1,0:T(8,128)S(1)} %get-tuple-element.31), channel_id=1, source_target_pairs={{0,8},{8,16},{16,24},{24,0},{1,9},{9,17},{17,25},{25,1},{2,10},{10... | collective-permute-start | bytes 417800 | tf_op jit(solution)/shard_map/ppermute | solution.py:460
  9.8 10.3 %collective-permute-start.3 = (f32[272,128]{1,0:T(8,128)S(1)}, f32[272,128]{1,0:T(8,128)S(1)}, u32[]{:S(2)}, u32[]{:S(2)}) collective-permute-start(f32[272,128]{1,0:T(8,128)S(1)} %get-tuple-element.32), channel_id=1, source_target_pairs={{8,0},{16,8},{24,16},{0,24},{9,1},{17,9},{25,17},{1,25},{10,2},{18... | collective-permute-start | bytes 417800 | tf_op jit(solution)/shard_map/ppermute | solution.py:461

commit v4 on v3

--- a/solution.py
+++ b/solution.py
@@ -36,7 +36,7 @@
 
 
 def edge_kernel(
-    conc_in, wlon_in, wlat_in, mix_in, to_pair, to_other, own, to_north, to_south, conc, coefs,
+    conc_in, wlon_in, wlat_in, mix_in, to_pair, to_other, own, to_near, to_next, conc, coefs,
     winds, columns, sem,
 ):
     rows, species, cells = conc.shape
@@ -73,8 +73,19 @@
         )
     base = 2 * species
     pad = jnp.zeros((2, cells), f32)
-    for ref, g in ((to_north, rows - 1), (to_south, 0)):
-        ref[base : base + 8, :] = jnp.concatenate([coefs[k, g : g + 1] for k in range(6)] + [pad])
+    even_band = lax.rem(lax.axis_index("lat"), 2) == 0
+
+    def send(span, north, south):
+        to_near[span, :] = jnp.where(even_band, north, south)
+        to_next[span, :] = jnp.where(even_band, south, north)
+
+    send(
+        slice(base, base + 8),
+        *[
+            jnp.concatenate([coefs[k, g : g + 1] for k in range(6)] + [pad])
+            for g in (rows - 1, 0)
+        ],
+    )
     fetches[3].wait()
     lane = iota((species, cells), 1)
     picked = jnp.zeros((species, cells), f32)
@@ -88,8 +99,7 @@
     own[0] = first1
     own[1] = last1
     for q in range(2):
-        to_north[q * species : (q + 1) * species, :] = conc[rows - 2 + q]
-        to_south[q * species : (q + 1) * species, :] = conc[q]
+        send(slice(q * species, (q + 1) * species), conc[rows - 2 + q], conc[q])
 
 
 def sides(of_pair, of_other):
@@ -100,14 +110,19 @@
     )
 
 
-def corner_kernel(of_pair, of_other, _, __, ___, to_north, to_south, ends, sem):
+def corner_kernel(of_pair, of_other, _, __, ___, to_near, to_next, ends, sem):
     rows = of_pair.shape[1]
     left, right = sides(of_pair, of_other)
     near_l, near_r = left(0), right(0)
     pad = jnp.zeros((6, near_l.shape[1]), f32)
+    north, south = [
+        jnp.concatenate([near_l[g : g + 1], near_r[g : g + 1], pad], axis=0) for g in (rows - 1, 0)
+    ]
+    even_band = lax.rem(lax.axis_index("lat"), 2) == 0
+    ends[0] = jnp.where(even_band, north, south)
+    ends[1] = jnp.where(even_band, south, north)
     copies = []
-    for p, (g, ref) in enumerate(((rows - 1, to_north), (0, to_south))):
-        ends[p] = jnp.concatenate([near_l[g : g + 1], near_r[g : g + 1], pad], axis=0)
+    for p, ref in enumerate((to_near, to_next)):
         dest = ref.at[pl.ds(ref.shape[0] - 8, 8), :]
         copies.append(pltpu.make_async_copy(ends.at[p], dest, sem.at[p]))
         copies[p].start()
@@ -336,7 +351,7 @@
 
 
 def outer_kernel(
-    once, coefs, of_pair, of_other, own, conc, of_south, of_north,
+    once, coefs, of_pair, of_other, own, conc, of_near, of_next,
     gather, products, losses, speeds, decay, sun, lit, _, out, stage, columns, sem,
 ):
     rows, species, cells = conc.shape
@@ -344,26 +359,34 @@
     band = lax.axis_index("lat")
     below = jnp.where(band > 0, 1.0, 0.0)
     above = jnp.where(band < lax.axis_size("lat") - 1, 1.0, 0.0)
+    even_band = lax.rem(band, 2) == 0
+
+    def of_south(span):
+        return jnp.where(even_band, of_next[span, :], of_near[span, :])
+
+    def of_north(span):
+        return jnp.where(even_band, of_near[span, :], of_next[span, :])
+
     corners = [
-        r[base + 8 + k : base + 9 + k, :] * inside
-        for r, inside in ((of_south, below), (of_north, above))
+        got(slice(base + 8 + k, base + 9 + k)) * inside
+        for got, inside in ((of_south, below), (of_north, above))
         for k in range(2)
     ]
     turned = side_columns(of_pair, of_other, own, corners, columns)
 
-    def halo(ref, q, inside):
-        return ref[q * species : (q + 1) * species, :] * inside
-
-    def across(ref, k, inside):
-        return ref[base + k : base + k + 1, :] * inside
-
-    def outside(ref, near, far, beyond, home, back, inside):
-        center = halo(ref, near, inside)
-        stay, west, east = [across(ref, k, inside) for k in (0, 1, 3)]
+    def halo(got, q, inside):
+        return got(slice(q * species, (q + 1) * species)) * inside
+
+    def across(got, k, inside):
+        return got(slice(base + k, base + k + 1)) * inside
+
+    def outside(got, near, far, beyond, home, back, inside):
+        center = halo(got, near, inside)
+        stay, west, east = [across(got, k, inside) for k in (0, 1, 3)]
         row = stay * center + west * pltpu.roll(center, 1, 1)
         row = row + east * pltpu.roll(center, cells - 1, 1)
-        row = row + across(ref, beyond, inside) * halo(ref, far, inside)
-        return row + across(ref, back, inside) * home, across(ref, 5, inside)
+        row = row + across(got, beyond, inside) * halo(got, far, inside)
+        return row + across(got, back, inside) * home, across(got, 5, inside)
 
     def first(g):
         if g < 0:
@@ -400,7 +423,7 @@
 
     side = shape(6, rows, species)
     ends = shape(2 * species + 16, cells)
-    to_pair, to_other, own, to_north, to_south, held, coefs = pl.pallas_call(
+    to_pair, to_other, own, to_near, to_next, held, coefs = pl.pallas_call(
         edge_kernel,
         out_shape=(
             side, side, shape(2, rows, species), ends, ends,
@@ -417,8 +440,9 @@
 
     pair = [(i, i ^ 1) for i in range(lons)]
     other = [(i, (i - 1) % lons if i % 2 == 0 else (i + 1) % lons) for i in range(lons)]
-    north = [(i, (i + 1) % lats) for i in range(lats)]
-    south = [(j, i) for i, j in north]
+    near = [(i, i ^ 1 if i ^ 1 < lats else i) for i in range(lats)]
+    after = [i - 1 if i % 2 == 0 else i + 1 for i in range(lats)]
+    after = [(i, j if 0 <= j < lats else i) for i, j in enumerate(after)]
     of_pair = lax.ppermute(to_pair, "lon", pair)
     of_other = lax.ppermute(to_other, "lon", other)
 
@@ -450,15 +474,15 @@
         pinned(jnp.swapaxes(plan, 1, 2)), pinned(night_loss.reshape(1, species)), pinned(sun),
     )
 
-    to_north, to_south = pl.pallas_call(
+    to_near, to_next = pl.pallas_call(
         corner_kernel, out_shape=(ends, ends),
         in_specs=[vmem] * 2 + [hbm] * 3, out_specs=[hbm] * 2,
         scratch_shapes=[pltpu.VMEM((2, 8, species), f32), pltpu.SemaphoreType.DMA((2,))],
         input_output_aliases={2: 0, 3: 1},
         compiler_params=params, name="corners",
-    )(of_pair, of_other, to_north, to_south, tables[5])
-    of_south = lax.ppermute(to_north, "lat", north)
-    of_north = lax.ppermute(to_south, "lat", south)
+    )(of_pair, of_other, to_near, to_next, tables[5])
+    of_near = lax.ppermute(to_near, "lat", near)
+    of_next = lax.ppermute(to_next, "lat", after)
 
     shared = (once, coefs, of_pair, of_other, own)
     scratch = [
@@ -476,7 +500,7 @@
         in_specs=[vmem] * 15 + [hbm], out_specs=hbm, scratch_shapes=scratch,
         input_output_aliases={15: 0},
         compiler_params=params, name="outer",
-    )(*shared, held, of_south, of_north, *tables, inner)
+    )(*shared, held, of_near, of_next, *tables, inner)
 
 
 def solution(mesh):

time: 28.8 us -> 28.3 us (0.983)
  the two profiles are of different devices: /device:TPU:0 before, /device:TPU:8 now
where the time goes in v4:
time: 28.3 us; the launch traced here: 28.1 us
  Pallas kernels  20.3 us (72%)
  starting transfers between devices  7.74 us (27%)
    pallas_call x1, Pallas kernels, local(): pl.pallas_call(outer_kernel, out_shape=jax.ShapeDtypeStruct(conc.shape, f...  8.14 us
    pallas_call x1, Pallas kernels, local(): pl.pallas_call(inner_kernel, out_shape=jax.ShapeDtypeStruct(conc.shape, f...  8.04 us
    ppermute x1, starting transfers between devices, local(): of_next = lax.ppermute(to_next, 'lat', after)  4.6 us
    ppermute x1, starting transfers between devices, local(): of_other = lax.ppermute(to_other, 'lon', other)  2.55 us
    pallas_call x1, Pallas kernels, local(): pl.pallas_call(table_kernel, out_shape=(shape(rows, species, cells), shap...  2.31 us
    pallas_call x1, Pallas kernels, local(): pl.pallas_call(edge_kernel, out_shape=(side, side, shape(2, rows, species...  1.72 us
  transfers between devices with their start and end apart: 4, of which 0 were waited for; matrix products, arithmetic and copies ran while one was open for 0% of the time, Pallas kernels for 37%

profile of v4, /device:TPU:8, one launch (start us, length us, event | category | flops | bytes accessed | tf_op | source)
XLA Modules:
  0.0 28.1 jit_solution(6622554354282863957)
XLA Ops:
  0.0 1.7 %edges.1 = (f32[6,16,128]{2,1,0:T(8,128)S(1)}, f32[6,16,128]{2,1,0:T(8,128)S(1)}, f32[2,16,128]{2,1,0:T(8,128)S(1)}, f32[272,128]{1,0:T(8,128)S(1)}, f32[272,128...) custom-call(f32[16,128,128]{2,1,0:T(8,128)} %conc_in.1, f32[16,128]{1,0:T(8,128)} %wlon_in.1, ...), custom_call_target="tpu_custom_call" | custom-call | tf_op jit(solution)/shard_map/edges/pallas_call | solution.py:426
  1.7 0.1 collective-permute-start
  1.8 2.5 %collective-permute-start.1 = (f32[6,16,128]{2,1,0:T(8,128)S(1)}, f32[6,16,128]{2,1,0:T(8,128)S(1)}, u32[]{:S(2)}, u32[]{:S(2)}) collective-permute-start(f32[6,16,128]{2,1,0:T(8,128)S(1)} %get-tuple-element.26), channel_id=1, source_target_pairs={{0,7},{1,2},{2,1},{3,4},{4,3},{5,6},{6,5},{7,0},{8,15},{9,10},{10,... | collective-permute-start | bytes 147464 | tf_op jit(solution)/shard_map/ppermute | solution.py:447
  4.4 2.3 %tables.1 = (f32[16,128,128]{2,1,0:T(8,128)S(1)}, bf16[1024,256]{1,0:T(8,128)(2,1)S(1)}, bf16[128,1024]{1,0:T(8,128)(2,1)S(1)}, bf16[128,768]{1,0:T(8,128)(2,1)S...) custom-call(f32[16,128,128]{2,1,0:T(8,128)S(1)} %get-tuple-element.22., ...), custom_call_target="tpu_custom_call" | custom-call | flops 1000000000 | bytes 2000000 | tf_op jit(solution)/shard_map/tables/pallas_call | solution.py:449
  6.7 0.0 collective-permute-done.of_pair
  6.7 0.0 collective-permute-done.1.of_other
  6.7 0.1 corners.1
  6.8 0.5 %collective-permute-start.2 = (f32[272,128]{1,0:T(8,128)S(1)}, f32[272,128]{1,0:T(8,128)S(1)}, u32[]{:S(2)}, u32[]{:S(2)}) collective-permute-start(f32[272,128]{1,0:T(8,128)S(1)} %get-tuple-element.31), channel_id=1, source_target_pairs={{0,8},{8,0},{16,24},{24,16},{1,9},{9,1},{17,25},{25,17},{2,10},{10... | collective-permute-start | bytes 417800 | tf_op jit(solution)/shard_map/ppermute | solution.py:484
  7.3 4.6 %collective-permute-start.3 = (f32[272,128]{1,0:T(8,128)S(1)}, f32[272,128]{1,0:T(8,128)S(1)}, u32[]{:S(2)}, u32[]{:S(2)}) collective-permute-start(f32[272,128]{1,0:T(8,128)S(1)} %get-tuple-element.32), channel_id=1, source_target_pairs={{0,0},{8,16},{16,8},{24,24},{1,1},{9,17},{17,9},{25,25},{2,2},{10,... | collective-permute-start | bytes 417800 | tf_op jit(solution)/shard_map/ppermute | solution.py:485
  11.9 8.0 %inner.1._ = f32[16,128,128]{2,1,0:T(8,128)} custom-call(f32[16,128,128]{2,1,0:T(8,128)S(1)} %get-tuple-element.24.once, f32[6,16,128]{2,1,0:T(8,128)S(1)} %get-tuple-element.23.coefs, f32[6,16,128]{2,1,0:T(8,128)S(1)} %collective-permute-done.of_pair, f32[6,16,128]{2,1,0:T(8,128)S(1)} %collective-permute-done.1.of_other, ...), custom_call_target="tpu_custom_call" | custom-call | tf_op jit(solution)/shard_map/inner/pallas_call | solution.py:493
  19.9 0.0 collective-permute-done.2.of_near
  19.9 0.0 collective-permute-done.3.of_next
  20.0 8.1 %outer.1 = f32[16,128,128]{2,1,0:T(8,128)} custom-call(f32[16,128,128]{2,1,0:T(8,128)S(1)} %get-tuple-element.24.once, f32[6,16,128]{2,1,0:T(8,128)S(1)} %get-tuple-element.23.coefs, f32[6,16,128]{2,1,0:T(8,128)S(1)} %collective-permute-done.of_pair, f32[6,16,128]{2,1,0:T(8,128)S(1)} %collective-permute-done.1.of_other, ...), custom_call_target="tpu_custom_call", output_to_operand_aliasing={{}: (15, {})} | custom-call | tf_op jit(solution)/shard_map/outer/pallas_call | solution.py:498
Async XLA Ops:
  1.7 5.0 %collective-permute-start = (f32[6,16,128]{2,1,0:T(8,128)S(1)}, f32[6,16,128]{2,1,0:T(8,128)S(1)}, u32[]{:S(2)}, u32[]{:S(2)}) collective-permute-start(f32[6,16,128]{2,1,0:T(8,128)S(1)} %get-tuple-element.25), channel_id=1, source_target_pairs={{0,1},{1,0},{2,3},{3,2},{4,5},{5,4},{6,7},{7,6},{8,9},{9,8},{10,11... | collective-permute-start | bytes 147464 | tf_op jit(solution)/shard_map/ppermute | solution.py:446
  1.8 4.9 %collective-permute-start.1 = (f32[6,16,128]{2,1,0:T(8,128)S(1)}, f32[6,16,128]{2,1,0:T(8,128)S(1)}, u32[]{:S(2)}, u32[]{:S(2)}) collective-permute-start(f32[6,16,128]{2,1,0:T(8,128)S(1)} %get-tuple-element.26), channel_id=1, source_target_pairs={{0,7},{1,2},{2,1},{3,4},{4,3},{5,6},{6,5},{7,0},{8,15},{9,10},{10,... | collective-permute-start | bytes 147464 | tf_op jit(solution)/shard_map/ppermute | solution.py:447
  6.8 13.2 %collective-permute-start.2 = (f32[272,128]{1,0:T(8,128)S(1)}, f32[272,128]{1,0:T(8,128)S(1)}, u32[]{:S(2)}, u32[]{:S(2)}) collective-permute-start(f32[272,128]{1,0:T(8,128)S(1)} %get-tuple-element.31), channel_id=1, source_target_pairs={{0,8},{8,0},{16,24},{24,16},{1,9},{9,1},{17,25},{25,17},{2,10},{10... | collective-permute-start | bytes 417800 | tf_op jit(solution)/shard_map/ppermute | solution.py:484
  7.3 12.7 %collective-permute-start.3 = (f32[272,128]{1,0:T(8,128)S(1)}, f32[272,128]{1,0:T(8,128)S(1)}, u32[]{:S(2)}, u32[]{:S(2)}) collective-permute-start(f32[272,128]{1,0:T(8,128)S(1)} %get-tuple-element.32), channel_id=1, source_target_pairs={{0,0},{8,16},{16,8},{24,24},{1,1},{9,17},{17,9},{25,25},{2,2},{10,... | collective-permute-start | bytes 417800 | tf_op jit(solution)/shard_map/ppermute | solution.py:485

commit v5 on v4

--- a/solution.py
+++ b/solution.py
@@ -440,9 +440,13 @@
 
     pair = [(i, i ^ 1) for i in range(lons)]
     other = [(i, (i - 1) % lons if i % 2 == 0 else (i + 1) % lons) for i in range(lons)]
-    near = [(i, i ^ 1 if i ^ 1 < lats else i) for i in range(lats)]
-    after = [i - 1 if i % 2 == 0 else i + 1 for i in range(lats)]
-    after = [(i, j if 0 <= j < lats else i) for i, j in enumerate(after)]
+    near, after = [], []
+    for b in range(lats):
+        step_near, step_after = (1, -1) if b % 2 == 0 else (-1, 1)
+        for perm, c in ((near, b + step_near), (after, b + step_after)):
+            for i in range(lons):
+                target = (c, i) if 0 <= c < lats else (b, i ^ 1)
+                perm.append((b * lons + i, target[0] * lons + target[1]))
     of_pair = lax.ppermute(to_pair, "lon", pair)
     of_other = lax.ppermute(to_other, "lon", other)
 
@@ -481,8 +485,8 @@
         input_output_aliases={2: 0, 3: 1},
         compiler_params=params, name="corners",
     )(of_pair, of_other, to_near, to_next, tables[5])
-    of_near = lax.ppermute(to_near, "lat", near)
-    of_next = lax.ppermute(to_next, "lat", after)
+    of_near = lax.ppermute(to_near, ("lat", "lon"), near)
+    of_next = lax.ppermute(to_next, ("lat", "lon"), after)
 
     shared = (once, coefs, of_pair, of_other, own)
     scratch = [

time: 28.3 us -> 26.8 us (0.947)
  the two profiles are of different devices: /device:TPU:8 before, /device:TPU:0 now
where the time goes in v5:
time: 26.8 us; the launch traced here: 26.4 us
  Pallas kernels  20.5 us (76%)
  starting transfers between devices  5.72 us (21%)
    pallas_call x1, Pallas kernels, local(): pl.pallas_call(outer_kernel, out_shape=jax.ShapeDtypeStruct(conc.shape, f...  8.35 us
    pallas_call x1, Pallas kernels, local(): pl.pallas_call(inner_kernel, out_shape=jax.ShapeDtypeStruct(conc.shape, f...  8.03 us
    ppermute x1, starting transfers between devices, local(): of_other = lax.ppermute(to_other, 'lon', other)  3.56 us
    pallas_call x1, Pallas kernels, local(): pl.pallas_call(table_kernel, out_shape=(shape(rows, species, cells), shap...  2.31 us
    pallas_call x1, Pallas kernels, local(): pl.pallas_call(edge_kernel, out_shape=(side, side, shape(2, rows, species...  1.72 us
    ppermute x1, starting transfers between devices, local(): of_near = lax.ppermute(to_near, ('lat', 'lon'), near)  1.64 us
  transfers between devices with their start and end apart: 4, of which 0 were waited for; matrix products, arithmetic and copies ran while one was open for 0% of the time, Pallas kernels for 39%

profile of v5, /device:TPU:0, one launch (start us, length us, event | category | flops | bytes accessed | tf_op | source)
XLA Modules:
  0.0 26.4 jit_solution(14767272590550771829)
XLA Ops:
  0.0 1.7 %edges.1 = (f32[6,16,128]{2,1,0:T(8,128)S(1)}, f32[6,16,128]{2,1,0:T(8,128)S(1)}, f32[2,16,128]{2,1,0:T(8,128)S(1)}, f32[272,128]{1,0:T(8,128)S(1)}, f32[272,128...) custom-call(f32[16,128,128]{2,1,0:T(8,128)} %conc_in.1, f32[16,128]{1,0:T(8,128)} %wlon_in.1, ...), custom_call_target="tpu_custom_call" | custom-call | tf_op jit(solution)/shard_map/edges/pallas_call | solution.py:426
  1.7 0.5 %collective-permute-start = (f32[6,16,128]{2,1,0:T(8,128)S(1)}, f32[6,16,128]{2,1,0:T(8,128)S(1)}, u32[]{:S(2)}, u32[]{:S(2)}) collective-permute-start(f32[6,16,128]{2,1,0:T(8,128)S(1)} %get-tuple-element.25), channel_id=1, source_target_pairs={{0,1},{1,0},{2,3},{3,2},{4,5},{5,4},{6,7},{7,6},{8,9},{9,8},{10,11... | collective-permute-start | bytes 147464 | tf_op jit(solution)/shard_map/ppermute | solution.py:450
  2.3 3.6 %collective-permute-start.1 = (f32[6,16,128]{2,1,0:T(8,128)S(1)}, f32[6,16,128]{2,1,0:T(8,128)S(1)}, u32[]{:S(2)}, u32[]{:S(2)}) collective-permute-start(f32[6,16,128]{2,1,0:T(8,128)S(1)} %get-tuple-element.26), channel_id=1, source_target_pairs={{0,7},{1,2},{2,1},{3,4},{4,3},{5,6},{6,5},{7,0},{8,15},{9,10},{10,... | collective-permute-start | bytes 147464 | tf_op jit(solution)/shard_map/ppermute | solution.py:451
  5.8 2.3 %tables.1 = (f32[16,128,128]{2,1,0:T(8,128)S(1)}, bf16[1024,256]{1,0:T(8,128)(2,1)S(1)}, bf16[128,1024]{1,0:T(8,128)(2,1)S(1)}, bf16[128,768]{1,0:T(8,128)(2,1)S...) custom-call(f32[16,128,128]{2,1,0:T(8,128)S(1)} %get-tuple-element.22., ...), custom_call_target="tpu_custom_call" | custom-call | flops 1000000000 | bytes 2000000 | tf_op jit(solution)/shard_map/tables/pallas_call | solution.py:453
  8.1 0.0 collective-permute-done.of_pair
  8.1 0.0 collective-permute-done.1.of_other
  8.1 0.1 corners.1
  8.2 1.6 %collective-permute-start.2 = (f32[272,128]{1,0:T(8,128)S(1)}, f32[272,128]{1,0:T(8,128)S(1)}, u32[]{:S(2)}, u32[]{:S(2)}) collective-permute-start(f32[272,128]{1,0:T(8,128)S(1)} %get-tuple-element.31), channel_id=1, source_target_pairs={{0,8},{1,9},{2,10},{3,11},{4,12},{5,13},{6,14},{7,15},{8,0},{9,1},... | collective-permute-start | bytes 417800 | tf_op jit(solution)/shard_map/ppermute | solution.py:488
  9.9 0.0 collective-permute-start.3
  9.9 8.0 %inner.1._ = f32[16,128,128]{2,1,0:T(8,128)} custom-call(f32[16,128,128]{2,1,0:T(8,128)S(1)} %get-tuple-element.24.once, f32[6,16,128]{2,1,0:T(8,128)S(1)} %get-tuple-element.23.coefs, f32[6,16,128]{2,1,0:T(8,128)S(1)} %collective-permute-done.of_pair, f32[6,16,128]{2,1,0:T(8,128)S(1)} %collective-permute-done.1.of_other, ...), custom_call_target="tpu_custom_call" | custom-call | tf_op jit(solution)/shard_map/inner/pallas_call | solution.py:497
  17.9 0.0 collective-permute-done.2.of_near
  17.9 0.0 collective-permute-done.3.of_next
  17.9 8.3 %outer.1 = f32[16,128,128]{2,1,0:T(8,128)} custom-call(f32[16,128,128]{2,1,0:T(8,128)S(1)} %get-tuple-element.24.once, f32[6,16,128]{2,1,0:T(8,128)S(1)} %get-tuple-element.23.coefs, f32[6,16,128]{2,1,0:T(8,128)S(1)} %collective-permute-done.of_pair, f32[6,16,128]{2,1,0:T(8,128)S(1)} %collective-permute-done.1.of_other, ...), custom_call_target="tpu_custom_call", output_to_operand_aliasing={{}: (15, {})} | custom-call | tf_op jit(solution)/shard_map/outer/pallas_call | solution.py:502
Async XLA Ops:
  1.7 6.4 %collective-permute-start = (f32[6,16,128]{2,1,0:T(8,128)S(1)}, f32[6,16,128]{2,1,0:T(8,128)S(1)}, u32[]{:S(2)}, u32[]{:S(2)}) collective-permute-start(f32[6,16,128]{2,1,0:T(8,128)S(1)} %get-tuple-element.25), channel_id=1, source_target_pairs={{0,1},{1,0},{2,3},{3,2},{4,5},{5,4},{6,7},{7,6},{8,9},{9,8},{10,11... | collective-permute-start | bytes 147464 | tf_op jit(solution)/shard_map/ppermute | solution.py:450
  2.3 5.9 %collective-permute-start.1 = (f32[6,16,128]{2,1,0:T(8,128)S(1)}, f32[6,16,128]{2,1,0:T(8,128)S(1)}, u32[]{:S(2)}, u32[]{:S(2)}) collective-permute-start(f32[6,16,128]{2,1,0:T(8,128)S(1)} %get-tuple-element.26), channel_id=1, source_target_pairs={{0,7},{1,2},{2,1},{3,4},{4,3},{5,6},{6,5},{7,0},{8,15},{9,10},{10,... | collective-permute-start | bytes 147464 | tf_op jit(solution)/shard_map/ppermute | solution.py:451
  8.2 9.7 %collective-permute-start.2 = (f32[272,128]{1,0:T(8,128)S(1)}, f32[272,128]{1,0:T(8,128)S(1)}, u32[]{:S(2)}, u32[]{:S(2)}) collective-permute-start(f32[272,128]{1,0:T(8,128)S(1)} %get-tuple-element.31), channel_id=1, source_target_pairs={{0,8},{1,9},{2,10},{3,11},{4,12},{5,13},{6,14},{7,15},{8,0},{9,1},... | collective-permute-start | bytes 417800 | tf_op jit(solution)/shard_map/ppermute | solution.py:488
  9.9 8.1 %collective-permute-start.3 = (f32[272,128]{1,0:T(8,128)S(1)}, f32[272,128]{1,0:T(8,128)S(1)}, u32[]{:S(2)}, u32[]{:S(2)}) collective-permute-start(f32[272,128]{1,0:T(8,128)S(1)} %get-tuple-element.32), channel_id=1, source_target_pairs={{0,1},{1,0},{2,3},{3,2},{4,5},{5,4},{6,7},{7,6},{8,16},{9,17},{10,... | collective-permute-start | bytes 417800 | tf_op jit(solution)/shard_map/ppermute | solution.py:489

commit v6 on v5

--- a/solution.py
+++ b/solution.py
@@ -44,7 +44,13 @@
         pltpu.make_async_copy(ref, winds.at[k], sem.at[k])
         for k, ref in enumerate((wlon_in, wlat_in, mix_in))
     ]
-    fetches.append(pltpu.make_async_copy(conc_in, conc, sem.at[3]))
+    part = rows // 4
+    fetches += [
+        pltpu.make_async_copy(
+            conc_in.at[pl.ds(q * part, part)], conc.at[pl.ds(q * part, part)], sem.at[3 + q]
+        )
+        for q in range(4)
+    ]
     for fetch in fetches:
         fetch.start()
     for fetch in fetches[:3]:
@@ -65,12 +71,11 @@
         to_pair[k] = jnp.where(even, right, left)
         to_other[k] = jnp.where(even, left, right)
 
+    right, left = jnp.zeros((rows, cells), f32), jnp.zeros((rows, cells), f32)
     for k, ref in enumerate((stay, west, south, mix)):
-        put(
-            2 + k,
-            jnp.broadcast_to(ref[:, cells - 1 : cells], (rows, species)),
-            jnp.broadcast_to(ref[:, 0:1], (rows, species)),
-        )
+        right = jnp.where(place == k, ref[:, cells - 1 : cells], right)
+        left = jnp.where(place == k, ref[:, 0:1], left)
+    put(2, right, left)
     base = 2 * species
     pad = jnp.zeros((2, cells), f32)
     even_band = lax.rem(lax.axis_index("lat"), 2) == 0
@@ -86,10 +91,11 @@
             for g in (rows - 1, 0)
         ],
     )
-    fetches[3].wait()
     lane = iota((species, cells), 1)
     picked = jnp.zeros((species, cells), f32)
     for g in range(rows):
+        if g % part == 0:
+            fetches[3 + g // part].wait()
         turned = pltpu.roll(conc[g], (4 * g + 2) % cells, 1)
         picked = jnp.where((lane >= 4 * g) & (lane < 4 * g + 4), turned, picked)
     columns[...] = picked.T
@@ -284,7 +290,8 @@
     def moved(near, west, east, south, north, side):
         south = jnp.concatenate([south, near[:-1]], axis=0)
         north = jnp.concatenate([near[1:], north], axis=0)
-        return side(2) * near + side(3) * west + side(4) * south + side(5) * (east + north)
+        stay, w, s, e = [side(2)[:, k : k + 1] for k in range(4)]
+        return stay * near + w * west + s * south + e * (east + north)
 
     columns[...] = jnp.zeros_like(columns)
     columns[pl.ds(0, rows, stride=2), :] = near_r
@@ -421,7 +428,7 @@
     def shape(*dims, dtype=f32):
         return KEPT(dims, dtype)
 
-    side = shape(6, rows, species)
+    side = shape(3, rows, species)
     ends = shape(2 * species + 16, cells)
     to_pair, to_other, own, to_near, to_next, held, coefs = pl.pallas_call(
         edge_kernel,
@@ -433,7 +440,7 @@
         scratch_shapes=[
             pltpu.VMEM((3, rows, cells), f32),
             pltpu.VMEM((cells, species), f32),
-            pltpu.SemaphoreType.DMA((4,)),
+            pltpu.SemaphoreType.DMA((7,)),
         ],
         compiler_params=params, name="edges",
     )(*[pinned(x) for x in (conc, wind_lon, wind_lat, mixing)])

time: 26.8 us -> 26.8 us (level)
  no operation moved by 1% of the time
where the time goes in v6:
time: 26.8 us; the launch traced here: 26.5 us
  Pallas kernels  20.5 us (76%)
  starting transfers between devices  5.72 us (21%)
    pallas_call x1, Pallas kernels, local(): pl.pallas_call(outer_kernel, out_shape=jax.ShapeDtypeStruct(conc.shape, f...  8.39 us
    pallas_call x1, Pallas kernels, local(): pl.pallas_call(inner_kernel, out_shape=jax.ShapeDtypeStruct(conc.shape, f...  8.09 us
    ppermute x1, starting transfers between devices, local(): of_other = lax.ppermute(to_other, 'lon', other)  3.56 us
    pallas_call x1, Pallas kernels, local(): pl.pallas_call(table_kernel, out_shape=(shape(rows, species, cells), shap...  2.31 us
    pallas_call x1, Pallas kernels, local(): pl.pallas_call(edge_kernel, out_shape=(side, side, shape(2, rows, species...  1.68 us
    ppermute x1, starting transfers between devices, local(): of_near = lax.ppermute(to_near, ('lat', 'lon'), near)  1.64 us
  transfers between devices with their start and end apart: 4, of which 0 were waited for; matrix products, arithmetic and copies ran while one was open for 0% of the time, Pallas kernels for 39%

profile of v6, /device:TPU:0, one launch (start us, length us, event | category | flops | bytes accessed | tf_op | source)
XLA Modules:
  0.0 26.5 jit_solution(2896557600723982042)
XLA Ops:
  0.0 1.7 %edges.1 = (f32[3,16,128]{2,1,0:T(8,128)S(1)}, f32[3,16,128]{2,1,0:T(8,128)S(1)}, f32[2,16,128]{2,1,0:T(8,128)S(1)}, f32[272,128]{1,0:T(8,128)S(1)}, f32[272,128...) custom-call(f32[16,128,128]{2,1,0:T(8,128)} %conc_in.1, f32[16,128]{1,0:T(8,128)} %wlon_in.1, ...), custom_call_target="tpu_custom_call" | custom-call | tf_op jit(solution)/shard_map/edges/pallas_call | solution.py:433
  1.7 0.5 %collective-permute-start = (f32[3,16,128]{2,1,0:T(8,128)S(1)}, f32[3,16,128]{2,1,0:T(8,128)S(1)}, u32[]{:S(2)}, u32[]{:S(2)}) collective-permute-start(f32[3,16,128]{2,1,0:T(8,128)S(1)} %get-tuple-element.25), channel_id=1, source_target_pairs={{0,1},{1,0},{2,3},{3,2},{4,5},{5,4},{6,7},{7,6},{8,9},{9,8},{10,11... | collective-permute-start | bytes 73736 | tf_op jit(solution)/shard_map/ppermute | solution.py:457
  2.2 3.6 %collective-permute-start.1 = (f32[3,16,128]{2,1,0:T(8,128)S(1)}, f32[3,16,128]{2,1,0:T(8,128)S(1)}, u32[]{:S(2)}, u32[]{:S(2)}) collective-permute-start(f32[3,16,128]{2,1,0:T(8,128)S(1)} %get-tuple-element.26), channel_id=1, source_target_pairs={{0,7},{1,2},{2,1},{3,4},{4,3},{5,6},{6,5},{7,0},{8,15},{9,10},{10,... | collective-permute-start | bytes 73736 | tf_op jit(solution)/shard_map/ppermute | solution.py:458
  5.8 2.3 %tables.1 = (f32[16,128,128]{2,1,0:T(8,128)S(1)}, bf16[1024,256]{1,0:T(8,128)(2,1)S(1)}, bf16[128,1024]{1,0:T(8,128)(2,1)S(1)}, bf16[128,768]{1,0:T(8,128)(2,1)S...) custom-call(f32[16,128,128]{2,1,0:T(8,128)S(1)} %get-tuple-element.22., ...), custom_call_target="tpu_custom_call" | custom-call | flops 1000000000 | bytes 2000000 | tf_op jit(solution)/shard_map/tables/pallas_call | solution.py:460
  8.1 0.0 collective-permute-done.of_pair
  8.1 0.0 collective-permute-done.1.of_other
  8.1 0.1 corners.1
  8.2 1.6 %collective-permute-start.2 = (f32[272,128]{1,0:T(8,128)S(1)}, f32[272,128]{1,0:T(8,128)S(1)}, u32[]{:S(2)}, u32[]{:S(2)}) collective-permute-start(f32[272,128]{1,0:T(8,128)S(1)} %get-tuple-element.31), channel_id=1, source_target_pairs={{0,8},{1,9},{2,10},{3,11},{4,12},{5,13},{6,14},{7,15},{8,0},{9,1},... | collective-permute-start | bytes 417800 | tf_op jit(solution)/shard_map/ppermute | solution.py:495
  9.8 0.0 collective-permute-start.3
  9.8 8.1 %inner.1._ = f32[16,128,128]{2,1,0:T(8,128)} custom-call(f32[16,128,128]{2,1,0:T(8,128)S(1)} %get-tuple-element.24.once, f32[6,16,128]{2,1,0:T(8,128)S(1)} %get-tuple-element.23.coefs, f32[3,16,128]{2,1,0:T(8,128)S(1)} %collective-permute-done.of_pair, f32[3,16,128]{2,1,0:T(8,128)S(1)} %collective-permute-done.1.of_other, ...), custom_call_target="tpu_custom_call" | custom-call | tf_op jit(solution)/shard_map/inner/pallas_call | solution.py:504
  17.9 0.0 collective-permute-done.2.of_near
  17.9 0.0 collective-permute-done.3.of_next
  17.9 8.4 %outer.1 = f32[16,128,128]{2,1,0:T(8,128)} custom-call(f32[16,128,128]{2,1,0:T(8,128)S(1)} %get-tuple-element.24.once, f32[6,16,128]{2,1,0:T(8,128)S(1)} %get-tuple-element.23.coefs, f32[3,16,128]{2,1,0:T(8,128)S(1)} %collective-permute-done.of_pair, f32[3,16,128]{2,1,0:T(8,128)S(1)} %collective-permute-done.1.of_other, ...), custom_call_target="tpu_custom_call", output_to_operand_aliasing={{}: (15, {})} | custom-call | tf_op jit(solution)/shard_map/outer/pallas_call | solution.py:509
Async XLA Ops:
  1.7 6.4 %collective-permute-start = (f32[3,16,128]{2,1,0:T(8,128)S(1)}, f32[3,16,128]{2,1,0:T(8,128)S(1)}, u32[]{:S(2)}, u32[]{:S(2)}) collective-permute-start(f32[3,16,128]{2,1,0:T(8,128)S(1)} %get-tuple-element.25), channel_id=1, source_target_pairs={{0,1},{1,0},{2,3},{3,2},{4,5},{5,4},{6,7},{7,6},{8,9},{9,8},{10,11... | collective-permute-start | bytes 73736 | tf_op jit(solution)/shard_map/ppermute | solution.py:457
  2.2 5.9 %collective-permute-start.1 = (f32[3,16,128]{2,1,0:T(8,128)S(1)}, f32[3,16,128]{2,1,0:T(8,128)S(1)}, u32[]{:S(2)}, u32[]{:S(2)}) collective-permute-start(f32[3,16,128]{2,1,0:T(8,128)S(1)} %get-tuple-element.26), channel_id=1, source_target_pairs={{0,7},{1,2},{2,1},{3,4},{4,3},{5,6},{6,5},{7,0},{8,15},{9,10},{10,... | collective-permute-start | bytes 73736 | tf_op jit(solution)/shard_map/ppermute | solution.py:458
  8.2 9.7 %collective-permute-start.2 = (f32[272,128]{1,0:T(8,128)S(1)}, f32[272,128]{1,0:T(8,128)S(1)}, u32[]{:S(2)}, u32[]{:S(2)}) collective-permute-start(f32[272,128]{1,0:T(8,128)S(1)} %get-tuple-element.31), channel_id=1, source_target_pairs={{0,8},{1,9},{2,10},{3,11},{4,12},{5,13},{6,14},{7,15},{8,0},{9,1},... | collective-permute-start | bytes 417800 | tf_op jit(solution)/shard_map/ppermute | solution.py:495
  9.8 8.1 %collective-permute-start.3 = (f32[272,128]{1,0:T(8,128)S(1)}, f32[272,128]{1,0:T(8,128)S(1)}, u32[]{:S(2)}, u32[]{:S(2)}) collective-permute-start(f32[272,128]{1,0:T(8,128)S(1)} %get-tuple-element.32), channel_id=1, source_target_pairs={{0,1},{1,0},{2,3},{3,2},{4,5},{5,4},{6,7},{7,6},{8,16},{9,17},{10,... | collective-permute-start | bytes 417800 | tf_op jit(solution)/shard_map/ppermute | solution.py:496

commit v7 on v6

--- a/solution.py
+++ b/solution.py
@@ -36,7 +36,7 @@
 
 
 def edge_kernel(
-    conc_in, wlon_in, wlat_in, mix_in, to_pair, to_other, own, to_near, to_next, conc, coefs,
+    conc_in, wlon_in, wlat_in, mix_in, to_other, to_pair, own, to_next, to_near, conc, coefs,
     winds, columns, sem,
 ):
     rows, species, cells = conc.shape
@@ -116,7 +116,7 @@
     )
 
 
-def corner_kernel(of_pair, of_other, _, __, ___, to_near, to_next, ends, sem):
+def corner_kernel(of_other, of_pair, _, __, ___, to_next, to_near, ends, sem):
     rows = of_pair.shape[1]
     left, right = sides(of_pair, of_other)
     near_l, near_r = left(0), right(0)
@@ -125,10 +125,10 @@
         jnp.concatenate([near_l[g : g + 1], near_r[g : g + 1], pad], axis=0) for g in (rows - 1, 0)
     ]
     even_band = lax.rem(lax.axis_index("lat"), 2) == 0
-    ends[0] = jnp.where(even_band, north, south)
-    ends[1] = jnp.where(even_band, south, north)
+    ends[0] = jnp.where(even_band, south, north)
+    ends[1] = jnp.where(even_band, north, south)
     copies = []
-    for p, ref in enumerate((to_near, to_next)):
+    for p, ref in enumerate((to_next, to_near)):
         dest = ref.at[pl.ds(ref.shape[0] - 8, 8), :]
         copies.append(pltpu.make_async_copy(ends.at[p], dest, sem.at[p]))
         copies[p].start()
@@ -430,7 +430,7 @@
 
     side = shape(3, rows, species)
     ends = shape(2 * species + 16, cells)
-    to_pair, to_other, own, to_near, to_next, held, coefs = pl.pallas_call(
+    to_other, to_pair, own, to_next, to_near, held, coefs = pl.pallas_call(
         edge_kernel,
         out_shape=(
             side, side, shape(2, rows, species), ends, ends,
@@ -454,8 +454,8 @@
             for i in range(lons):
                 target = (c, i) if 0 <= c < lats else (b, i ^ 1)
                 perm.append((b * lons + i, target[0] * lons + target[1]))
+    of_other = lax.ppermute(to_other, "lon", other)
     of_pair = lax.ppermute(to_pair, "lon", pair)
-    of_other = lax.ppermute(to_other, "lon", other)
 
     once, *tables = pl.pallas_call(
         table_kernel,
@@ -485,15 +485,15 @@
         pinned(jnp.swapaxes(plan, 1, 2)), pinned(night_loss.reshape(1, species)), pinned(sun),
     )
 
-    to_near, to_next = pl.pallas_call(
+    to_next, to_near = pl.pallas_call(
         corner_kernel, out_shape=(ends, ends),
         in_specs=[vmem] * 2 + [hbm] * 3, out_specs=[hbm] * 2,
         scratch_shapes=[pltpu.VMEM((2, 8, species), f32), pltpu.SemaphoreType.DMA((2,))],
         input_output_aliases={2: 0, 3: 1},
         compiler_params=params, name="corners",
-    )(of_pair, of_other, to_near, to_next, tables[5])
+    )(of_other, of_pair, to_next, to_near, tables[5])
+    of_next = lax.ppermute(to_next, ("lat", "lon"), after)
     of_near = lax.ppermute(to_near, ("lat", "lon"), near)
-    of_next = lax.ppermute(to_next, ("lat", "lon"), after)
 
     shared = (once, coefs, of_pair, of_other, own)
     scratch = [

time: 26.8 us -> 26.8 us (level)
  no operation moved by 1% of the time
where the time goes in v7:
time: 26.8 us; the launch traced here: 26.5 us
  Pallas kernels  20.5 us (76%)
  starting transfers between devices  5.72 us (21%)
    pallas_call x1, Pallas kernels, local(): pl.pallas_call(outer_kernel, out_shape=jax.ShapeDtypeStruct(conc.shape, f...  8.4 us
    pallas_call x1, Pallas kernels, local(): pl.pallas_call(inner_kernel, out_shape=jax.ShapeDtypeStruct(conc.shape, f...  8.1 us
    ppermute x1, starting transfers between devices, local(): of_other = lax.ppermute(to_other, 'lon', other)  3.56 us
    pallas_call x1, Pallas kernels, local(): pl.pallas_call(table_kernel, out_shape=(shape(rows, species, cells), shap...  2.31 us
    pallas_call x1, Pallas kernels, local(): pl.pallas_call(edge_kernel, out_shape=(side, side, shape(2, rows, species...  1.68 us
    ppermute x1, starting transfers between devices, local(): of_near = lax.ppermute(to_near, ('lat', 'lon'), near)  1.64 us
  transfers between devices with their start and end apart: 4, of which 0 were waited for; matrix products, arithmetic and copies ran while one was open for 0% of the time, Pallas kernels for 39%

profile of v7, /device:TPU:0, one launch (start us, length us, event | category | flops | bytes accessed | tf_op | source)
XLA Modules:
  0.0 26.5 jit_solution(8884350375891415393)
XLA Ops:
  0.0 1.7 %edges.1 = (f32[3,16,128]{2,1,0:T(8,128)S(1)}, f32[3,16,128]{2,1,0:T(8,128)S(1)}, f32[2,16,128]{2,1,0:T(8,128)S(1)}, f32[272,128]{1,0:T(8,128)S(1)}, f32[272,128...) custom-call(f32[16,128,128]{2,1,0:T(8,128)} %conc_in.1, f32[16,128]{1,0:T(8,128)} %wlon_in.1, ...), custom_call_target="tpu_custom_call" | custom-call | tf_op jit(solution)/shard_map/edges/pallas_call | solution.py:433
  1.7 0.5 %collective-permute-start = (f32[3,16,128]{2,1,0:T(8,128)S(1)}, f32[3,16,128]{2,1,0:T(8,128)S(1)}, u32[]{:S(2)}, u32[]{:S(2)}) collective-permute-start(f32[3,16,128]{2,1,0:T(8,128)S(1)} %get-tuple-element.25), channel_id=1, source_target_pairs={{0,1},{1,0},{2,3},{3,2},{4,5},{5,4},{6,7},{7,6},{8,9},{9,8},{10,11... | collective-permute-start | bytes 73736 | tf_op jit(solution)/shard_map/ppermute | solution.py:458
  2.2 3.6 %collective-permute-start.1 = (f32[3,16,128]{2,1,0:T(8,128)S(1)}, f32[3,16,128]{2,1,0:T(8,128)S(1)}, u32[]{:S(2)}, u32[]{:S(2)}) collective-permute-start(f32[3,16,128]{2,1,0:T(8,128)S(1)} %get-tuple-element.26), channel_id=1, source_target_pairs={{0,7},{1,2},{2,1},{3,4},{4,3},{5,6},{6,5},{7,0},{8,15},{9,10},{10,... | collective-permute-start | bytes 73736 | tf_op jit(solution)/shard_map/ppermute | solution.py:457
  5.8 2.3 %tables.1 = (f32[16,128,128]{2,1,0:T(8,128)S(1)}, bf16[1024,256]{1,0:T(8,128)(2,1)S(1)}, bf16[128,1024]{1,0:T(8,128)(2,1)S(1)}, bf16[128,768]{1,0:T(8,128)(2,1)S...) custom-call(f32[16,128,128]{2,1,0:T(8,128)S(1)} %get-tuple-element.22., ...), custom_call_target="tpu_custom_call" | custom-call | flops 1000000000 | bytes 2000000 | tf_op jit(solution)/shard_map/tables/pallas_call | solution.py:460
  8.1 0.0 collective-permute-done.of_pair
  8.1 0.0 collective-permute-done.1.of_other
  8.1 0.1 corners.1
  8.2 1.6 %collective-permute-start.2 = (f32[272,128]{1,0:T(8,128)S(1)}, f32[272,128]{1,0:T(8,128)S(1)}, u32[]{:S(2)}, u32[]{:S(2)}) collective-permute-start(f32[272,128]{1,0:T(8,128)S(1)} %get-tuple-element.31), channel_id=1, source_target_pairs={{0,8},{1,9},{2,10},{3,11},{4,12},{5,13},{6,14},{7,15},{8,0},{9,1},... | collective-permute-start | bytes 417800 | tf_op jit(solution)/shard_map/ppermute | solution.py:496
  9.8 0.0 collective-permute-start.3
  9.8 8.1 %inner.1._ = f32[16,128,128]{2,1,0:T(8,128)} custom-call(f32[16,128,128]{2,1,0:T(8,128)S(1)} %get-tuple-element.24.once, f32[6,16,128]{2,1,0:T(8,128)S(1)} %get-tuple-element.23.coefs, f32[3,16,128]{2,1,0:T(8,128)S(1)} %collective-permute-done.of_pair, f32[3,16,128]{2,1,0:T(8,128)S(1)} %collective-permute-done.1.of_other, ...), custom_call_target="tpu_custom_call" | custom-call | tf_op jit(solution)/shard_map/inner/pallas_call | solution.py:504
  17.9 0.0 collective-permute-done.2.of_near
  17.9 0.0 collective-permute-done.3.of_next
  17.9 8.4 %outer.1 = f32[16,128,128]{2,1,0:T(8,128)} custom-call(f32[16,128,128]{2,1,0:T(8,128)S(1)} %get-tuple-element.24.once, f32[6,16,128]{2,1,0:T(8,128)S(1)} %get-tuple-element.23.coefs, f32[3,16,128]{2,1,0:T(8,128)S(1)} %collective-permute-done.of_pair, f32[3,16,128]{2,1,0:T(8,128)S(1)} %collective-permute-done.1.of_other, ...), custom_call_target="tpu_custom_call", output_to_operand_aliasing={{}: (15, {})} | custom-call | tf_op jit(solution)/shard_map/outer/pallas_call | solution.py:509
Async XLA Ops:
  1.7 6.4 %collective-permute-start = (f32[3,16,128]{2,1,0:T(8,128)S(1)}, f32[3,16,128]{2,1,0:T(8,128)S(1)}, u32[]{:S(2)}, u32[]{:S(2)}) collective-permute-start(f32[3,16,128]{2,1,0:T(8,128)S(1)} %get-tuple-element.25), channel_id=1, source_target_pairs={{0,1},{1,0},{2,3},{3,2},{4,5},{5,4},{6,7},{7,6},{8,9},{9,8},{10,11... | collective-permute-start | bytes 73736 | tf_op jit(solution)/shard_map/ppermute | solution.py:458
  2.2 5.9 %collective-permute-start.1 = (f32[3,16,128]{2,1,0:T(8,128)S(1)}, f32[3,16,128]{2,1,0:T(8,128)S(1)}, u32[]{:S(2)}, u32[]{:S(2)}) collective-permute-start(f32[3,16,128]{2,1,0:T(8,128)S(1)} %get-tuple-element.26), channel_id=1, source_target_pairs={{0,7},{1,2},{2,1},{3,4},{4,3},{5,6},{6,5},{7,0},{8,15},{9,10},{10,... | collective-permute-start | bytes 73736 | tf_op jit(solution)/shard_map/ppermute | solution.py:457
  8.2 9.8 %collective-permute-start.2 = (f32[272,128]{1,0:T(8,128)S(1)}, f32[272,128]{1,0:T(8,128)S(1)}, u32[]{:S(2)}, u32[]{:S(2)}) collective-permute-start(f32[272,128]{1,0:T(8,128)S(1)} %get-tuple-element.31), channel_id=1, source_target_pairs={{0,8},{1,9},{2,10},{3,11},{4,12},{5,13},{6,14},{7,15},{8,0},{9,1},... | collective-permute-start | bytes 417800 | tf_op jit(solution)/shard_map/ppermute | solution.py:496
  9.8 8.1 %collective-permute-start.3 = (f32[272,128]{1,0:T(8,128)S(1)}, f32[272,128]{1,0:T(8,128)S(1)}, u32[]{:S(2)}, u32[]{:S(2)}) collective-permute-start(f32[272,128]{1,0:T(8,128)S(1)} %get-tuple-element.32), channel_id=1, source_target_pairs={{0,1},{1,0},{2,3},{3,2},{4,5},{5,4},{6,7},{7,6},{8,16},{9,17},{10,... | collective-permute-start | bytes 417800 | tf_op jit(solution)/shard_map/ppermute | solution.py:495

commit v8 on v7

--- a/solution.py
+++ b/solution.py
@@ -347,7 +347,7 @@
 
 
 def inner_kernel(
-    once, coefs, of_pair, of_other, own,
+    once, coefs, of_other, of_pair, own,
     gather, products, losses, speeds, decay, sun, lit, out, stage, columns, sem,
 ):
     rows = once.shape[0]
@@ -358,7 +358,7 @@
 
 
 def outer_kernel(
-    once, coefs, of_pair, of_other, own, conc, of_near, of_next,
+    once, coefs, of_other, of_pair, own, conc, of_next, of_near,
     gather, products, losses, speeds, decay, sun, lit, _, out, stage, columns, sem,
 ):
     rows, species, cells = conc.shape
@@ -495,7 +495,7 @@
     of_next = lax.ppermute(to_next, ("lat", "lon"), after)
     of_near = lax.ppermute(to_near, ("lat", "lon"), near)
 
-    shared = (once, coefs, of_pair, of_other, own)
+    shared = (once, coefs, of_other, of_pair, own)
     scratch = [
         pltpu.VMEM((rows // 2, species, cells), f32),
         pltpu.VMEM((LANES, species), f32),
@@ -511,7 +511,7 @@
         in_specs=[vmem] * 15 + [hbm], out_specs=hbm, scratch_shapes=scratch,
         input_output_aliases={15: 0},
         compiler_params=params, name="outer",
-    )(*shared, held, of_near, of_next, *tables, inner)
+    )(*shared, held, of_next, of_near, *tables, inner)
 
 
 def solution(mesh):

time: 26.8 us -> 27.7 us (1.034)
  starting transfers between devices: 5.72 us -> 6.69 us
    ppermute x1, starting transfers between devices: 1.64 us -> 2.71 us  [local(): of_near = lax.ppermute(to_near, ('lat', 'lon'), near)]
    ppermute x1, starting transfers between devices: 0.01 us -> 0.57 us  [local(): of_next = lax.ppermute(to_next, ('lat', 'lon'), after)]
    ppermute x1, starting transfers between devices: 0.52 us -> 0.01 us  [local(): of_pair = lax.ppermute(to_pair, 'lon', pair)]
  transfers between devices with their start and end apart: 4 -> 4, of which waited for: 0 -> 0; matrix products, arithmetic and copies ran while one was open for 0% -> 0% of each run, Pallas kernels for 39% -> 38%
where the time goes in v8:
time: 27.7 us; the launch traced here: 27.4 us
  Pallas kernels  20.5 us (74%)
  starting transfers between devices  6.69 us (24%)
    pallas_call x1, Pallas kernels, local(): pl.pallas_call(outer_kernel, out_shape=jax.ShapeDtypeStruct(conc.shape, f...  8.39 us
    pallas_call x1, Pallas kernels, local(): pl.pallas_call(inner_kernel, out_shape=jax.ShapeDtypeStruct(conc.shape, f...  8.09 us
    ppermute x1, starting transfers between devices, local(): of_other = lax.ppermute(to_other, 'lon', other)  3.4 us
    ppermute x1, starting transfers between devices, local(): of_near = lax.ppermute(to_near, ('lat', 'lon'), near)  2.71 us
    pallas_call x1, Pallas kernels, local(): pl.pallas_call(table_kernel, out_shape=(shape(rows, species, cells), shap...  2.31 us
    pallas_call x1, Pallas kernels, local(): pl.pallas_call(edge_kernel, out_shape=(side, side, shape(2, rows, species...  1.68 us
    ppermute x1, starting transfers between devices, local(): of_next = lax.ppermute(to_next, ('lat', 'lon'), after)  0.57 us
  transfers between devices with their start and end apart: 4, of which 0 were waited for; matrix products, arithmetic and copies ran while one was open for 0% of the time, Pallas kernels for 38%

profile of v8, /device:TPU:0, one launch (start us, length us, event | category | flops | bytes accessed | tf_op | source)
XLA Modules:
  0.0 27.4 jit_solution(9011321137134269311)
XLA Ops:
  0.0 1.7 %edges.1 = (f32[3,16,128]{2,1,0:T(8,128)S(1)}, f32[3,16,128]{2,1,0:T(8,128)S(1)}, f32[2,16,128]{2,1,0:T(8,128)S(1)}, f32[272,128]{1,0:T(8,128)S(1)}, f32[272,128...) custom-call(f32[16,128,128]{2,1,0:T(8,128)} %conc_in.1, f32[16,128]{1,0:T(8,128)} %wlon_in.1, ...), custom_call_target="tpu_custom_call" | custom-call | tf_op jit(solution)/shard_map/edges/pallas_call | solution.py:433
  1.7 3.4 %collective-permute-start = (f32[3,16,128]{2,1,0:T(8,128)S(1)}, f32[3,16,128]{2,1,0:T(8,128)S(1)}, u32[]{:S(2)}, u32[]{:S(2)}) collective-permute-start(f32[3,16,128]{2,1,0:T(8,128)S(1)} %get-tuple-element.25), channel_id=1, source_target_pairs={{0,7},{1,2},{2,1},{3,4},{4,3},{5,6},{6,5},{7,0},{8,15},{9,10},{10,... | collective-permute-start | bytes 73736 | tf_op jit(solution)/shard_map/ppermute | solution.py:457
  5.1 0.0 collective-permute-start.1
  5.1 2.3 %tables.1 = (f32[16,128,128]{2,1,0:T(8,128)S(1)}, bf16[1024,256]{1,0:T(8,128)(2,1)S(1)}, bf16[128,1024]{1,0:T(8,128)(2,1)S(1)}, bf16[128,768]{1,0:T(8,128)(2,1)S...) custom-call(f32[16,128,128]{2,1,0:T(8,128)S(1)} %get-tuple-element.22., ...), custom_call_target="tpu_custom_call" | custom-call | flops 1000000000 | bytes 2000000 | tf_op jit(solution)/shard_map/tables/pallas_call | solution.py:460
  7.4 0.0 collective-permute-done.of_other
  7.4 0.0 collective-permute-done.1.of_pair
  7.4 0.1 corners.1
  7.5 0.6 %collective-permute-start.2 = (f32[272,128]{1,0:T(8,128)S(1)}, f32[272,128]{1,0:T(8,128)S(1)}, u32[]{:S(2)}, u32[]{:S(2)}) collective-permute-start(f32[272,128]{1,0:T(8,128)S(1)} %get-tuple-element.31), channel_id=1, source_target_pairs={{0,1},{1,0},{2,3},{3,2},{4,5},{5,4},{6,7},{7,6},{8,16},{9,17},{10,... | collective-permute-start | bytes 417800 | tf_op jit(solution)/shard_map/ppermute | solution.py:495
  8.1 2.7 %collective-permute-start.3 = (f32[272,128]{1,0:T(8,128)S(1)}, f32[272,128]{1,0:T(8,128)S(1)}, u32[]{:S(2)}, u32[]{:S(2)}) collective-permute-start(f32[272,128]{1,0:T(8,128)S(1)} %get-tuple-element.32), channel_id=1, source_target_pairs={{0,8},{1,9},{2,10},{3,11},{4,12},{5,13},{6,14},{7,15},{8,0},{9,1},... | collective-permute-start | bytes 417800 | tf_op jit(solution)/shard_map/ppermute | solution.py:496
  10.8 8.1 %inner.1._ = f32[16,128,128]{2,1,0:T(8,128)} custom-call(f32[16,128,128]{2,1,0:T(8,128)S(1)} %get-tuple-element.24.once, f32[6,16,128]{2,1,0:T(8,128)S(1)} %get-tuple-element.23.coefs, f32[3,16,128]{2,1,0:T(8,128)S(1)} %collective-permute-done.of_other, f32[3,16,128]{2,1,0:T(8,128)S(1)} %collective-permute-done.1.of_pair, ...), custom_call_target="tpu_custom_call" | custom-call | tf_op jit(solution)/shard_map/inner/pallas_call | solution.py:504
  18.9 0.0 collective-permute-done.2.of_next
  18.9 0.0 collective-permute-done.3.of_near
  18.9 8.4 %outer.1 = f32[16,128,128]{2,1,0:T(8,128)} custom-call(f32[16,128,128]{2,1,0:T(8,128)S(1)} %get-tuple-element.24.once, f32[6,16,128]{2,1,0:T(8,128)S(1)} %get-tuple-element.23.coefs, f32[3,16,128]{2,1,0:T(8,128)S(1)} %collective-permute-done.of_other, f32[3,16,128]{2,1,0:T(8,128)S(1)} %collective-permute-done.1.of_pair, ...), custom_call_target="tpu_custom_call", output_to_operand_aliasing={{}: (15, {})} | custom-call | tf_op jit(solution)/shard_map/outer/pallas_call | solution.py:509
Async XLA Ops:
  1.7 5.7 %collective-permute-start = (f32[3,16,128]{2,1,0:T(8,128)S(1)}, f32[3,16,128]{2,1,0:T(8,128)S(1)}, u32[]{:S(2)}, u32[]{:S(2)}) collective-permute-start(f32[3,16,128]{2,1,0:T(8,128)S(1)} %get-tuple-element.25), channel_id=1, source_target_pairs={{0,7},{1,2},{2,1},{3,4},{4,3},{5,6},{6,5},{7,0},{8,15},{9,10},{10,... | collective-permute-start | bytes 73736 | tf_op jit(solution)/shard_map/ppermute | solution.py:457
  5.1 2.3 %collective-permute-start.1 = (f32[3,16,128]{2,1,0:T(8,128)S(1)}, f32[3,16,128]{2,1,0:T(8,128)S(1)}, u32[]{:S(2)}, u32[]{:S(2)}) collective-permute-start(f32[3,16,128]{2,1,0:T(8,128)S(1)} %get-tuple-element.26), channel_id=1, source_target_pairs={{0,1},{1,0},{2,3},{3,2},{4,5},{5,4},{6,7},{7,6},{8,9},{9,8},{10,11... | collective-permute-start | bytes 73736 | tf_op jit(solution)/shard_map/ppermute | solution.py:458
  7.5 11.4 %collective-permute-start.2 = (f32[272,128]{1,0:T(8,128)S(1)}, f32[272,128]{1,0:T(8,128)S(1)}, u32[]{:S(2)}, u32[]{:S(2)}) collective-permute-start(f32[272,128]{1,0:T(8,128)S(1)} %get-tuple-element.31), channel_id=1, source_target_pairs={{0,1},{1,0},{2,3},{3,2},{4,5},{5,4},{6,7},{7,6},{8,16},{9,17},{10,... | collective-permute-start | bytes 417800 | tf_op jit(solution)/shard_map/ppermute | solution.py:495
  8.1 10.8 %collective-permute-start.3 = (f32[272,128]{1,0:T(8,128)S(1)}, f32[272,128]{1,0:T(8,128)S(1)}, u32[]{:S(2)}, u32[]{:S(2)}) collective-permute-start(f32[272,128]{1,0:T(8,128)S(1)} %get-tuple-element.32), channel_id=1, source_target_pairs={{0,8},{1,9},{2,10},{3,11},{4,12},{5,13},{6,14},{7,15},{8,0},{9,1},... | collective-permute-start | bytes 417800 | tf_op jit(solution)/shard_map/ppermute | solution.py:496

commit v9 on v8

--- a/solution.py
+++ b/solution.py
@@ -358,7 +358,7 @@
 
 
 def outer_kernel(
-    once, coefs, of_other, of_pair, own, conc, of_next, of_near,
+    once, coefs, of_other, of_pair, own, conc, of_near, of_next,
     gather, products, losses, speeds, decay, sun, lit, _, out, stage, columns, sem,
 ):
     rows, species, cells = conc.shape
@@ -511,7 +511,7 @@
         in_specs=[vmem] * 15 + [hbm], out_specs=hbm, scratch_shapes=scratch,
         input_output_aliases={15: 0},
         compiler_params=params, name="outer",
-    )(*shared, held, of_next, of_near, *tables, inner)
+    )(*shared, held, of_near, of_next, *tables, inner)
 
 
 def solution(mesh):

time: 27.7 us -> 26.3 us (0.949)
  starting transfers between devices: 6.69 us -> 5.27 us
    ppermute x1, starting transfers between devices: 2.71 us -> 1.71 us  [local(): of_near = lax.ppermute(to_near, ('lat', 'lon'), near)]
    ppermute x1, starting transfers between devices: 0.57 us -> 0.16 us  [local(): of_next = lax.ppermute(to_next, ('lat', 'lon'), after)]
  transfers between devices with their start and end apart: 4 -> 4, of which waited for: 0 -> 0; matrix products, arithmetic and copies ran while one was open for 0% -> 0% of each run, Pallas kernels for 38% -> 40%
where the time goes in v9:
time: 26.3 us; the launch traced here: 26 us
  Pallas kernels  20.5 us (78%)
  starting transfers between devices  5.27 us (20%)
    pallas_call x1, Pallas kernels, local(): pl.pallas_call(outer_kernel, out_shape=jax.ShapeDtypeStruct(conc.shape, f...  8.39 us
    pallas_call x1, Pallas kernels, local(): pl.pallas_call(inner_kernel, out_shape=jax.ShapeDtypeStruct(conc.shape, f...  8.09 us
    ppermute x1, starting transfers between devices, local(): of_other = lax.ppermute(to_other, 'lon', other)  3.4 us
    pallas_call x1, Pallas kernels, local(): pl.pallas_call(table_kernel, out_shape=(shape(rows, species, cells), shap...  2.31 us
    ppermute x1, starting transfers between devices, local(): of_near = lax.ppermute(to_near, ('lat', 'lon'), near)  1.71 us
    pallas_call x1, Pallas kernels, local(): pl.pallas_call(edge_kernel, out_shape=(side, side, shape(2, rows, species...  1.68 us
  transfers between devices with their start and end apart: 4, of which 0 were waited for; matrix products, arithmetic and copies ran while one was open for 0% of the time, Pallas kernels for 40%

profile of v9, /device:TPU:0, one launch (start us, length us, event | category | flops | bytes accessed | tf_op | source)
XLA Modules:
  0.0 26.0 jit_solution(10683260214925410885)
XLA Ops:
  0.0 1.7 %edges.1 = (f32[3,16,128]{2,1,0:T(8,128)S(1)}, f32[3,16,128]{2,1,0:T(8,128)S(1)}, f32[2,16,128]{2,1,0:T(8,128)S(1)}, f32[272,128]{1,0:T(8,128)S(1)}, f32[272,128...) custom-call(f32[16,128,128]{2,1,0:T(8,128)} %conc_in.1, f32[16,128]{1,0:T(8,128)} %wlon_in.1, ...), custom_call_target="tpu_custom_call" | custom-call | tf_op jit(solution)/shard_map/edges/pallas_call | solution.py:433
  1.7 3.4 %collective-permute-start = (f32[3,16,128]{2,1,0:T(8,128)S(1)}, f32[3,16,128]{2,1,0:T(8,128)S(1)}, u32[]{:S(2)}, u32[]{:S(2)}) collective-permute-start(f32[3,16,128]{2,1,0:T(8,128)S(1)} %get-tuple-element.25), channel_id=1, source_target_pairs={{0,7},{1,2},{2,1},{3,4},{4,3},{5,6},{6,5},{7,0},{8,15},{9,10},{10,... | collective-permute-start | bytes 73736 | tf_op jit(solution)/shard_map/ppermute | solution.py:457
  5.1 0.0 collective-permute-start.1
  5.1 2.3 %tables.1 = (f32[16,128,128]{2,1,0:T(8,128)S(1)}, bf16[1024,256]{1,0:T(8,128)(2,1)S(1)}, bf16[128,1024]{1,0:T(8,128)(2,1)S(1)}, bf16[128,768]{1,0:T(8,128)(2,1)S...) custom-call(f32[16,128,128]{2,1,0:T(8,128)S(1)} %get-tuple-element.22., ...), custom_call_target="tpu_custom_call" | custom-call | flops 1000000000 | bytes 2000000 | tf_op jit(solution)/shard_map/tables/pallas_call | solution.py:460
  7.4 0.0 collective-permute-done.of_other
  7.4 0.0 collective-permute-done.1.of_pair
  7.4 0.1 corners.1
  7.5 1.7 %collective-permute-start.2 = (f32[272,128]{1,0:T(8,128)S(1)}, f32[272,128]{1,0:T(8,128)S(1)}, u32[]{:S(2)}, u32[]{:S(2)}) collective-permute-start(f32[272,128]{1,0:T(8,128)S(1)} %get-tuple-element.31), channel_id=1, source_target_pairs={{0,8},{1,9},{2,10},{3,11},{4,12},{5,13},{6,14},{7,15},{8,0},{9,1},... | collective-permute-start | bytes 417800 | tf_op jit(solution)/shard_map/ppermute | solution.py:496
  9.2 0.2 collective-permute-start.3
  9.4 8.1 %inner.1._ = f32[16,128,128]{2,1,0:T(8,128)} custom-call(f32[16,128,128]{2,1,0:T(8,128)S(1)} %get-tuple-element.24.once, f32[6,16,128]{2,1,0:T(8,128)S(1)} %get-tuple-element.23.coefs, f32[3,16,128]{2,1,0:T(8,128)S(1)} %collective-permute-done.of_other, f32[3,16,128]{2,1,0:T(8,128)S(1)} %collective-permute-done.1.of_pair, ...), custom_call_target="tpu_custom_call" | custom-call | tf_op jit(solution)/shard_map/inner/pallas_call | solution.py:504
  17.5 0.0 collective-permute-done.2.of_near
  17.5 0.0 collective-permute-done.3.of_next
  17.5 8.4 %outer.1 = f32[16,128,128]{2,1,0:T(8,128)} custom-call(f32[16,128,128]{2,1,0:T(8,128)S(1)} %get-tuple-element.24.once, f32[6,16,128]{2,1,0:T(8,128)S(1)} %get-tuple-element.23.coefs, f32[3,16,128]{2,1,0:T(8,128)S(1)} %collective-permute-done.of_other, f32[3,16,128]{2,1,0:T(8,128)S(1)} %collective-permute-done.1.of_pair, ...), custom_call_target="tpu_custom_call", output_to_operand_aliasing={{}: (15, {})} | custom-call | tf_op jit(solution)/shard_map/outer/pallas_call | solution.py:509
Async XLA Ops:
  1.7 5.7 %collective-permute-start = (f32[3,16,128]{2,1,0:T(8,128)S(1)}, f32[3,16,128]{2,1,0:T(8,128)S(1)}, u32[]{:S(2)}, u32[]{:S(2)}) collective-permute-start(f32[3,16,128]{2,1,0:T(8,128)S(1)} %get-tuple-element.25), channel_id=1, source_target_pairs={{0,7},{1,2},{2,1},{3,4},{4,3},{5,6},{6,5},{7,0},{8,15},{9,10},{10,... | collective-permute-start | bytes 73736 | tf_op jit(solution)/shard_map/ppermute | solution.py:457
  5.1 2.3 %collective-permute-start.1 = (f32[3,16,128]{2,1,0:T(8,128)S(1)}, f32[3,16,128]{2,1,0:T(8,128)S(1)}, u32[]{:S(2)}, u32[]{:S(2)}) collective-permute-start(f32[3,16,128]{2,1,0:T(8,128)S(1)} %get-tuple-element.26), channel_id=1, source_target_pairs={{0,1},{1,0},{2,3},{3,2},{4,5},{5,4},{6,7},{7,6},{8,9},{9,8},{10,11... | collective-permute-start | bytes 73736 | tf_op jit(solution)/shard_map/ppermute | solution.py:458
  7.5 10.0 %collective-permute-start.2 = (f32[272,128]{1,0:T(8,128)S(1)}, f32[272,128]{1,0:T(8,128)S(1)}, u32[]{:S(2)}, u32[]{:S(2)}) collective-permute-start(f32[272,128]{1,0:T(8,128)S(1)} %get-tuple-element.31), channel_id=1, source_target_pairs={{0,8},{1,9},{2,10},{3,11},{4,12},{5,13},{6,14},{7,15},{8,0},{9,1},... | collective-permute-start | bytes 417800 | tf_op jit(solution)/shard_map/ppermute | solution.py:496
  9.2 8.3 %collective-permute-start.3 = (f32[272,128]{1,0:T(8,128)S(1)}, f32[272,128]{1,0:T(8,128)S(1)}, u32[]{:S(2)}, u32[]{:S(2)}) collective-permute-start(f32[272,128]{1,0:T(8,128)S(1)} %get-tuple-element.32), channel_id=1, source_target_pairs={{0,1},{1,0},{2,3},{3,2},{4,5},{5,4},{6,7},{7,6},{8,16},{9,17},{10,... | collective-permute-start | bytes 417800 | tf_op jit(solution)/shard_map/ppermute | solution.py:495

commit v10 on v9

--- a/solution.py
+++ b/solution.py
@@ -36,8 +36,9 @@
 
 
 def edge_kernel(
-    conc_in, wlon_in, wlat_in, mix_in, to_other, to_pair, own, to_next, to_near, conc, coefs,
-    winds, columns, sem,
+    conc_in, wlon_in, wlat_in, mix_in, stoich_in, rate_in, plan_in, night_in, sun,
+    to_other, to_pair, own, to_next, to_near, conc, coefs,
+    stoich, rate, plan, night, sun_own, winds, columns, sem,
 ):
     rows, species, cells = conc.shape
     fetches = [
@@ -51,6 +52,14 @@
         )
         for q in range(4)
     ]
+    here = sun.at[
+        pl.ds(pl.multiple_of(lax.axis_index("lat") * rows, 8), rows),
+        pl.ds(pl.multiple_of(lax.axis_index("lon") * cells, LANES), cells),
+    ]
+    small = (
+        (stoich_in, stoich), (rate_in, rate), (plan_in, plan), (night_in, night), (here, sun_own)
+    )
+    fetches += [pltpu.make_async_copy(a, b, sem.at[7 + k]) for k, (a, b) in enumerate(small)]
     for fetch in fetches:
         fetch.start()
     for fetch in fetches[:3]:
@@ -106,6 +115,8 @@
     own[1] = last1
     for q in range(2):
         send(slice(q * species, (q + 1) * species), conc[rows - 2 + q], conc[q])
+    for fetch in fetches[7:]:
+        fetch.wait()
 
 
 def sides(of_pair, of_other):
@@ -137,25 +148,15 @@
 
 
 def table_kernel(
-    conc, coefs, stoich_in, rate_in, plan_in, night_in, sun, once, gather, products, losses, speeds, decay, sun_own, lit,
-    stoich, rate, plan, night, turned, sem,
+    conc, coefs, stoich, rate, plan, night, once, gather, products, losses, speeds, decay, lit,
+    turned,
 ):
     species = decay.shape[0]
-    reactions = stoich_in.shape[1]
-    rows = sun_own.shape[0]
+    reactions = stoich.shape[1]
+    rows = conc.shape[0]
     chunks = reactions // LANES
     band = lax.axis_index("lat")
     sector = lax.axis_index("lon")
-    here = sun.at[
-        pl.ds(pl.multiple_of(band * rows, 8), rows),
-        pl.ds(pl.multiple_of(sector * LANES, LANES), LANES),
-    ]
-    moves = (
-        (here, sun_own), (stoich_in, stoich), (rate_in, rate), (plan_in, plan), (night_in, night)
-    )
-    fetches = [pltpu.make_async_copy(a, b, sem.at[k]) for k, (a, b) in enumerate(moves)]
-    for fetch in fetches:
-        fetch.start()
     for g in range(rows):
         row = inner_step(conc[g], coefs, g)
         if g > 0:
@@ -163,8 +164,6 @@
         if g < rows - 1:
             row = row + coefs[4, g : g + 1, :] * conc[g + 1]
         once[g] = row
-    for fetch in fetches:
-        fetch.wait()
     down = iota((species, LANES), 0)
     across = iota((LANES, species), 1).astype(f32)
     mats = []
@@ -430,20 +429,31 @@
 
     side = shape(3, rows, species)
     ends = shape(2 * species + 16, cells)
-    to_other, to_pair, own, to_next, to_near, held, coefs = pl.pallas_call(
+    to_other, to_pair, own, to_next, to_near, held, coefs, *small, sun_own = pl.pallas_call(
         edge_kernel,
         out_shape=(
             side, side, shape(2, rows, species), ends, ends,
             shape(rows, species, cells), shape(6, rows, cells),
+            shape(*stoich.shape, dtype=jnp.int32), shape(1, reactions),
+            shape(plan.shape[0], plan.shape[2], plan.shape[1], dtype=jnp.int32),
+            shape(1, species), shape(rows, cells),
         ),
-        in_specs=[far] * 4, out_specs=[vmem] * 7,
+        in_specs=[far] * 9, out_specs=[vmem] * 12,
         scratch_shapes=[
             pltpu.VMEM((3, rows, cells), f32),
             pltpu.VMEM((cells, species), f32),
-            pltpu.SemaphoreType.DMA((7,)),
+            pltpu.SemaphoreType.DMA((12,)),
         ],
         compiler_params=params, name="edges",
-    )(*[pinned(x) for x in (conc, wind_lon, wind_lat, mixing)])
+    )(
+        *[
+            pinned(x)
+            for x in (
+                conc, wind_lon, wind_lat, mixing, stoich, rate.reshape(1, reactions),
+                jnp.swapaxes(plan, 1, 2), night_loss.reshape(1, species), sun,
+            )
+        ]
+    )
 
     pair = [(i, i ^ 1) for i in range(lons)]
     other = [(i, (i - 1) % lons if i % 2 == 0 else (i + 1) % lons) for i in range(lons)]
@@ -466,23 +476,16 @@
             shape(species, 6 * species, dtype=bf16),
             shape(reactions, LANES),
             shape(species, LANES),
-            shape(rows, LANES),
             shape(SUBSTEPS, rows, LANES),
         ),
-        in_specs=[vmem] * 2 + [far] * 5, out_specs=[vmem] * 8,
+        in_specs=[vmem] * 6, out_specs=[vmem] * 7,
         scratch_shapes=[
-            pltpu.VMEM(stoich.shape, jnp.int32),
-            pltpu.VMEM((1, reactions), f32),
-            pltpu.VMEM((plan.shape[0], plan.shape[2], plan.shape[1]), jnp.int32),
-            pltpu.VMEM((1, species), f32),
             pltpu.VMEM((LANES, LANES), f32),
-            pltpu.SemaphoreType.DMA((5,)),
         ],
         cost_estimate=pl.CostEstimate(flops=10**9, transcendentals=0, bytes_accessed=2 * 10**6),
         compiler_params=params, name="tables",
     )(
-        held, coefs, pinned(stoich), pinned(rate.reshape(1, reactions)),
-        pinned(jnp.swapaxes(plan, 1, 2)), pinned(night_loss.reshape(1, species)), pinned(sun),
+        held, coefs, *small,
     )
 
     to_next, to_near = pl.pallas_call(
@@ -491,10 +494,11 @@
         scratch_shapes=[pltpu.VMEM((2, 8, species), f32), pltpu.SemaphoreType.DMA((2,))],
         input_output_aliases={2: 0, 3: 1},
         compiler_params=params, name="corners",
-    )(of_other, of_pair, to_next, to_near, tables[5])
+    )(of_other, of_pair, to_next, to_near, tables[-1])
     of_next = lax.ppermute(to_next, ("lat", "lon"), after)
     of_near = lax.ppermute(to_near, ("lat", "lon"), near)
 
+    tables.insert(5, sun_own)
     shared = (once, coefs, of_other, of_pair, own)
     scratch = [
         pltpu.VMEM((rows // 2, species, cells), f32),

time: 26.3 us -> 28.6 us (1.087)
  Pallas kernels: 20.5 us -> 22 us
  starting transfers between devices: 5.27 us -> 5.95 us
    pallas_call x1, Pallas kernels: 8.09 us -> 9.26 us  [local(): pl.pallas_call(inner_kernel, out_shape=jax.ShapeDtypeStruct(conc.shape, f...]
    pallas_call x1, Pallas kernels: 8.39 us -> 9.56 us  [local(): pl.pallas_call(outer_kernel, out_shape=jax.ShapeDtypeStruct(conc.shape, f...]
    pallas_call x1, Pallas kernels: 2.31 us -> 1.39 us  [local(): pl.pallas_call(table_kernel, out_shape=(shape(rows, species, cells), shap...]
    ppermute x1, starting transfers between devices: 1.71 us -> 2.54 us  [local(): of_near = lax.ppermute(to_near, ('lat', 'lon'), near)]
  transfers between devices with their start and end apart: 4 -> 4, of which waited for: 0 -> 1; matrix products, arithmetic and copies ran while one was open for 0% -> 0% of each run, Pallas kernels for 40% -> 38%
where the time goes in v10:
time: 28.6 us; the launch traced here: 28.3 us
  Pallas kernels  22 us (77%)
  starting transfers between devices  5.95 us (21%)
    pallas_call x1, Pallas kernels, local(): pl.pallas_call(outer_kernel, out_shape=jax.ShapeDtypeStruct(conc.shape, f...  9.56 us
    pallas_call x1, Pallas kernels, local(): pl.pallas_call(inner_kernel, out_shape=jax.ShapeDtypeStruct(conc.shape, f...  9.26 us
    ppermute x1, starting transfers between devices, local(): of_other = lax.ppermute(to_other, 'lon', other)  3.4 us
    ppermute x1, starting transfers between devices, local(): of_near = lax.ppermute(to_near, ('lat', 'lon'), near)  2.54 us
    pallas_call x1, Pallas kernels, local(): pl.pallas_call(edge_kernel, out_shape=(side, side, shape(2, rows, species...  1.74 us
    pallas_call x1, Pallas kernels, local(): pl.pallas_call(table_kernel, out_shape=(shape(rows, species, cells), shap...  1.39 us
  transfers between devices with their start and end apart: 4, of which 1 were waited for; matrix products, arithmetic and copies ran while one was open for 0% of the time, Pallas kernels for 38%

profile of v10, /device:TPU:0, one launch (start us, length us, event | category | flops | bytes accessed | tf_op | source)
XLA Modules:
  0.0 28.3 jit_solution(17584426162673898240)
XLA Ops:
  0.0 1.7 %edges.1 = (f32[3,16,128]{2,1,0:T(8,128)S(1)}, f32[3,16,128]{2,1,0:T(8,128)S(1)}, f32[2,16,128]{2,1,0:T(8,128)S(1)}, f32[272,128]{1,0:T(8,128)S(1)}, f32[272,128...) custom-call(f32[16,128,128]{2,1,0:T(8,128)} %conc_in.1, ...), custom_call_target="tpu_custom_call" | custom-call | tf_op jit(solution)/shard_map/edges/pallas_call | solution.py:432
  1.7 3.4 %collective-permute-start = (f32[3,16,128]{2,1,0:T(8,128)S(1)}, f32[3,16,128]{2,1,0:T(8,128)S(1)}, u32[]{:S(2)}, u32[]{:S(2)}) collective-permute-start(f32[3,16,128]{2,1,0:T(8,128)S(1)} %get-tuple-element.33), channel_id=1, source_target_pairs={{0,7},{1,2},{2,1},{3,4},{4,3},{5,6},{6,5},{7,0},{8,15},{9,10},{10,... | collective-permute-start | bytes 73736 | tf_op jit(solution)/shard_map/ppermute | solution.py:467
  5.1 0.0 collective-permute-start.1
  5.1 1.4 %tables.1 = (f32[16,128,128]{2,1,0:T(8,128)S(1)}, bf16[1024,256]{1,0:T(8,128)(2,1)S(1)}, bf16[128,1024]{1,0:T(8,128)(2,1)S(1)}, bf16[128,768]{1,0:T(8,128)(2,1)S...) custom-call(f32[16,128,128]{2,1,0:T(8,128)S(1)} %get-tuple-element.26.conc, ...), custom_call_target="tpu_custom_call" | custom-call | flops 1000000000 | bytes 2000000 | tf_op jit(solution)/shard_map/tables/pallas_call | solution.py:470
  6.5 0.1 collective-permute-done.of_other
  6.7 0.0 collective-permute-done.1.of_pair
  6.7 2.5 %collective-permute-start.2 = (f32[272,128]{1,0:T(8,128)S(1)}, f32[272,128]{1,0:T(8,128)S(1)}, u32[]{:S(2)}, u32[]{:S(2)}) collective-permute-start(f32[272,128]{1,0:T(8,128)S(1)} %get-tuple-element.39), channel_id=1, source_target_pairs={{0,8},{1,9},{2,10},{3,11},{4,12},{5,13},{6,14},{7,15},{8,0},{9,1},... | collective-permute-start | bytes 417800 | tf_op jit(solution)/shard_map/ppermute | solution.py:499
  9.3 0.0 collective-permute-start.3
  9.3 9.3 %inner.1._ = f32[16,128,128]{2,1,0:T(8,128)} custom-call(f32[16,128,128]{2,1,0:T(8,128)S(1)} %get-tuple-element.32.once, f32[6,16,128]{2,1,0:T(8,128)S(1)} %get-tuple-element.27.coefs, f32[3,16,128]{2,1,0:T(8,128)S(1)} %collective-permute-done.of_other, f32[3,16,128]{2,1,0:T(8,128)S(1)} %collective-permute-done.1.of_pair, ...), custom_call_target="tpu_custom_call" | custom-call | tf_op jit(solution)/shard_map/inner/pallas_call | solution.py:508
  18.5 0.0 collective-permute-done.2.of_near
  18.5 0.0 collective-permute-done.3.of_next
  18.6 9.6 %outer.1 = f32[16,128,128]{2,1,0:T(8,128)} custom-call(f32[16,128,128]{2,1,0:T(8,128)S(1)} %get-tuple-element.32.once, f32[6,16,128]{2,1,0:T(8,128)S(1)} %get-tuple-element.27.coefs, f32[3,16,128]{2,1,0:T(8,128)S(1)} %collective-permute-done.of_other, f32[3,16,128]{2,1,0:T(8,128)S(1)} %collective-permute-done.1.of_pair, ...), custom_call_target="tpu_custom_call", output_to_operand_aliasing={{}: (15, {})} | custom-call | tf_op jit(solution)/shard_map/outer/pallas_call | solution.py:513
  (1 shorter events, 0.0 us)
Async XLA Ops:
  1.7 4.9 %collective-permute-start = (f32[3,16,128]{2,1,0:T(8,128)S(1)}, f32[3,16,128]{2,1,0:T(8,128)S(1)}, u32[]{:S(2)}, u32[]{:S(2)}) collective-permute-start(f32[3,16,128]{2,1,0:T(8,128)S(1)} %get-tuple-element.33), channel_id=1, source_target_pairs={{0,7},{1,2},{2,1},{3,4},{4,3},{5,6},{6,5},{7,0},{8,15},{9,10},{10,... | collective-permute-start | bytes 73736 | tf_op jit(solution)/shard_map/ppermute | solution.py:467
  5.1 1.5 %collective-permute-start.1 = (f32[3,16,128]{2,1,0:T(8,128)S(1)}, f32[3,16,128]{2,1,0:T(8,128)S(1)}, u32[]{:S(2)}, u32[]{:S(2)}) collective-permute-start(f32[3,16,128]{2,1,0:T(8,128)S(1)} %get-tuple-element.34), channel_id=1, source_target_pairs={{0,1},{1,0},{2,3},{3,2},{4,5},{5,4},{6,7},{7,6},{8,9},{9,8},{10,11... | collective-permute-start | bytes 73736 | tf_op jit(solution)/shard_map/ppermute | solution.py:468
  6.7 11.8 %collective-permute-start.2 = (f32[272,128]{1,0:T(8,128)S(1)}, f32[272,128]{1,0:T(8,128)S(1)}, u32[]{:S(2)}, u32[]{:S(2)}) collective-permute-start(f32[272,128]{1,0:T(8,128)S(1)} %get-tuple-element.39), channel_id=1, source_target_pairs={{0,8},{1,9},{2,10},{3,11},{4,12},{5,13},{6,14},{7,15},{8,0},{9,1},... | collective-permute-start | bytes 417800 | tf_op jit(solution)/shard_map/ppermute | solution.py:499
  9.3 9.3 %collective-permute-start.3 = (f32[272,128]{1,0:T(8,128)S(1)}, f32[272,128]{1,0:T(8,128)S(1)}, u32[]{:S(2)}, u32[]{:S(2)}) collective-permute-start(f32[272,128]{1,0:T(8,128)S(1)} %get-tuple-element.40), channel_id=1, source_target_pairs={{0,1},{1,0},{2,3},{3,2},{4,5},{5,4},{6,7},{7,6},{8,16},{9,17},{10,... | collective-permute-start | bytes 417800 | tf_op jit(solution)/shard_map/ppermute | solution.py:498

commit v11 on v9

--- a/solution.py
+++ b/solution.py
@@ -11,8 +11,8 @@
 LANES = 128
 VMEM_LIMIT = 48 << 20
 KEPT = jax.ShapeDtypeStruct
-CHUNK = 256
-STAGGER = 2
+CHUNK = 512
+STAGGER = 1
 
 f32 = jnp.float32
 bf16 = jnp.bfloat16

time: 26.3 us -> 26.3 us (level)
  no operation moved by 1% of the time
where the time goes in v11:
time: 26.3 us; the launch traced here: 26.1 us
  Pallas kernels  20.6 us (78%)
  starting transfers between devices  5.27 us (20%)
    pallas_call x1, Pallas kernels, local(): pl.pallas_call(outer_kernel, out_shape=jax.ShapeDtypeStruct(conc.shape, f...  8.4 us
    pallas_call x1, Pallas kernels, local(): pl.pallas_call(inner_kernel, out_shape=jax.ShapeDtypeStruct(conc.shape, f...  8.1 us
    ppermute x1, starting transfers between devices, local(): of_other = lax.ppermute(to_other, 'lon', other)  3.4 us
    pallas_call x1, Pallas kernels, local(): pl.pallas_call(table_kernel, out_shape=(shape(rows, species, cells), shap...  2.31 us
    ppermute x1, starting transfers between devices, local(): of_near = lax.ppermute(to_near, ('lat', 'lon'), near)  1.71 us
    pallas_call x1, Pallas kernels, local(): pl.pallas_call(edge_kernel, out_shape=(side, side, shape(2, rows, species...  1.68 us
  transfers between devices with their start and end apart: 4, of which 0 were waited for; matrix products, arithmetic and copies ran while one was open for 0% of the time, Pallas kernels for 40%

profile of v11, /device:TPU:0, one launch (start us, length us, event | category | flops | bytes accessed | tf_op | source)
XLA Modules:
  0.0 26.1 jit_solution(2607688525703642325)
XLA Ops:
  0.0 1.7 %edges.1 = (f32[3,16,128]{2,1,0:T(8,128)S(1)}, f32[3,16,128]{2,1,0:T(8,128)S(1)}, f32[2,16,128]{2,1,0:T(8,128)S(1)}, f32[272,128]{1,0:T(8,128)S(1)}, f32[272,128...) custom-call(f32[16,128,128]{2,1,0:T(8,128)} %conc_in.1, f32[16,128]{1,0:T(8,128)} %wlon_in.1, ...), custom_call_target="tpu_custom_call" | custom-call | tf_op jit(solution)/shard_map/edges/pallas_call | solution.py:433
  1.7 3.4 %collective-permute-start = (f32[3,16,128]{2,1,0:T(8,128)S(1)}, f32[3,16,128]{2,1,0:T(8,128)S(1)}, u32[]{:S(2)}, u32[]{:S(2)}) collective-permute-start(f32[3,16,128]{2,1,0:T(8,128)S(1)} %get-tuple-element.25), channel_id=1, source_target_pairs={{0,7},{1,2},{2,1},{3,4},{4,3},{5,6},{6,5},{7,0},{8,15},{9,10},{10,... | collective-permute-start | bytes 73736 | tf_op jit(solution)/shard_map/ppermute | solution.py:457
  5.1 0.0 collective-permute-start.1
  5.1 2.3 %tables.1 = (f32[16,128,128]{2,1,0:T(8,128)S(1)}, bf16[1024,256]{1,0:T(8,128)(2,1)S(1)}, bf16[128,1024]{1,0:T(8,128)(2,1)S(1)}, bf16[128,768]{1,0:T(8,128)(2,1)S...) custom-call(f32[16,128,128]{2,1,0:T(8,128)S(1)} %get-tuple-element.22., ...), custom_call_target="tpu_custom_call" | custom-call | flops 1000000000 | bytes 2000000 | tf_op jit(solution)/shard_map/tables/pallas_call | solution.py:460
  7.4 0.0 collective-permute-done.of_other
  7.4 0.0 collective-permute-done.1.of_pair
  7.4 0.1 corners.1
  7.5 1.7 %collective-permute-start.2 = (f32[272,128]{1,0:T(8,128)S(1)}, f32[272,128]{1,0:T(8,128)S(1)}, u32[]{:S(2)}, u32[]{:S(2)}) collective-permute-start(f32[272,128]{1,0:T(8,128)S(1)} %get-tuple-element.31), channel_id=1, source_target_pairs={{0,8},{1,9},{2,10},{3,11},{4,12},{5,13},{6,14},{7,15},{8,0},{9,1},... | collective-permute-start | bytes 417800 | tf_op jit(solution)/shard_map/ppermute | solution.py:496
  9.2 0.2 collective-permute-start.3
  9.4 8.1 %inner.1._ = f32[16,128,128]{2,1,0:T(8,128)} custom-call(f32[16,128,128]{2,1,0:T(8,128)S(1)} %get-tuple-element.24.once, f32[6,16,128]{2,1,0:T(8,128)S(1)} %get-tuple-element.23.coefs, f32[3,16,128]{2,1,0:T(8,128)S(1)} %collective-permute-done.of_other, f32[3,16,128]{2,1,0:T(8,128)S(1)} %collective-permute-done.1.of_pair, ...), custom_call_target="tpu_custom_call" | custom-call | tf_op jit(solution)/shard_map/inner/pallas_call | solution.py:504
  17.5 0.0 collective-permute-done.2.of_near
  17.5 0.0 collective-permute-done.3.of_next
  17.5 8.4 %outer.1 = f32[16,128,128]{2,1,0:T(8,128)} custom-call(f32[16,128,128]{2,1,0:T(8,128)S(1)} %get-tuple-element.24.once, f32[6,16,128]{2,1,0:T(8,128)S(1)} %get-tuple-element.23.coefs, f32[3,16,128]{2,1,0:T(8,128)S(1)} %collective-permute-done.of_other, f32[3,16,128]{2,1,0:T(8,128)S(1)} %collective-permute-done.1.of_pair, ...), custom_call_target="tpu_custom_call", output_to_operand_aliasing={{}: (15, {})} | custom-call | tf_op jit(solution)/shard_map/outer/pallas_call | solution.py:509
Async XLA Ops:
  1.7 5.7 %collective-permute-start = (f32[3,16,128]{2,1,0:T(8,128)S(1)}, f32[3,16,128]{2,1,0:T(8,128)S(1)}, u32[]{:S(2)}, u32[]{:S(2)}) collective-permute-start(f32[3,16,128]{2,1,0:T(8,128)S(1)} %get-tuple-element.25), channel_id=1, source_target_pairs={{0,7},{1,2},{2,1},{3,4},{4,3},{5,6},{6,5},{7,0},{8,15},{9,10},{10,... | collective-permute-start | bytes 73736 | tf_op jit(solution)/shard_map/ppermute | solution.py:457
  5.1 2.3 %collective-permute-start.1 = (f32[3,16,128]{2,1,0:T(8,128)S(1)}, f32[3,16,128]{2,1,0:T(8,128)S(1)}, u32[]{:S(2)}, u32[]{:S(2)}) collective-permute-start(f32[3,16,128]{2,1,0:T(8,128)S(1)} %get-tuple-element.26), channel_id=1, source_target_pairs={{0,1},{1,0},{2,3},{3,2},{4,5},{5,4},{6,7},{7,6},{8,9},{9,8},{10,11... | collective-permute-start | bytes 73736 | tf_op jit(solution)/shard_map/ppermute | solution.py:458
  7.5 10.0 %collective-permute-start.2 = (f32[272,128]{1,0:T(8,128)S(1)}, f32[272,128]{1,0:T(8,128)S(1)}, u32[]{:S(2)}, u32[]{:S(2)}) collective-permute-start(f32[272,128]{1,0:T(8,128)S(1)} %get-tuple-element.31), channel_id=1, source_target_pairs={{0,8},{1,9},{2,10},{3,11},{4,12},{5,13},{6,14},{7,15},{8,0},{9,1},... | collective-permute-start | bytes 417800 | tf_op jit(solution)/shard_map/ppermute | solution.py:496
  9.2 8.3 %collective-permute-start.3 = (f32[272,128]{1,0:T(8,128)S(1)}, f32[272,128]{1,0:T(8,128)S(1)}, u32[]{:S(2)}, u32[]{:S(2)}) collective-permute-start(f32[272,128]{1,0:T(8,128)S(1)} %get-tuple-element.32), channel_id=1, source_target_pairs={{0,1},{1,0},{2,3},{3,2},{4,5},{5,4},{6,7},{7,6},{8,16},{9,17},{10,... | collective-permute-start | bytes 417800 | tf_op jit(solution)/shard_map/ppermute | solution.py:495

commit v12 on v9

--- a/solution.py
+++ b/solution.py
@@ -182,10 +182,16 @@
         products[:, 2 * k * LANES : (2 * k + 2) * LANES] = twice((hot[2] + hot[3]).astype(bf16))
         speeds[pl.ds(k * LANES, LANES), :] = jnp.broadcast_to(small[:, 4:5], (LANES, LANES))
         parts = jnp.concatenate(split(hot[0] * row), axis=0)
-        both = dot(parts, seconds)
-        mats.append(both[:species] + both[species:])
-    photo = sum(mats[1 : PHOT // LANES], mats[0])
-    dark = sum(mats[PHOT // LANES + 1 :], mats[PHOT // LANES])
+        mats.append((parts, seconds))
+
+    def total(pairs):
+        both = dot(
+            jnp.concatenate([p for p, _ in pairs], axis=1),
+            jnp.concatenate([q for _, q in pairs], axis=0),
+        )
+        return both[:species] + both[species:]
+
+    photo, dark = total(mats[: PHOT // LANES]), total(mats[PHOT // LANES :])
     for q, mat in enumerate((dark, photo)):
         high, low = split(mat + mat.T)
         losses[:, 2 * q * species : 2 * (q + 1) * species] = twice(high)

time: 26.3 us -> 26.3 us (level)
  no operation moved by 1% of the time
where the time goes in v12:
time: 26.3 us; the launch traced here: 26 us
  Pallas kernels  20.5 us (78%)
  starting transfers between devices  5.27 us (20%)
    pallas_call x1, Pallas kernels, local(): pl.pallas_call(outer_kernel, out_shape=jax.ShapeDtypeStruct(conc.shape, f...  8.39 us
    pallas_call x1, Pallas kernels, local(): pl.pallas_call(inner_kernel, out_shape=jax.ShapeDtypeStruct(conc.shape, f...  8.09 us
    ppermute x1, starting transfers between devices, local(): of_other = lax.ppermute(to_other, 'lon', other)  3.4 us
    pallas_call x1, Pallas kernels, local(): pl.pallas_call(table_kernel, out_shape=(shape(rows, species, cells), shap...  2.31 us
    ppermute x1, starting transfers between devices, local(): of_near = lax.ppermute(to_near, ('lat', 'lon'), near)  1.71 us
    pallas_call x1, Pallas kernels, local(): pl.pallas_call(edge_kernel, out_shape=(side, side, shape(2, rows, species...  1.68 us
  transfers between devices with their start and end apart: 4, of which 0 were waited for; matrix products, arithmetic and copies ran while one was open for 0% of the time, Pallas kernels for 40%

profile of v12, /device:TPU:0, one launch (start us, length us, event | category | flops | bytes accessed | tf_op | source)
XLA Modules:
  0.0 26.0 jit_solution(3612928877005992608)
XLA Ops:
  0.0 1.7 %edges.1 = (f32[3,16,128]{2,1,0:T(8,128)S(1)}, f32[3,16,128]{2,1,0:T(8,128)S(1)}, f32[2,16,128]{2,1,0:T(8,128)S(1)}, f32[272,128]{1,0:T(8,128)S(1)}, f32[272,128...) custom-call(f32[16,128,128]{2,1,0:T(8,128)} %conc_in.1, f32[16,128]{1,0:T(8,128)} %wlon_in.1, ...), custom_call_target="tpu_custom_call" | custom-call | tf_op jit(solution)/shard_map/edges/pallas_call | solution.py:439
  1.7 3.4 %collective-permute-start = (f32[3,16,128]{2,1,0:T(8,128)S(1)}, f32[3,16,128]{2,1,0:T(8,128)S(1)}, u32[]{:S(2)}, u32[]{:S(2)}) collective-permute-start(f32[3,16,128]{2,1,0:T(8,128)S(1)} %get-tuple-element.25), channel_id=1, source_target_pairs={{0,7},{1,2},{2,1},{3,4},{4,3},{5,6},{6,5},{7,0},{8,15},{9,10},{10,... | collective-permute-start | bytes 73736 | tf_op jit(solution)/shard_map/ppermute | solution.py:463
  5.1 0.0 collective-permute-start.1
  5.1 2.3 %tables.1 = (f32[16,128,128]{2,1,0:T(8,128)S(1)}, bf16[1024,256]{1,0:T(8,128)(2,1)S(1)}, bf16[128,1024]{1,0:T(8,128)(2,1)S(1)}, bf16[128,768]{1,0:T(8,128)(2,1)S...) custom-call(f32[16,128,128]{2,1,0:T(8,128)S(1)} %get-tuple-element.22., ...), custom_call_target="tpu_custom_call" | custom-call | flops 1000000000 | bytes 2000000 | tf_op jit(solution)/shard_map/tables/pallas_call | solution.py:466
  7.4 0.0 collective-permute-done.of_other
  7.4 0.0 collective-permute-done.1.of_pair
  7.4 0.1 corners.1
  7.5 1.7 %collective-permute-start.2 = (f32[272,128]{1,0:T(8,128)S(1)}, f32[272,128]{1,0:T(8,128)S(1)}, u32[]{:S(2)}, u32[]{:S(2)}) collective-permute-start(f32[272,128]{1,0:T(8,128)S(1)} %get-tuple-element.31), channel_id=1, source_target_pairs={{0,8},{1,9},{2,10},{3,11},{4,12},{5,13},{6,14},{7,15},{8,0},{9,1},... | collective-permute-start | bytes 417800 | tf_op jit(solution)/shard_map/ppermute | solution.py:502
  9.2 0.2 collective-permute-start.3
  9.4 8.1 %inner.1._ = f32[16,128,128]{2,1,0:T(8,128)} custom-call(f32[16,128,128]{2,1,0:T(8,128)S(1)} %get-tuple-element.24.once, f32[6,16,128]{2,1,0:T(8,128)S(1)} %get-tuple-element.23.coefs, f32[3,16,128]{2,1,0:T(8,128)S(1)} %collective-permute-done.of_other, f32[3,16,128]{2,1,0:T(8,128)S(1)} %collective-permute-done.1.of_pair, ...), custom_call_target="tpu_custom_call" | custom-call | tf_op jit(solution)/shard_map/inner/pallas_call | solution.py:510
  17.5 0.0 collective-permute-done.2.of_near
  17.5 0.0 collective-permute-done.3.of_next
  17.5 8.4 %outer.1 = f32[16,128,128]{2,1,0:T(8,128)} custom-call(f32[16,128,128]{2,1,0:T(8,128)S(1)} %get-tuple-element.24.once, f32[6,16,128]{2,1,0:T(8,128)S(1)} %get-tuple-element.23.coefs, f32[3,16,128]{2,1,0:T(8,128)S(1)} %collective-permute-done.of_other, f32[3,16,128]{2,1,0:T(8,128)S(1)} %collective-permute-done.1.of_pair, ...), custom_call_target="tpu_custom_call", output_to_operand_aliasing={{}: (15, {})} | custom-call | tf_op jit(solution)/shard_map/outer/pallas_call | solution.py:515
Async XLA Ops:
  1.7 5.7 %collective-permute-start = (f32[3,16,128]{2,1,0:T(8,128)S(1)}, f32[3,16,128]{2,1,0:T(8,128)S(1)}, u32[]{:S(2)}, u32[]{:S(2)}) collective-permute-start(f32[3,16,128]{2,1,0:T(8,128)S(1)} %get-tuple-element.25), channel_id=1, source_target_pairs={{0,7},{1,2},{2,1},{3,4},{4,3},{5,6},{6,5},{7,0},{8,15},{9,10},{10,... | collective-permute-start | bytes 73736 | tf_op jit(solution)/shard_map/ppermute | solution.py:463
  5.1 2.3 %collective-permute-start.1 = (f32[3,16,128]{2,1,0:T(8,128)S(1)}, f32[3,16,128]{2,1,0:T(8,128)S(1)}, u32[]{:S(2)}, u32[]{:S(2)}) collective-permute-start(f32[3,16,128]{2,1,0:T(8,128)S(1)} %get-tuple-element.26), channel_id=1, source_target_pairs={{0,1},{1,0},{2,3},{3,2},{4,5},{5,4},{6,7},{7,6},{8,9},{9,8},{10,11... | collective-permute-start | bytes 73736 | tf_op jit(solution)/shard_map/ppermute | solution.py:464
  7.5 10.0 %collective-permute-start.2 = (f32[272,128]{1,0:T(8,128)S(1)}, f32[272,128]{1,0:T(8,128)S(1)}, u32[]{:S(2)}, u32[]{:S(2)}) collective-permute-start(f32[272,128]{1,0:T(8,128)S(1)} %get-tuple-element.31), channel_id=1, source_target_pairs={{0,8},{1,9},{2,10},{3,11},{4,12},{5,13},{6,14},{7,15},{8,0},{9,1},... | collective-permute-start | bytes 417800 | tf_op jit(solution)/shard_map/ppermute | solution.py:502
  9.2 8.3 %collective-permute-start.3 = (f32[272,128]{1,0:T(8,128)S(1)}, f32[272,128]{1,0:T(8,128)S(1)}, u32[]{:S(2)}, u32[]{:S(2)}) collective-permute-start(f32[272,128]{1,0:T(8,128)S(1)} %get-tuple-element.32), channel_id=1, source_target_pairs={{0,1},{1,0},{2,3},{3,2},{4,5},{5,4},{6,7},{7,6},{8,16},{9,17},{10,... | collective-permute-start | bytes 417800 | tf_op jit(solution)/shard_map/ppermute | solution.py:501
